TPU v7x, 256 devices: a whole 4x4x8 slice. The times are simulated.
256 devices in a mesh: lat: 16 (over x, z_hi, core), tm: 16 (over y, z_lo).
Axes of the slice: x: 4, y: 4, z: 8 (z_hi: 2, z_lo: 4; z = z_hi * 4 + z_lo), core: 2. Of those that a mesh axis runs over, the one named last changes fastest.
Arguments:
- data: float32 [8, 256, 92160], P(None, 'tm', 'lat'), may hold values from -6 to 6
- space_init: float32 [32, 92160], P(None, 'lat'), may hold values from -0.01953125 to 0.01953125
- time_init: float32 [32, 256], P(None, 'tm'), may hold values from -6 to 6
- variable_factor: float32 [8, 32], replicated, may hold values from -2 to 2
- neighbours: int32 [4, 92160], P(None, 'lat'), may hold values from -1 to 92159, as said below
Outputs:
- time_factor: float32 [32, 256], P(None, 'tm')
- space_factor: float32 [32, 92160], P(None, 'lat')
Inputs may be any that keep to these rules, and one draw needn't show every extreme that they name: `neighbours`: points are numbered row by row: latitude row i holds points i * 360 to (i + 1) * 360 - 1. Rows 0 and 1 name the east and west neighbour in the same latitude row (cyclic in longitude); rows 2 and 3 name a point of the latitude row before and after, at most one column away (cyclic); -1 where the grid has no such row.
All inputs are finite; a program needn't handle non-finite values.
Results may differ from a plain program's by a relative error of at most 0.0001.
Values sent between devices are 32-bit elements; how exact they have to be, the bound alone decides.
No kernel may reach another device: no remote copies, remote signals or barrier semaphores. Data moves between devices by JAX's collectives and lax.ppermute only.
A program may use at most 64 MiB of HBM per device.

v0:
```python
import jax
import jax.numpy as jnp
from jax import lax
from jax.sharding import PartitionSpec as P

NLON = 360
SWEEPS = 8


def copy_for_each(shard, axis):
    copies = jnp.broadcast_to(shard, (lax.axis_size(axis), *shard.shape))
    return lax.all_to_all(copies, axis, split_axis=0, concat_axis=0, tiled=True)


def taken_together(shard, axis):
    return copy_for_each(shard, axis).sum(axis=0)


def padded_2(cells, sides, width):
    for axis, dim in sides:
        count = lax.axis_size(axis)
        ends = count - 1
        head = lax.slice_in_dim(cells, 0, width, axis=dim)
        tail = lax.slice_in_dim(cells, cells.shape[dim] - width, cells.shape[dim], axis=dim)
        cells = jnp.concatenate(
            [
                lax.ppermute(tail, axis, [(i, (i + 1) % count) for i in range(ends)]),
                cells,
                lax.ppermute(head, axis, [((i + 1) % count, i) for i in range(ends)]),
            ],
            axis=dim,
        )
    return cells


def cut_along(shard, dim, size):
    lengths = shard.shape
    pieces = shard.reshape(*lengths[:dim], size, lengths[dim] // size, *lengths[dim + 1 :])
    return jnp.moveaxis(pieces, dim, 0)


def sum_at_owner(shard, axis, dim):
    size = lax.axis_size(axis)
    pieces = lax.all_to_all(cut_along(shard, dim, size), axis, 0, 0, tiled=True)
    return jnp.sum(pieces, axis=0)


def extended_2(shard, sides, width):
    edges = {}
    for axis, dim in sides:
        size, length = (lax.axis_size(axis), shard.shape[dim])
        up = [(i, (i + 1) % size) for i in range(size - 1)]
        last = lax.slice_in_dim(shard, length - width, length, axis=dim)
        initial = lax.slice_in_dim(shard, 0, width, axis=dim)
        edges[dim] = (
            lax.ppermute(last, axis, up),
            lax.ppermute(initial, axis, [(b, a) for a, b in up]),
        )
    done = []
    for _, dim in sides:
        low, high = edges[dim]
        around = [(width, width) if d in done else (0, 0) for d in range(shard.ndim)]
        shard = jnp.concatenate([jnp.pad(low, around), shard, jnp.pad(high, around)], axis=dim)
        done.append(dim)
    return shard


def laid_out(pieces, dim):
    lengths = list(pieces.shape[1:])
    lengths[dim] *= pieces.shape[0]
    return jnp.moveaxis(pieces, 0, dim).reshape(lengths)


def collect(shard, axis, dim):
    return laid_out(copy_for_each(shard, axis), dim)


def inverse(matrix):
    lower = jnp.linalg.cholesky(matrix)
    identity = jnp.eye(matrix.shape[0], dtype=jnp.float32)
    return jax.scipy.linalg.cho_solve((lower, True), identity)


def link_masks(link, column, row_count):
    target = (link % NLON - column + NLON) % NLON
    ahead = (target == 1).reshape(row_count, NLON)
    behind = (target == NLON - 1).reshape(row_count, NLON)
    present = (link >= 0).reshape(row_count, NLON)
    return (ahead, behind, present)


def pick_row(block, masks):
    ahead, behind, present = masks
    moved = jnp.where(
        ahead[None],
        jnp.roll(block, -1, axis=2),
        jnp.where(behind[None], jnp.roll(block, 1, axis=2), block),
    )
    return jnp.where(present[None], moved, jnp.float32(0.0))


def run_sweeps(extend, start_factor, point_rhs, point_inv, neighbours):
    highest = lax.Precision.HIGHEST
    rank_count, point_count = start_factor.shape
    row_count = point_count // NLON
    column = jnp.arange(point_count, dtype=jnp.int32) % NLON
    north_masks = link_masks(neighbours[2], column, row_count)
    south_masks = link_masks(neighbours[3], column, row_count)
    current = start_factor
    for sweep_index in range(SWEEPS):
        extended = extend(current).reshape(rank_count, row_count + 2, NLON)
        center = extended[:, 1:-1]
        near_sum = jnp.roll(center, -1, axis=2) + jnp.roll(center, 1, axis=2)
        near_sum = (
            near_sum
            + pick_row(extended[:, :-2], north_masks)
            + pick_row(extended[:, 2:], south_masks)
        )
        near_sum = near_sum.reshape(rank_count, point_count)
        current = jnp.dot(
            point_inv,
            point_rhs + 0.5 * near_sum,
            precision=highest,
            preferred_element_type=jnp.float32,
        )
    return current


def per_device(data, space_init, time_init, variable_factor, neighbours):
    highest = lax.Precision.HIGHEST
    var_count, hour_count, point_count = data.shape
    rank_count = space_init.shape[0]
    identity = jnp.eye(rank_count, dtype=jnp.float32)
    unfolded = data.reshape(var_count * hour_count, point_count)
    var_gram = jnp.dot(
        variable_factor.T, variable_factor, precision=highest, preferred_element_type=jnp.float32
    )
    local_gram = lax.dot_general(
        space_init,
        space_init,
        (((1,), (1,)), ((), ())),
        precision=highest,
        preferred_element_type=jnp.float32,
    )
    space_gram = taken_together(local_gram, "lat")
    padded = padded_2(time_init, (("tm", 1),), 2)
    stencil = padded[:, :-4] - 4.0 * padded[:, 1:-3] - 4.0 * padded[:, 3:-1] + padded[:, 4:]
    projected = lax.dot_general(
        space_init,
        unfolded,
        (((1,), (1,)), ((), ())),
        precision=highest,
        preferred_element_type=jnp.float32,
    )
    projected = projected.reshape(rank_count, var_count, hour_count)
    rhs_terms = jnp.sum(projected * variable_factor.T[:, :, None], axis=1)
    time_inv = inverse(space_gram * var_gram + 3.0 * identity)
    time_rhs = taken_together(rhs_terms, "lat")
    time_factor = jnp.dot(
        time_inv, time_rhs - 0.5 * stencil, precision=highest, preferred_element_type=jnp.float32
    )
    weighted = (variable_factor.T[:, :, None] * time_factor[:, None, :]).reshape(
        rank_count, var_count * hour_count
    )
    point_terms = jnp.dot(weighted, unfolded, precision=highest, preferred_element_type=jnp.float32)
    hour_gram = lax.dot_general(
        time_factor,
        time_factor,
        (((1,), (1,)), ((), ())),
        precision=highest,
        preferred_element_type=jnp.float32,
    )
    time_gram = taken_together(hour_gram, "tm")
    scale = jnp.sqrt(jnp.diagonal(time_gram) + 1e-06)
    point_op = time_gram / (scale[:, None] * scale[None, :]) * var_gram + 2.0 * identity
    point_inv = inverse(point_op)
    share_points = point_count // lax.axis_size("tm")
    share_start = lax.axis_index("tm") * share_points
    rhs_share = sum_at_owner(point_terms, "tm", 1) / scale[:, None]
    start_share = lax.dynamic_slice_in_dim(space_init, share_start, share_points, 1)
    links_share = lax.dynamic_slice_in_dim(neighbours, share_start, share_points, 1)

    def extend_share(current):
        return extended_2(current, ((("lat", "tm"), 1),), NLON)

    result_share = run_sweeps(extend_share, start_share, rhs_share, point_inv, links_share)
    space_factor = collect(result_share, "tm", 1)
    return (time_factor, space_factor)


def solution(mesh):
    placed = (P(None, "tm", "lat"), P(None, "lat"), P(None, "tm"), P(), P(None, "lat"))
    return jax.shard_map(
        per_device,
        mesh=mesh,
        in_specs=placed,
        out_specs=(P(None, "tm"), P(None, "lat")),
        check_vma=False,
    )
```

profile of v0, /device:TPU:32, one launch (start us, length us, event | category | flops | bytes accessed | tf_op | source)
XLA Modules:
  0.0 223.4 jit_solution(254703548067909295)
XLA Ops:
  1.8 3.8 %collective-permute-start.2 = (f32[32,360]{1,0:T(8,128)S(1)}, f32[32,360]{1,0:T(8,128)S(1)}, u32[]{:S(2)}, u32[]{:S(2)}) collective-permute-start(f32[32,360]{1,0:T(8,128)S(1)} %constant_dynamic-slice_fusion), channel_id=1, source_target_pairs={{0,1},{1,2},{2,3},{3,4},{4,5},{5,6},{6,7},{7,8},{8,9},{9,10},{10,1... | collective-permute-start | bytes 138248 | tf_op jit(solution)/shard_map/ppermute | solution.py:56
  7.7 4.3 %fusion = f32[32,16]{0,1:T(8,128)S(1)} fusion(f32[8,16,5760]{2,1,0:T(8,128)} %param.8, f32[32,5760]{1,0:T(8,128)S(1)} %copy-done, f32[32,8]{0,1:T(8,128)} %bitcast.202), kind=kOutput, calls=%fused_computation.3 | convolution fusion | flops 283123200 | bytes 3689472 | tf_op jit(solution)/shard_map/dot_general | solution.py:148
  12.7 10.1 %all-to-all-start.1 = ((f32[16,1,512]{2,1,0:T(1,128)}), f32[16,1,512]{2,1,0:T(1,128)S(1)}, u32[]{:S(2)}, u32[]{:S(2)}) async-start(f32[16,1,512]{2,1,0:T(1,128)} %reshape.622), calls=%async_computation.1 | async-start | bytes 65536 | tf_op jit(solution)/shard_map/all_to_all | solution.py:12
  22.9 6.0 %collective-permute-start.1 = (f32[32,2]{0,1:T(2,128)S(1)}, f32[32,2]{0,1:T(2,128)S(1)}, u32[]{:S(2)}, u32[]{:S(2)}) collective-permute-start(f32[32,2]{0,1:T(2,128)S(1)} %get-tuple-element.124), channel_id=1, source_target_pairs={{1,0},{2,1},{3,2},{4,3},{5,4},{6,5},{7,6},{8,7},{9,8},{10,9},{11,1... | collective-permute-start | bytes 776 | tf_op jit(solution)/shard_map/ppermute | solution.py:29
  34.2 3.5 %copy.736 = f32[5760,128]{1,0:T(8,128)} copy(f32[5760,128]{0,1:T(8,128)} %bitcast.150) | data formatting | bytes 5898240 | tf_op jit(solution)/shard_map/dot_general | solution.py:165
  38.5 9.6 %all-to-all-start = ((f32[16,1,1024]{2,1,0:T(1,128)}), f32[16,1,1024]{2,1,0:T(1,128)S(1)}, u32[]{:S(2)}, u32[]{:S(2)}) async-start(f32[16,1,1024]{2,1,0:T(1,128)} %reshape.620), calls=%async_computation | async-start | bytes 131072 | tf_op jit(solution)/shard_map/all_to_all | solution.py:12
  49.8 8.5 %all-to-all-done = f32[16,1,1024]{2,1,0:T(1,128)S(1)} async-done(((f32[16,1,1024]{2,1,0:T(1,128)}), f32[16,1,1024]{2,1,0:T(1,128)S(1)}, u32[]{:S(2)}, u32[]{:S(2)}) %all-to-all-start) | async-done | bytes 65568 | tf_op jit(solution)/shard_map/all_to_all | solution.py:12
  59.5 2.9 %cholesky.44 = f32[32,32]{1,0:T(8,128)S(1)} custom-call(f32[32,32]{1,0:T(8,128)S(1)} %fusion.287), custom_call_target="Cholesky" | custom-call | tf_op jit(solution)/shard_map/jit(cholesky)/cholesky | solution.py:79
  63.8 2.4 %custom-call.10 = f32[1,32,32]{1,2,0:T(8,128)S(1)} custom-call(f32[1,32,32]{2,1,0:T(8,128)S(1)} %fusion.278), custom_call_target="InvertDiagBlocksLowerTriangular" | custom-call | tf_op jit(solution)/shard_map/jit(_cho_solve)/triangular_solve | solution.py:81
  67.8 8.1 %all-to-all-start.2 = ((f32[16,1,1024]{2,1,0:T(1,128)}), f32[16,1,1024]{2,1,0:T(1,128)S(1)}, u32[]{:S(2)}, u32[]{:S(2)}) async-start(f32[16,1,1024]{2,1,0:T(1,128)} %reshape.624), calls=%async_computation.2 | async-start | bytes 131072 | tf_op jit(solution)/shard_map/all_to_all | solution.py:12
  75.9 6.2 %convolution_bitcast_fusion = f32[16,32,360]{2,1,0:T(8,128)} fusion(f32[32,128,1]{0,1,2:T(8,128)S(1)} %bitcast.153, f32[16,360,128]{2,1,0:T(8,128)} %bitcast.151), kind=kOutput, calls=%fused_computation.1 | convolution fusion | flops 283115520 | bytes 3702784 | tf_op jit(solution)/shard_map/dot_general | solution.py:165
  82.7 7.0 %all-to-all-start.3 = ((f32[16,32,360]{2,1,0:T(8,128)}), f32[16,32,360]{2,1,0:T(8,128)S(1)}, u32[]{:S(2)}, u32[]{:S(2)}) async-start(f32[16,32,360]{2,1,0:T(8,128)} %convolution_bitcast_fusion), calls=%async_computation.3 | async-start | bytes 1572864 | tf_op jit(solution)/shard_map/all_to_all | solution.py:44
  91.6 2.9 %cholesky.55 = f32[32,32]{1,0:T(8,128)S(1)} custom-call(f32[32,32]{1,0:T(8,128)S(1)} %fusion.283), custom_call_target="Cholesky" | custom-call | tf_op jit(solution)/shard_map/jit(cholesky)/cholesky | solution.py:79
  95.8 2.4 %custom-call.11 = f32[1,32,32]{1,2,0:T(8,128)S(1)} custom-call(f32[1,32,32]{2,1,0:T(8,128)S(1)} %fusion.279), custom_call_target="InvertDiagBlocksLowerTriangular" | custom-call | tf_op jit(solution)/shard_map/jit(_cho_solve)/triangular_solve | solution.py:81
  98.6 9.6 %all-to-all-done.3 = f32[16,32,360]{2,1,0:T(8,128)S(1)} async-done(((f32[16,32,360]{2,1,0:T(8,128)}), f32[16,32,360]{2,1,0:T(8,128)S(1)}, u32[]{:S(2)}, u32[]{:S(2)}) %all-to-all-start.3) | async-done | bytes 737312 | tf_op jit(solution)/shard_map/all_to_all | solution.py:44
  108.6 2.7 %collective-permute-start.4 = (f32[32,360]{1,0:T(8,128)S(1)}, f32[32,360]{1,0:T(8,128)S(1)}, u32[]{:S(2)}, u32[]{:S(2)}) collective-permute-start(f32[32,360]{1,0:T(8,128)S(1)} %fusion.7), channel_id=1, source_target_pairs={{0,1},{1,2},{2,3},{3,4},{4,5},{5,6},{6,7},{7,8},{8,9},{9,10},{10,1... | collective-permute-start | bytes 138248 | tf_op jit(solution)/shard_map/ppermute | solution.py:56
  111.3 3.9 %collective-permute-start.5 = (f32[32,360]{1,0:T(8,128)S(1)}, f32[32,360]{1,0:T(8,128)S(1)}, u32[]{:S(2)}, u32[]{:S(2)}) collective-permute-start(f32[32,360]{1,0:T(8,128)S(1)} %fusion.7), channel_id=1, source_target_pairs={{1,0},{2,1},{3,2},{4,3},{5,4},{6,5},{7,6},{8,7},{9,8},{10,9},{11,1... | collective-permute-start | bytes 138248 | tf_op jit(solution)/shard_map/ppermute | solution.py:57
  115.3 2.4 %collective-permute-done.5 = f32[32,360]{1,0:T(8,128)S(1)} collective-permute-done((f32[32,360]{1,0:T(8,128)S(1)}, f32[32,360]{1,0:T(8,128)S(1)}, u32[]{:S(2)}, u32[]{:S(2)}) %collective-permute-start.5) | collective-permute-done | bytes 46112 | tf_op jit(solution)/shard_map/ppermute | solution.py:57
  119.0 3.8 %collective-permute-start.6 = (f32[32,360]{1,0:T(8,128)S(1)}, f32[32,360]{1,0:T(8,128)S(1)}, u32[]{:S(2)}, u32[]{:S(2)}) collective-permute-start(f32[32,360]{1,0:T(8,128)S(1)} %fusion.31), channel_id=1, source_target_pairs={{0,1},{1,2},{2,3},{3,4},{4,5},{5,6},{6,7},{7,8},{8,9},{9,10},{10,1... | collective-permute-start | bytes 138248 | tf_op jit(solution)/shard_map/ppermute | solution.py:56
  122.8 2.1 collective-permute-start.7
  125.0 6.5 %collective-permute-done.7 = f32[32,360]{1,0:T(8,128)S(1)} collective-permute-done((f32[32,360]{1,0:T(8,128)S(1)}, f32[32,360]{1,0:T(8,128)S(1)}, u32[]{:S(2)}, u32[]{:S(2)}) %collective-permute-start.7) | collective-permute-done | bytes 46112 | tf_op jit(solution)/shard_map/ppermute | solution.py:57
  132.8 3.9 %collective-permute-start.8 = (f32[32,360]{1,0:T(8,128)S(1)}, f32[32,360]{1,0:T(8,128)S(1)}, u32[]{:S(2)}, u32[]{:S(2)}) collective-permute-start(f32[32,360]{1,0:T(8,128)S(1)} %fusion.55), channel_id=1, source_target_pairs={{0,1},{1,2},{2,3},{3,4},{4,5},{5,6},{6,7},{7,8},{8,9},{9,10},{10,1... | collective-permute-start | bytes 138248 | tf_op jit(solution)/shard_map/ppermute | solution.py:56
  139.1 4.3 %collective-permute-done.9 = f32[32,360]{1,0:T(8,128)S(1)} collective-permute-done((f32[32,360]{1,0:T(8,128)S(1)}, f32[32,360]{1,0:T(8,128)S(1)}, u32[]{:S(2)}, u32[]{:S(2)}) %collective-permute-start.9) | collective-permute-done | bytes 46112 | tf_op jit(solution)/shard_map/ppermute | solution.py:57
  144.7 3.9 %collective-permute-start.10 = (f32[32,360]{1,0:T(8,128)S(1)}, f32[32,360]{1,0:T(8,128)S(1)}, u32[]{:S(2)}, u32[]{:S(2)}) collective-permute-start(f32[32,360]{1,0:T(8,128)S(1)} %fusion.79), channel_id=1, source_target_pairs={{0,1},{1,2},{2,3},{3,4},{4,5},{5,6},{6,7},{7,8},{8,9},{9,10},{10,1... | collective-permute-start | bytes 138248 | tf_op jit(solution)/shard_map/ppermute | solution.py:56
  150.8 4.5 %collective-permute-done.11 = f32[32,360]{1,0:T(8,128)S(1)} collective-permute-done((f32[32,360]{1,0:T(8,128)S(1)}, f32[32,360]{1,0:T(8,128)S(1)}, u32[]{:S(2)}, u32[]{:S(2)}) %collective-permute-start.11) | collective-permute-done | bytes 46112 | tf_op jit(solution)/shard_map/ppermute | solution.py:57
  156.7 3.9 %collective-permute-start.12 = (f32[32,360]{1,0:T(8,128)S(1)}, f32[32,360]{1,0:T(8,128)S(1)}, u32[]{:S(2)}, u32[]{:S(2)}) collective-permute-start(f32[32,360]{1,0:T(8,128)S(1)} %fusion.103), channel_id=1, source_target_pairs={{0,1},{1,2},{2,3},{3,4},{4,5},{5,6},{6,7},{7,8},{8,9},{9,10},{10,1... | collective-permute-start | bytes 138248 | tf_op jit(solution)/shard_map/ppermute | solution.py:56
  162.7 4.9 %collective-permute-done.13 = f32[32,360]{1,0:T(8,128)S(1)} collective-permute-done((f32[32,360]{1,0:T(8,128)S(1)}, f32[32,360]{1,0:T(8,128)S(1)}, u32[]{:S(2)}, u32[]{:S(2)}) %collective-permute-start.13) | collective-permute-done | bytes 46112 | tf_op jit(solution)/shard_map/ppermute | solution.py:57
  168.8 4.0 %collective-permute-start.14 = (f32[32,360]{1,0:T(8,128)S(1)}, f32[32,360]{1,0:T(8,128)S(1)}, u32[]{:S(2)}, u32[]{:S(2)}) collective-permute-start(f32[32,360]{1,0:T(8,128)S(1)} %fusion.127), channel_id=1, source_target_pairs={{0,1},{1,2},{2,3},{3,4},{4,5},{5,6},{6,7},{7,8},{8,9},{9,10},{10,1... | collective-permute-start | bytes 138248 | tf_op jit(solution)/shard_map/ppermute | solution.py:56
  174.8 4.6 %collective-permute-done.15 = f32[32,360]{1,0:T(8,128)S(1)} collective-permute-done((f32[32,360]{1,0:T(8,128)S(1)}, f32[32,360]{1,0:T(8,128)S(1)}, u32[]{:S(2)}, u32[]{:S(2)}) %collective-permute-start.15) | collective-permute-done | bytes 46112 | tf_op jit(solution)/shard_map/ppermute | solution.py:57
  180.8 3.9 %collective-permute-start.16 = (f32[32,360]{1,0:T(8,128)S(1)}, f32[32,360]{1,0:T(8,128)S(1)}, u32[]{:S(2)}, u32[]{:S(2)}) collective-permute-start(f32[32,360]{1,0:T(8,128)S(1)} %fusion.151), channel_id=1, source_target_pairs={{0,1},{1,2},{2,3},{3,4},{4,5},{5,6},{6,7},{7,8},{8,9},{9,10},{10,1... | collective-permute-start | bytes 138248 | tf_op jit(solution)/shard_map/ppermute | solution.py:56
  186.8 4.6 %collective-permute-done.17 = f32[32,360]{1,0:T(8,128)S(1)} collective-permute-done((f32[32,360]{1,0:T(8,128)S(1)}, f32[32,360]{1,0:T(8,128)S(1)}, u32[]{:S(2)}, u32[]{:S(2)}) %collective-permute-start.17) | collective-permute-done | bytes 46112 | tf_op jit(solution)/shard_map/ppermute | solution.py:57
  192.8 28.9 %all_to_all.25 = f32[16,32,360]{2,1,0:T(8,128)S(1)} all-to-all(f32[16,32,360]{2,1,0:T(8,128)S(1)} %broadcast_in_dim.214), channel_id=1, replica_groups=mesh['lat'=16,'tm'=16] {'tm'}, dimensions={0} | all-to-all | bytes 1474560 | tf_op jit(solution)/shard_map/all_to_all | solution.py:12
  (178 shorter events, 41.5 us)
Async XLA Ops:
  0.6 1.1 copy-start
  0.6 22.2 %copy-start.2 = (f32[32,16]{0,1:T(8,128)S(1)}, f32[32,16]{0,1:T(8,128)}, u32[]{:S(2)}) copy-start(f32[32,16]{0,1:T(8,128)} %param.10) | copy-start | bytes 6148
  1.8 35.9 %collective-permute-start.2 = (f32[32,360]{1,0:T(8,128)S(1)}, f32[32,360]{1,0:T(8,128)S(1)}, u32[]{:S(2)}, u32[]{:S(2)}) collective-permute-start(f32[32,360]{1,0:T(8,128)S(1)} %constant_dynamic-slice_fusion), channel_id=1, source_target_pairs={{0,1},{1,2},{2,3},{3,4},{4,5},{5,6},{6,7},{7,8},{8,9},{9,10},{10,1... | collective-permute-start | bytes 138248 | tf_op jit(solution)/shard_map/ppermute | solution.py:56
  5.7 32.0 %collective-permute-start.3 = (f32[32,360]{1,0:T(8,128)S(1)}, f32[32,360]{1,0:T(8,128)S(1)}, u32[]{:S(2)}, u32[]{:S(2)}) collective-permute-start(f32[32,360]{1,0:T(8,128)S(1)} %constant_dynamic-slice_fusion), channel_id=1, source_target_pairs={{1,0},{2,1},{3,2},{4,3},{5,4},{6,5},{7,6},{8,7},{9,8},{10,9},{11,1... | collective-permute-start | bytes 138248 | tf_op jit(solution)/shard_map/ppermute | solution.py:57
  12.7 25.8 %all-to-all-start.1 = ((f32[16,1,512]{2,1,0:T(1,128)}), f32[16,1,512]{2,1,0:T(1,128)S(1)}, u32[]{:S(2)}, u32[]{:S(2)}) async-start(f32[16,1,512]{2,1,0:T(1,128)} %reshape.622), calls=%async_computation.1 | async-start | bytes 65536 | tf_op jit(solution)/shard_map/all_to_all | solution.py:12
  22.9 14.8 %collective-permute-start.1 = (f32[32,2]{0,1:T(2,128)S(1)}, f32[32,2]{0,1:T(2,128)S(1)}, u32[]{:S(2)}, u32[]{:S(2)}) collective-permute-start(f32[32,2]{0,1:T(2,128)S(1)} %get-tuple-element.124), channel_id=1, source_target_pairs={{1,0},{2,1},{3,2},{4,3},{5,4},{6,5},{7,6},{8,7},{9,8},{10,9},{11,1... | collective-permute-start | bytes 776 | tf_op jit(solution)/shard_map/ppermute | solution.py:29
  28.9 37.7 %collective-permute-start = (f32[32,2]{0,1:T(2,128)S(1)}, f32[32,2]{0,1:T(2,128)S(1)}, u32[]{:S(2)}, u32[]{:S(2)}) collective-permute-start(f32[32,2]{0,1:T(2,128)S(1)} %get-tuple-element.125), channel_id=1, source_target_pairs={{0,1},{1,2},{2,3},{3,4},{4,5},{5,6},{6,7},{7,8},{8,9},{9,10},{10,1... | collective-permute-start | bytes 776 | tf_op jit(solution)/shard_map/ppermute | solution.py:27
  37.7 21.5 %copy-start.3 = (f32[8,32]{1,0:T(8,128)S(1)}, f32[8,32]{1,0:T(8,128)}, u32[]{:S(2)}) copy-start(f32[8,32]{1,0:T(8,128)} %param.11) | copy-start | bytes 3076
  38.5 19.7 %all-to-all-start = ((f32[16,1,1024]{2,1,0:T(1,128)}), f32[16,1,1024]{2,1,0:T(1,128)S(1)}, u32[]{:S(2)}, u32[]{:S(2)}) async-start(f32[16,1,1024]{2,1,0:T(1,128)} %reshape.620), calls=%async_computation | async-start | bytes 131072 | tf_op jit(solution)/shard_map/all_to_all | solution.py:12
  66.8 15.9 %copy-start.1 = (f32[32,16]{0,1:T(8,128)}, f32[32,16]{0,1:T(8,128)S(1)}, u32[]{:S(2)}) copy-start(f32[32,16]{0,1:T(8,128)S(1)} %fusion.294) | copy-start | bytes 6148
  67.8 14.8 %all-to-all-start.2 = ((f32[16,1,1024]{2,1,0:T(1,128)}), f32[16,1,1024]{2,1,0:T(1,128)S(1)}, u32[]{:S(2)}, u32[]{:S(2)}) async-start(f32[16,1,1024]{2,1,0:T(1,128)} %reshape.624), calls=%async_computation.2 | async-start | bytes 131072 | tf_op jit(solution)/shard_map/all_to_all | solution.py:12
  82.7 25.5 %all-to-all-start.3 = ((f32[16,32,360]{2,1,0:T(8,128)}), f32[16,32,360]{2,1,0:T(8,128)S(1)}, u32[]{:S(2)}, u32[]{:S(2)}) async-start(f32[16,32,360]{2,1,0:T(8,128)} %convolution_bitcast_fusion), calls=%async_computation.3 | async-start | bytes 1572864 | tf_op jit(solution)/shard_map/all_to_all | solution.py:44
  108.6 6.7 %collective-permute-start.4 = (f32[32,360]{1,0:T(8,128)S(1)}, f32[32,360]{1,0:T(8,128)S(1)}, u32[]{:S(2)}, u32[]{:S(2)}) collective-permute-start(f32[32,360]{1,0:T(8,128)S(1)} %fusion.7), channel_id=1, source_target_pairs={{0,1},{1,2},{2,3},{3,4},{4,5},{5,6},{6,7},{7,8},{8,9},{9,10},{10,1... | collective-permute-start | bytes 138248 | tf_op jit(solution)/shard_map/ppermute | solution.py:56
  111.3 6.4 %collective-permute-start.5 = (f32[32,360]{1,0:T(8,128)S(1)}, f32[32,360]{1,0:T(8,128)S(1)}, u32[]{:S(2)}, u32[]{:S(2)}) collective-permute-start(f32[32,360]{1,0:T(8,128)S(1)} %fusion.7), channel_id=1, source_target_pairs={{1,0},{2,1},{3,2},{4,3},{5,4},{6,5},{7,6},{8,7},{9,8},{10,9},{11,1... | collective-permute-start | bytes 138248 | tf_op jit(solution)/shard_map/ppermute | solution.py:57
  119.0 6.0 %collective-permute-start.6 = (f32[32,360]{1,0:T(8,128)S(1)}, f32[32,360]{1,0:T(8,128)S(1)}, u32[]{:S(2)}, u32[]{:S(2)}) collective-permute-start(f32[32,360]{1,0:T(8,128)S(1)} %fusion.31), channel_id=1, source_target_pairs={{0,1},{1,2},{2,3},{3,4},{4,5},{5,6},{6,7},{7,8},{8,9},{9,10},{10,1... | collective-permute-start | bytes 138248 | tf_op jit(solution)/shard_map/ppermute | solution.py:56
  122.8 8.7 %collective-permute-start.7 = (f32[32,360]{1,0:T(8,128)S(1)}, f32[32,360]{1,0:T(8,128)S(1)}, u32[]{:S(2)}, u32[]{:S(2)}) collective-permute-start(f32[32,360]{1,0:T(8,128)S(1)} %fusion.31), channel_id=1, source_target_pairs={{1,0},{2,1},{3,2},{4,3},{5,4},{6,5},{7,6},{8,7},{9,8},{10,9},{11,1... | collective-permute-start | bytes 138248 | tf_op jit(solution)/shard_map/ppermute | solution.py:57
  132.8 6.3 %collective-permute-start.8 = (f32[32,360]{1,0:T(8,128)S(1)}, f32[32,360]{1,0:T(8,128)S(1)}, u32[]{:S(2)}, u32[]{:S(2)}) collective-permute-start(f32[32,360]{1,0:T(8,128)S(1)} %fusion.55), channel_id=1, source_target_pairs={{0,1},{1,2},{2,3},{3,4},{4,5},{5,6},{6,7},{7,8},{8,9},{9,10},{10,1... | collective-permute-start | bytes 138248 | tf_op jit(solution)/shard_map/ppermute | solution.py:56
  136.7 6.7 %collective-permute-start.9 = (f32[32,360]{1,0:T(8,128)S(1)}, f32[32,360]{1,0:T(8,128)S(1)}, u32[]{:S(2)}, u32[]{:S(2)}) collective-permute-start(f32[32,360]{1,0:T(8,128)S(1)} %fusion.55), channel_id=1, source_target_pairs={{1,0},{2,1},{3,2},{4,3},{5,4},{6,5},{7,6},{8,7},{9,8},{10,9},{11,1... | collective-permute-start | bytes 138248 | tf_op jit(solution)/shard_map/ppermute | solution.py:57
  144.7 6.1 %collective-permute-start.10 = (f32[32,360]{1,0:T(8,128)S(1)}, f32[32,360]{1,0:T(8,128)S(1)}, u32[]{:S(2)}, u32[]{:S(2)}) collective-permute-start(f32[32,360]{1,0:T(8,128)S(1)} %fusion.79), channel_id=1, source_target_pairs={{0,1},{1,2},{2,3},{3,4},{4,5},{5,6},{6,7},{7,8},{8,9},{9,10},{10,1... | collective-permute-start | bytes 138248 | tf_op jit(solution)/shard_map/ppermute | solution.py:56
  148.7 6.7 %collective-permute-start.11 = (f32[32,360]{1,0:T(8,128)S(1)}, f32[32,360]{1,0:T(8,128)S(1)}, u32[]{:S(2)}, u32[]{:S(2)}) collective-permute-start(f32[32,360]{1,0:T(8,128)S(1)} %fusion.79), channel_id=1, source_target_pairs={{1,0},{2,1},{3,2},{4,3},{5,4},{6,5},{7,6},{8,7},{9,8},{10,9},{11,1... | collective-permute-start | bytes 138248 | tf_op jit(solution)/shard_map/ppermute | solution.py:57
  156.7 6.0 %collective-permute-start.12 = (f32[32,360]{1,0:T(8,128)S(1)}, f32[32,360]{1,0:T(8,128)S(1)}, u32[]{:S(2)}, u32[]{:S(2)}) collective-permute-start(f32[32,360]{1,0:T(8,128)S(1)} %fusion.103), channel_id=1, source_target_pairs={{0,1},{1,2},{2,3},{3,4},{4,5},{5,6},{6,7},{7,8},{8,9},{9,10},{10,1... | collective-permute-start | bytes 138248 | tf_op jit(solution)/shard_map/ppermute | solution.py:56
  160.6 6.9 %collective-permute-start.13 = (f32[32,360]{1,0:T(8,128)S(1)}, f32[32,360]{1,0:T(8,128)S(1)}, u32[]{:S(2)}, u32[]{:S(2)}) collective-permute-start(f32[32,360]{1,0:T(8,128)S(1)} %fusion.103), channel_id=1, source_target_pairs={{1,0},{2,1},{3,2},{4,3},{5,4},{6,5},{7,6},{8,7},{9,8},{10,9},{11,1... | collective-permute-start | bytes 138248 | tf_op jit(solution)/shard_map/ppermute | solution.py:57
  168.8 6.0 %collective-permute-start.14 = (f32[32,360]{1,0:T(8,128)S(1)}, f32[32,360]{1,0:T(8,128)S(1)}, u32[]{:S(2)}, u32[]{:S(2)}) collective-permute-start(f32[32,360]{1,0:T(8,128)S(1)} %fusion.127), channel_id=1, source_target_pairs={{0,1},{1,2},{2,3},{3,4},{4,5},{5,6},{6,7},{7,8},{8,9},{9,10},{10,1... | collective-permute-start | bytes 138248 | tf_op jit(solution)/shard_map/ppermute | solution.py:56
  172.8 6.6 %collective-permute-start.15 = (f32[32,360]{1,0:T(8,128)S(1)}, f32[32,360]{1,0:T(8,128)S(1)}, u32[]{:S(2)}, u32[]{:S(2)}) collective-permute-start(f32[32,360]{1,0:T(8,128)S(1)} %fusion.127), channel_id=1, source_target_pairs={{1,0},{2,1},{3,2},{4,3},{5,4},{6,5},{7,6},{8,7},{9,8},{10,9},{11,1... | collective-permute-start | bytes 138248 | tf_op jit(solution)/shard_map/ppermute | solution.py:57
  180.8 6.0 %collective-permute-start.16 = (f32[32,360]{1,0:T(8,128)S(1)}, f32[32,360]{1,0:T(8,128)S(1)}, u32[]{:S(2)}, u32[]{:S(2)}) collective-permute-start(f32[32,360]{1,0:T(8,128)S(1)} %fusion.151), channel_id=1, source_target_pairs={{0,1},{1,2},{2,3},{3,4},{4,5},{5,6},{6,7},{7,8},{8,9},{9,10},{10,1... | collective-permute-start | bytes 138248 | tf_op jit(solution)/shard_map/ppermute | solution.py:56
  184.7 6.7 %collective-permute-start.17 = (f32[32,360]{1,0:T(8,128)S(1)}, f32[32,360]{1,0:T(8,128)S(1)}, u32[]{:S(2)}, u32[]{:S(2)}) collective-permute-start(f32[32,360]{1,0:T(8,128)S(1)} %fusion.151), channel_id=1, source_target_pairs={{1,0},{2,1},{3,2},{4,3},{5,4},{6,5},{7,6},{8,7},{9,8},{10,9},{11,1... | collective-permute-start | bytes 138248 | tf_op jit(solution)/shard_map/ppermute | solution.py:57
where the time goes:
time: 225 us; the launch traced here: 223 us
  starting transfers between devices  90.2 us (40%)
  waiting for transfers between devices  51.6 us (23%)
  blocking collectives  28.9 us (13%)
  local copies, waits for them, and re-layouts  18.2 us (8%)
  other arithmetic  17.7 us (8%)
  matrix products  15 us (7%)
    ppermute x8, waiting for transfers between devices, extended_2(): lax.ppermute(initial, axis, [(b, a) for a, b in up])  31.8 us
    ppermute x8, starting transfers between devices, extended_2(): lax.ppermute(last, axis, up)  29.9 us
    all_to_all x1, blocking collectives, copy_for_each(): return lax.all_to_all(copies, axis, split_axis=0, concat_axis=0, tiled=True)  28.9 us
    all_to_all x3, starting transfers between devices, copy_for_each(): return lax.all_to_all(copies, axis, split_axis=0, concat_axis=0, tiled=True)  27.9 us
    ppermute x8, starting transfers between devices, extended_2(): lax.ppermute(initial, axis, [(b, a) for a, b in up])  17.6 us
    all_to_all x1, waiting for transfers between devices, sum_at_owner(): pieces = lax.all_to_all(cut_along(shard, dim, size), axis, 0, 0, tiled=True)  9.57 us
    all_to_all x3, waiting for transfers between devices, copy_for_each(): return lax.all_to_all(copies, axis, split_axis=0, concat_axis=0, tiled=True)  9.01 us
    another operation x6, other arithmetic, inverse(): lower = jnp.linalg.cholesky(matrix)  7.19 us
  transfers between devices with their start and end apart: 22, of which 17 were waited for; matrix products, arithmetic and copies ran while one was open for 17% of the time, Pallas kernels for 0%

commit v1 on v0

v1 whole, which is shorter than its diff:
```python
import jax
import jax.numpy as jnp
from jax import lax
from jax.experimental import pallas as pl
from jax.experimental.pallas import tpu as pltpu
from jax.sharding import PartitionSpec as P

RANK = 32
NLON = 360
ROWS = 16
SWEEPS = 8
LANES = 128
PARTS = 4
WIDTH = NLON // PARTS
HIGHEST = lax.Precision.HIGHEST
F32 = jnp.float32
NT = (((1,), (1,)), ((), ()))

Y_GROUPS = [[y * 4 + z for y in range(4)] for z in range(4)]
Z_GROUPS = [[y * 4 + z for z in range(4)] for y in range(4)]
SWAP_NEAR = [(i, i ^ 1) for i in range(16)]
SWAP_FAR = [(i, (i + 1) % 16 if i % 2 else (i - 1) % 16) for i in range(16)]


def lane_iota(rows):
    return lax.broadcasted_iota(jnp.int32, (rows, LANES), 1)


def row_iota(rows):
    return lax.broadcasted_iota(jnp.int32, (rows, LANES), 0)


def turn(x, shift):
    shift = shift % LANES
    return x if shift == 0 else pltpu.roll(x, shift, axis=1)


def packed(rep, width):
    lane = lane_iota(8)
    total = jnp.zeros((8, LANES), F32)
    for g in range(4):
        here = (lane >= g * width) & (lane < (g + 1) * width)
        total = jnp.where(here, rep[8 * g : 8 * g + 8], total)
    return total


def unpacked(pack, width, at):
    lane = lane_iota(8)
    keep = (lane >= at) & (lane < at + width)
    tiles = [jnp.where(keep, turn(pack, at - g * width), 0.0) for g in range(4)]
    return jnp.concatenate(tiles, axis=0)


def eliminated(a):
    row = row_iota(RANK)
    for k in range(RANK):
        pivot_row = a[k : k + 1, :]
        q = pivot_row / pivot_row[:, k : k + 1]
        a = jnp.where(row == k, q, a - a[:, k : k + 1] * q)
    return a


def project_kernel(data_ref, space_ref, vf_ref, out_ref, proj_ref, gram_ref):
    step = pl.program_id(0)

    @pl.when(step == 0)
    def _():
        proj_ref[...] = jnp.zeros_like(proj_ref)
        gram_ref[...] = jnp.zeros_like(gram_ref)

    space = space_ref[...]
    data = data_ref[...].reshape(LANES, space.shape[1])
    proj_ref[...] += lax.dot_general(space, data, NT, precision=HIGHEST, preferred_element_type=F32)
    four = jnp.concatenate([space] * 4, axis=0)
    gram_ref[...] += lax.dot_general(space, four, NT, precision=HIGHEST, preferred_element_type=F32)

    @pl.when(step == pl.num_programs(0) - 1)
    def _():
        rhs = proj_ref[...] * vf_ref[...]
        for s in (64, 32, 16):
            rhs = rhs + turn(rhs, s)
        g = packed(gram_ref[...], 32)
        r = packed(rhs, 16)
        for k in range(16):
            out_ref[k, :, 0:128] = g
            out_ref[k, :, 128:256] = r


def project(data, space, vf_lanes):
    chunk = 1152
    return pl.pallas_call(
        project_kernel,
        grid=(5760 // chunk,),
        in_specs=[
            pl.BlockSpec((8, 16, chunk), lambda i: (0, 0, i)),
            pl.BlockSpec((RANK, chunk), lambda i: (0, i)),
            pl.BlockSpec((RANK, LANES), lambda i: (0, 0)),
        ],
        out_specs=pl.BlockSpec((16, 8, 256), lambda i: (0, 0, 0)),
        out_shape=jax.ShapeDtypeStruct((16, 8, 256), F32),
        scratch_shapes=[pltpu.VMEM((RANK, LANES), F32), pltpu.VMEM((RANK, LANES), F32)],
        name="project",
    )(data, space, vf_lanes)


def window(ref, start):
    count = ref.shape[1] // LANES
    t0, off = start // LANES, start % LANES
    lo = ref[:, t0 * LANES : (t0 + 1) * LANES] if 0 <= t0 < count else None
    t1 = t0 + 1
    hi = ref[:, t1 * LANES : (t1 + 1) * LANES] if off and 0 <= t1 < count else None
    if lo is None:
        return turn(hi, -off)
    if hi is None:
        return turn(lo, -off)
    lane = lane_iota(ref.shape[0])
    return jnp.where(lane < LANES - off, turn(lo, -off), turn(hi, -off))


def hour_kernel(got_ref, side_ref, vg_ref, vf_ref, data_ref, tf_ref, out_ref, dbuf, terms, sem):
    copy = pltpu.make_async_copy(data_ref, dbuf, sem)
    copy.start()
    total = got_ref[0]
    for k in range(1, 16):
        total = total + got_ref[k]
    lane = lane_iota(RANK)
    eye = jnp.where(lane == row_iota(RANK), 1.0, 0.0)
    gram = unpacked(total[:, 0:128], 32, 0)
    rhs = unpacked(total[:, 128:256], 16, 32)
    a = gram * vg_ref[...] + 3.0 * eye + rhs + side_ref[...]
    a = eliminated(a)
    tf = jnp.where((lane >= 32) & (lane < 48), a, 0.0)
    tf_ref[...] = turn(tf, -32)[:, 0:16]
    four = jnp.concatenate([tf] * 4, axis=0)
    hour_gram = packed(
        lax.dot_general(tf, four, NT, precision=HIGHEST, preferred_element_type=F32), 32
    )
    rep = tf
    for s in (64, 32, 16):
        rep = rep + turn(rep, s)
    weighted = rep * vf_ref[...]
    copy.wait()
    for c in range(5):
        at = slice(c * 1152, (c + 1) * 1152)
        terms[:, at] = jnp.dot(
            weighted,
            dbuf[:, :, at].reshape(LANES, 1152),
            precision=HIGHEST,
            preferred_element_type=F32,
        )
    for i in range(ROWS):
        base = i * NLON
        for y in range(PARTS):
            w = window(terms, base + y * WIDTH - 8)
            if y == 0:
                w = jnp.where(lane < 8, window(terms, base + NLON - 8), w)
            if y == PARTS - 1:
                w = jnp.where(lane < 98, w, window(terms, base - 98))
            for z in range(4):
                out_ref[y * 4 + z, :, i * LANES : (i + 1) * LANES] = w[8 * z : 8 * z + 8]
    for k in range(16):
        out_ref[k, :, ROWS * LANES :] = hour_gram


def hour_mode(got, side, vg_lanes, vf_lanes, data):
    vmem = pl.BlockSpec(memory_space=pltpu.VMEM)
    return pl.pallas_call(
        hour_kernel,
        in_specs=[vmem, vmem, vmem, vmem, pl.BlockSpec(memory_space=pl.ANY)],
        out_specs=(vmem, vmem),
        out_shape=(
            jax.ShapeDtypeStruct((RANK, 16), F32),
            jax.ShapeDtypeStruct((16, 8, ROWS * LANES + LANES), F32),
        ),
        scratch_shapes=[
            pltpu.VMEM((8, 16, 5760), F32),
            pltpu.VMEM((RANK, 5760), F32),
            pltpu.SemaphoreType.DMA,
        ],
        name="hour_mode",
    )(got, side, vg_lanes, vf_lanes, data)


def total_kernel(got_ref, piece_ref, gram_ref):
    for c in range(ROWS + 1):
        at = slice(c * LANES, (c + 1) * LANES)
        total = got_ref[0, :, at]
        for k in range(1, 16):
            total = total + got_ref[k, :, at]
        if c < ROWS:
            for k in range(4):
                piece_ref[k, :, at] = total
        else:
            gram_ref[...] = total


def totals(got):
    vmem = pl.BlockSpec(memory_space=pltpu.VMEM)
    return pl.pallas_call(
        total_kernel,
        in_specs=[vmem],
        out_specs=(vmem, vmem),
        out_shape=(
            jax.ShapeDtypeStruct((4, 8, ROWS * LANES), F32),
            jax.ShapeDtypeStruct((8, LANES), F32),
        ),
        name="totals",
    )(got)


def operator_kernel(gram_ref, vg_ref, weight_ref, scale_ref):
    lane = lane_iota(RANK)
    row = row_iota(RANK)
    on_diag = lane == row
    gram = unpacked(gram_ref[...], 32, 0)
    diag = jnp.where(on_diag, gram, 0.0)
    scale_col = jnp.sqrt(jnp.sum(diag, axis=1, keepdims=True) + 1e-06)
    scale_row = jnp.sqrt(jnp.sum(diag, axis=0, keepdims=True) + 1e-06)
    op = gram / (scale_col * scale_row) * vg_ref[...] + 2.0 * jnp.where(on_diag, 1.0, 0.0)
    a = eliminated(op + jnp.where(lane == row + 32, 1.0, 0.0))
    inv = jnp.where((lane >= 32) & (lane < 64), a, 0.0)
    high = inv.astype(jnp.bfloat16).astype(F32)
    low = inv - high
    weight = turn(high, -32) + high + turn(low, 32) + turn(low, 64)
    weight_ref[...] = weight.astype(jnp.bfloat16)
    scale_ref[...] = jnp.broadcast_to(scale_col, (RANK, LANES))


def operator(gram, vg_lanes):
    vmem = pl.BlockSpec(memory_space=pltpu.VMEM)
    return pl.pallas_call(
        operator_kernel,
        in_specs=[vmem, vmem],
        out_specs=(vmem, vmem),
        out_shape=(
            jax.ShapeDtypeStruct((RANK, LANES), jnp.bfloat16),
            jax.ShapeDtypeStruct((RANK, LANES), F32),
        ),
        name="operator",
        cost_estimate=pl.CostEstimate(flops=10_000_000, bytes_accessed=100_000, transcendentals=0),
    )(gram, vg_lanes)


EXT = ROWS + 16


def sweep_kernel(even_ref, rhs_ref, near_ref, far_ref, start_ref, weight_ref, scale_ref, out_ref, state, rhs, x4):
    even = even_ref[0] == 1
    scale = scale_ref[...]
    for i in range(1, EXT - 1):
        at = slice(i * LANES, (i + 1) * LANES)
        if i < 8:
            h = slice((i - 1) * LANES, i * LANES)
            v = jnp.where(even, far_ref[:, h], near_ref[:, h])
        elif i < 8 + ROWS:
            v = rhs_ref[:, (i - 8) * LANES : (i - 7) * LANES]
        else:
            h = slice((i - 24) * LANES, (i - 23) * LANES)
            v = jnp.where(even, near_ref[:, h], far_ref[:, h])
        rhs[:, at] = v / scale
    for i in range(EXT):
        at = slice(i * LANES, (i + 1) * LANES)
        state[:, at] = start_ref[0:RANK, at]
    weight = weight_ref[...]

    def line(i):
        c = state[:, i * LANES : (i + 1) * LANES]
        return (turn(c, -1), c, turn(c, 1))

    def pick(code, triple):
        ahead, same, behind = triple
        return jnp.where(
            code == 2.0,
            ahead,
            jnp.where(code == 3.0, behind, jnp.where(code == 1.0, same, 0.0)),
        )

    def sweep(_, carry):
        before, here = line(0), line(1)
        for i in range(1, EXT - 1):
            at = slice(i * LANES, (i + 1) * LANES)
            after = line(i + 1)
            north = jnp.broadcast_to(start_ref[RANK : RANK + 1, at], (RANK, LANES))
            south = jnp.broadcast_to(start_ref[RANK + 1 : RANK + 2, at], (RANK, LANES))
            near = here[0] + here[2] + pick(north, before) + pick(south, after)
            x = rhs[:, at] + 0.5 * near
            high = x.astype(jnp.bfloat16)
            low = (x - high.astype(F32)).astype(jnp.bfloat16)
            x4[0:32, at] = high
            x4[32:64, at] = low
            x4[64:96, at] = high
            x4[96:128, at] = low
            before, here = here, after
        for c in range(EXT // 2):
            first, last = max(1, 2 * c), min(EXT - 1, 2 * c + 2)
            at = slice(first * LANES, last * LANES)
            state[:, at] = jnp.dot(weight, x4[:, at], preferred_element_type=F32)
        return carry

    lax.fori_loop(0, SWEEPS, sweep, 0)
    lane = lane_iota(RANK)
    tiles = {}
    for i in range(ROWS):
        c = state[:, (8 + i) * LANES : (9 + i) * LANES]
        t, off = i * WIDTH // LANES, i * WIDTH % LANES
        moved = turn(c, off - 8)
        tiles[t] = jnp.where(lane < off, tiles[t], moved) if t in tiles else moved
        if off + WIDTH > LANES:
            tiles[t + 1] = moved
    for t in sorted(tiles):
        for k in range(PARTS):
            out_ref[k, :, t * LANES : (t + 1) * LANES] = tiles[t]


def sweeps(even, rhs, near, far, start, weight, scale):
    vmem = pl.BlockSpec(memory_space=pltpu.VMEM)
    return pl.pallas_call(
        sweep_kernel,
        in_specs=[pl.BlockSpec(memory_space=pltpu.SMEM)] + [vmem] * 6,
        out_specs=vmem,
        out_shape=jax.ShapeDtypeStruct((PARTS, RANK, 12 * LANES), F32),
        scratch_shapes=[
            pltpu.VMEM((RANK, EXT * LANES), F32),
            pltpu.VMEM((RANK, EXT * LANES), F32),
            pltpu.VMEM((4 * RANK, EXT * LANES), jnp.bfloat16),
        ],
        name="sweeps",
    )(even, rhs, near, far, start, weight, scale)


def join_kernel(got_ref, out_ref):
    lane = lane_iota(RANK)
    tiles = {}
    for i in range(ROWS):
        for y in range(PARTS):
            src, dst = i * WIDTH, i * NLON + y * WIDTH
            w = window(got_ref.at[y], src)
            t, off = dst // LANES, dst % LANES
            moved = turn(w, off)
            tiles[t] = jnp.where(lane < off, tiles[t], moved) if t in tiles else moved
            if off + WIDTH > LANES:
                tiles[t + 1] = moved
    for t in sorted(tiles):
        out_ref[:, t * LANES : (t + 1) * LANES] = tiles[t]


def join(got):
    vmem = pl.BlockSpec(memory_space=pltpu.VMEM)
    return pl.pallas_call(
        join_kernel,
        in_specs=[vmem],
        out_specs=vmem,
        out_shape=jax.ShapeDtypeStruct((RANK, ROWS * NLON), F32),
        name="join",
    )(got)


def link_codes(links):
    column = jnp.arange(links.shape[1], dtype=jnp.int32) % NLON
    target = (links % NLON - column + NLON) % NLON
    code = jnp.where(target == 1, 2.0, jnp.where(target == NLON - 1, 3.0, 1.0))
    return jnp.where(links >= 0, code, 0.0).astype(F32)


def swapped(edge_near, edge_far):
    return (
        lax.ppermute(edge_near, "lat", SWAP_NEAR),
        lax.ppermute(edge_far, "lat", SWAP_FAR),
    )


def edges(block, rows, even):
    width = rows * LANES
    top, bottom = block[:, :width], block[:, block.shape[1] - width :]
    return swapped(jnp.where(even, bottom, top), jnp.where(even, top, bottom))


def per_device(data, space_init, time_init, variable_factor, neighbours):
    tm = lax.axis_index("tm")
    lat = lax.axis_index("lat")
    even = lat % 2 == 0
    part = tm // 4
    vf_lanes = jnp.repeat(variable_factor.T, 16, axis=1)
    var_gram = jnp.dot(variable_factor.T, variable_factor, precision=HIGHEST, preferred_element_type=F32)
    vg_lanes = jnp.pad(var_gram, ((0, 0), (0, LANES - RANK)))

    sums = project(data, space_init, vf_lanes)
    got = lax.all_to_all(sums, "lat", 0, 0, tiled=True)

    low = lax.ppermute(time_init[:, -2:], "tm", [(i, (i + 1) % 16) for i in range(16)])
    high = lax.ppermute(time_init[:, :2], "tm", [((i + 1) % 16, i) for i in range(16)])
    low = jnp.where(tm == 0, 0.0, low)
    high = jnp.where(tm == 15, 0.0, high)
    padded = jnp.concatenate([low, time_init, high], axis=1)
    stencil = padded[:, :-4] - 4.0 * padded[:, 1:-3] - 4.0 * padded[:, 3:-1] + padded[:, 4:]
    side = jnp.pad(-0.5 * stencil, ((0, 0), (32, 80)))

    own = jnp.concatenate([space_init, link_codes(neighbours[2:4])], axis=0)
    own = own.reshape(RANK + 2, ROWS, NLON)
    own = jnp.concatenate([own[:, :, NLON - 8 :], own, own[:, :, :30]], axis=2)
    own = lax.dynamic_slice_in_dim(own, part * WIDTH, LANES, axis=2)
    own = own.reshape(RANK + 2, ROWS * LANES)
    start_near, start_far = edges(own, 8, even)
    start = jnp.concatenate(
        [
            jnp.where(even, start_far, start_near),
            own,
            jnp.where(even, start_near, start_far),
        ],
        axis=1,
    )

    time_factor, terms = hour_mode(got, side, vg_lanes, vf_lanes, data)
    got = lax.all_to_all(terms, "tm", 0, 0, tiled=True)
    pieces, gram = totals(got)
    rhs = lax.all_to_all(pieces, "tm", 0, 0, tiled=True, axis_index_groups=Z_GROUPS)
    weight, scale = operator(gram, vg_lanes)
    rhs = rhs.reshape(RANK, ROWS * LANES)
    near, far = edges(rhs, 7, even)
    even_flag = jnp.where(even, 1, 0).astype(jnp.int32).reshape(1)
    blocks = sweeps(even_flag, rhs, near, far, start, weight, scale)
    blocks = lax.all_to_all(blocks, "tm", 0, 0, tiled=True, axis_index_groups=Y_GROUPS)
    return (time_factor, join(blocks))


def solution(mesh):
    placed = (P(None, "tm", "lat"), P(None, "lat"), P(None, "tm"), P(), P(None, "lat"))
    return jax.shard_map(
        per_device,
        mesh=mesh,
        in_specs=placed,
        out_specs=(P(None, "tm"), P(None, "lat")),
        check_vma=False,
    )
```

time: 225 us -> 140 us (0.62)
  starting transfers between devices: 90.2 us -> 37.8 us
  Pallas kernels: 0 us -> 34.5 us
  blocking collectives: 28.9 us -> 0 us
  other arithmetic: 17.7 us -> 1.72 us
  matrix products: 15 us -> 0.2 us
  local copies, waits for them, and re-layouts: 18.2 us -> 7.7 us
  waiting for transfers between devices: 51.6 us -> 56.4 us
    ppermute x18 -> x6, starting transfers between devices: 55.4 us -> 9.69 us  [the longest x2 7.55 us: swapped(): lax.ppermute(edge_far, 'lat', SWAP_FAR)]
    pallas_call x0 -> x6, Pallas kernels: none -> 34.5 us  [the longest x1 8.46 us: project(): pl.pallas_call(project_kernel, grid=(5760 // chunk,), in_specs=[pl.BlockS...]
    all_to_all x1 -> x0, blocking collectives: 28.9 us -> none  [copy_for_each(): return lax.all_to_all(copies, axis, split_axis=0, concat_axis=0, tiled=True)]
    all_to_all x4, waiting for transfers between devices: 18.6 us -> 38.1 us  [the longest x1 23.2 us: per_device(): got = lax.all_to_all(terms, 'tm', 0, 0, tiled=True)]
    ppermute x18 -> x6, waiting for transfers between devices: 33.1 us -> 18.3 us  [the longest x2 13.2 us: swapped(): lax.ppermute(edge_far, 'lat', SWAP_FAR)]
    dot_general x14 -> x1, matrix products: 14.2 us -> 0.2 us  [per_device(): jnp.dot(variable_factor.T, variable_factor, precision=HIGHEST, preferred_...]
    another operation x10 -> x0, other arithmetic: 13.4 us -> none  [the longest x6 7.19 us: inverse(): lower = jnp.linalg.cholesky(matrix)]
    all_to_all x4, starting transfers between devices: 34.8 us -> 28.2 us  [the longest x1 10.1 us: per_device(): got = lax.all_to_all(sums, 'lat', 0, 0, tiled=True)]
  transfers between devices with their start and end apart: 22 -> 10, of which waited for: 17 -> 7; matrix products, arithmetic and copies ran while one was open for 17% -> 4% of each run, Pallas kernels for 0% -> 3%
where the time goes in v1:
time: 140 us; the launch traced here: 139 us
  waiting for transfers between devices  56.4 us (40%)
  starting transfers between devices  37.8 us (27%)
  Pallas kernels  34.5 us (25%)
  local copies, waits for them, and re-layouts  7.7 us (6%)
  other arithmetic  1.72 us (1%)
    all_to_all x1, waiting for transfers between devices, per_device(): got = lax.all_to_all(terms, 'tm', 0, 0, tiled=True)  23.2 us
    ppermute x2, waiting for transfers between devices, swapped(): lax.ppermute(edge_far, 'lat', SWAP_FAR)  13.2 us
    all_to_all x1, waiting for transfers between devices, per_device(): lax.all_to_all(blocks, 'tm', 0, 0, tiled=True, axis_index_groups=Y_GROUPS)  11.7 us
    all_to_all x1, starting transfers between devices, per_device(): got = lax.all_to_all(sums, 'lat', 0, 0, tiled=True)  10.1 us
    pallas_call x1, Pallas kernels, project(): pl.pallas_call(project_kernel, grid=(5760 // chunk,), in_specs=[pl.BlockS...  8.46 us
    all_to_all x1, starting transfers between devices, per_device(): lax.all_to_all(pieces, 'tm', 0, 0, tiled=True, axis_index_groups=Z_GROUPS)  7.69 us
    ppermute x2, starting transfers between devices, swapped(): lax.ppermute(edge_far, 'lat', SWAP_FAR)  7.55 us
    pallas_call x1, Pallas kernels, sweeps(): pl.pallas_call(sweep_kernel, in_specs=[pl.BlockSpec(memory_space=pltpu.SM...  7.19 us
  transfers between devices with their start and end apart: 10, of which 7 were waited for; matrix products, arithmetic and copies ran while one was open for 4% of the time, Pallas kernels for 3%

profile of v1, /device:TPU:32, one launch (start us, length us, event | category | flops | bytes accessed | tf_op | source)
XLA Modules:
  0.0 139.3 jit_solution(460594085135048980)
XLA Ops:
  0.6 0.7 broadcast_in_dim.25
  1.3 0.7 copy.13.vf_ref
  2.0 8.5 %project.1 = f32[16,8,256]{2,1,0:T(8,128)} custom-call(f32[8,16,5760]{2,1,0:T(8,128)} %data_ref.3, f32[32,5760]{1,0:T(8,128)} %space_ref.1, f32[32,128]{1,0:T(8,128)} %copy.13.vf_ref), custom_call_target="tpu_custom_call" | custom-call | tf_op jit(solution)/shard_map/project/pallas_call | solution.py:91
  10.5 10.1 %all-to-all-start = ((f32[16,8,256]{2,1,0:T(8,128)}), f32[16,8,256]{2,1,0:T(8,128)S(1)}, u32[]{:S(2)}, u32[]{:S(2)}) async-start(f32[16,8,256]{2,1,0:T(8,128)} %project.1), calls=%async_computation | async-start | bytes 262144 | tf_op jit(solution)/shard_map/all_to_all | solution.py:388
  20.8 1.0 collective-permute-start.1
  21.8 1.0 collective-permute-start
  23.1 0.6 pad.9.vg_ref
  23.7 1.6 %collective-permute-done.1 = f32[32,2]{1,0:T(8,128)S(1)} collective-permute-done((f32[32,2]{1,0:T(8,128)S(1)}, f32[32,2]{1,0:T(8,128)S(1)}, u32[]{:S(2)}, u32[]{:S(2)}) %collective-permute-start.1) | collective-permute-done | bytes 288 | tf_op jit(solution)/shard_map/ppermute | solution.py:391
  25.3 3.5 %collective-permute-done = f32[32,2]{1,0:T(8,128)S(1)} collective-permute-done((f32[32,2]{1,0:T(8,128)S(1)}, f32[32,2]{1,0:T(8,128)S(1)}, u32[]{:S(2)}, u32[]{:S(2)}) %collective-permute-start) | collective-permute-done | bytes 288 | tf_op jit(solution)/shard_map/ppermute | solution.py:390
  28.9 0.7 pad.8.side_ref
  29.6 3.1 %all-to-all-done.got_ref = f32[16,8,256]{2,1,0:T(8,128)S(1)} async-done(((f32[16,8,256]{2,1,0:T(8,128)}), f32[16,8,256]{2,1,0:T(8,128)S(1)}, u32[]{:S(2)}, u32[]{:S(2)}) %all-to-all-start) | async-done | bytes 131104 | tf_op jit(solution)/shard_map/all_to_all | solution.py:388
  32.7 0.7 copy-done.4
  33.4 6.6 %hour_mode.1 = (f32[32,16]{1,0:T(8,128)}, f32[16,8,2176]{2,1,0:T(8,128)}) custom-call(f32[16,8,256]{2,1,0:T(8,128)} %copy-done.4, f32[32,128]{1,0:T(8,128)} %pad.8.side_ref, f32[32,128]{1,0:T(8,128)} %pad.9.vg_ref, f32[32,128]{1,0:T(8,128)} %copy.13.vf_ref, f32[8,16,5760]{2,1,0:T(8,128)} %data_ref.3), custom_call_target="tpu_custom_call" | custom-call | tf_op jit(solution)/shard_map/hour_mode/pallas_call | solution.py:167
  40.0 6.7 %all-to-all-start.1 = ((f32[16,8,2176]{2,1,0:T(8,128)}), f32[16,8,2176]{2,1,0:T(8,128)S(1)}, u32[]{:S(2)}, u32[]{:S(2)}) async-start(f32[16,8,2176]{2,1,0:T(8,128)} %get-tuple-element.9), calls=%async_computation.1 | async-start | bytes 2228224 | tf_op jit(solution)/shard_map/all_to_all | solution.py:414
  47.1 0.7 reshape.31
  48.5 23.2 %all-to-all-done.1.got_ref = f32[16,8,2176]{2,1,0:T(8,128)S(1)} async-done(((f32[16,8,2176]{2,1,0:T(8,128)}), f32[16,8,2176]{2,1,0:T(8,128)S(1)}, u32[]{:S(2)}, u32[]{:S(2)}) %all-to-all-start.1) | async-done | bytes 1114144 | tf_op jit(solution)/shard_map/all_to_all | solution.py:414
  71.7 1.0 copy-done
  72.7 2.0 %totals.1 = (f32[4,8,2048]{2,1,0:T(8,128)}, f32[8,128]{1,0:T(8,128)}) custom-call(f32[16,8,2176]{2,1,0:T(8,128)} %copy-done), custom_call_target="tpu_custom_call" | custom-call | tf_op jit(solution)/shard_map/totals/pallas_call | solution.py:199
  74.7 7.7 %all-to-all-start.2 = ((f32[4,8,2048]{2,1,0:T(8,128)}), f32[4,8,2048]{2,1,0:T(8,128)S(1)}, u32[]{:S(2)}, u32[]{:S(2)}) async-start(f32[4,8,2048]{2,1,0:T(8,128)} %get-tuple-element.10), calls=%async_computation.2 | async-start | bytes 524288 | tf_op jit(solution)/shard_map/all_to_all | solution.py:416
  82.5 4.2 %collective-permute-start.4 = (f32[34,1024]{1,0:T(8,128)S(1)}, f32[34,1024]{1,0:T(8,128)S(1)}, u32[]{:S(2)}, u32[]{:S(2)}) collective-permute-start(f32[34,1024]{1,0:T(8,128)S(1)} %get-tuple-element.20), channel_id=1, source_target_pairs={{0,240},{16,32},{32,16},{48,64},{64,48},{80,96},{96,80},{112,128},... | collective-permute-start | bytes 417800 | tf_op jit(solution)/shard_map/ppermute | solution.py:368
  86.6 11.2 %collective-permute-done.4 = f32[34,1024]{1,0:T(8,128)S(1)} collective-permute-done((f32[34,1024]{1,0:T(8,128)S(1)}, f32[34,1024]{1,0:T(8,128)S(1)}, u32[]{:S(2)}, u32[]{:S(2)}) %collective-permute-start.4) | collective-permute-done | bytes 139296 | tf_op jit(solution)/shard_map/ppermute | solution.py:368
  98.0 3.4 %collective-permute-start.3 = (f32[32,896]{1,0:T(8,128)S(1)}, f32[32,896]{1,0:T(8,128)S(1)}, u32[]{:S(2)}, u32[]{:S(2)}) collective-permute-start(f32[32,896]{1,0:T(8,128)S(1)} %get-tuple-element.22), channel_id=1, source_target_pairs={{0,240},{16,32},{32,16},{48,64},{64,48},{80,96},{96,80},{112,128},... | collective-permute-start | bytes 344072 | tf_op jit(solution)/shard_map/ppermute | solution.py:368
  101.4 0.9 pad_maximum_fusion.1.start_ref
  102.3 4.2 %operator.1 = (bf16[32,128]{1,0:T(8,128)(2,1)}, f32[32,128]{1,0:T(8,128)}) custom-call(f32[8,128]{1,0:T(8,128)} %get-tuple-element.11.gram_ref, f32[32,128]{1,0:T(8,128)} %pad.9.vg_ref), custom_call_target="tpu_custom_call" | custom-call | flops 10000000 | bytes 100000 | tf_op jit(solution)/shard_map/operator/pallas_call | solution.py:231
  106.5 1.9 %collective-permute-done.3.far_ref = f32[32,896]{1,0:T(8,128)S(1)} collective-permute-done((f32[32,896]{1,0:T(8,128)S(1)}, f32[32,896]{1,0:T(8,128)S(1)}, u32[]{:S(2)}, u32[]{:S(2)}) %collective-permute-start.3) | collective-permute-done | bytes 114720 | tf_op jit(solution)/shard_map/ppermute | solution.py:368
  108.5 0.6 copy-done.6
  109.1 7.2 %sweeps.1 = f32[4,32,1536]{2,1,0:T(8,128)} custom-call(s32[1]{0:T(128)} %bitcast.2.even_ref, f32[32,2048]{1,0:T(8,128)} %bitcast.12, f32[32,896]{1,0:T(8,128)} %copy-done.5, f32[32,896]{1,0:T(8,128)} %copy-done.6, f32[34,4096]{1,0:T(8,128)} %pad_maximum_fusion.1.start_ref, bf16[32,128]{1,0:T(8,128)(2,1)} %get-tuple-element.12.weight_ref, ...), custom_call_target="tpu_custom_call" | custom-call | tf_op jit(solution)/shard_map/sweeps/pallas_call | solution.py:317
  116.3 3.6 %all-to-all-start.3 = ((f32[4,32,1536]{2,1,0:T(8,128)}), f32[4,32,1536]{2,1,0:T(8,128)S(1)}, u32[]{:S(2)}, u32[]{:S(2)}) async-start(f32[4,32,1536]{2,1,0:T(8,128)} %sweeps.1), calls=%async_computation.3 | async-start | bytes 1572864 | tf_op jit(solution)/shard_map/all_to_all | solution.py:422
  120.0 0.7 copy.19
  120.6 11.7 %all-to-all-done.3.got_ref = f32[4,32,1536]{2,1,0:T(8,128)S(1)} async-done(((f32[4,32,1536]{2,1,0:T(8,128)}), f32[4,32,1536]{2,1,0:T(8,128)S(1)}, u32[]{:S(2)}, u32[]{:S(2)}) %all-to-all-start.3) | async-done | bytes 786464 | tf_op jit(solution)/shard_map/all_to_all | solution.py:422
  132.4 0.9 copy-done.1
  133.3 6.0 %join.1 = f32[32,5760]{1,0:T(8,128)} custom-call(f32[4,32,1536]{2,1,0:T(8,128)} %copy-done.1), custom_call_target="tpu_custom_call" | custom-call | tf_op jit(solution)/shard_map/join/pallas_call | solution.py:349
  (40 shorter events, 1.6 us)
Async XLA Ops:
  2.0 18.6 %copy-start.10 = (f32[32,16]{0,1:T(8,128)S(1)}, f32[32,16]{0,1:T(8,128)}, u32[]{:S(2)}) copy-start(f32[32,16]{0,1:T(8,128)} %param.7) | copy-start | bytes 6148
  2.0 20.8 %copy-start.7 = (f32[8,32]{1,0:T(8,128)S(1)}, f32[8,32]{1,0:T(8,128)}, u32[]{:S(2)}) copy-start(f32[8,32]{1,0:T(8,128)} %param.8) | copy-start | bytes 3076
  10.5 22.3 %all-to-all-start = ((f32[16,8,256]{2,1,0:T(8,128)}), f32[16,8,256]{2,1,0:T(8,128)S(1)}, u32[]{:S(2)}, u32[]{:S(2)}) async-start(f32[16,8,256]{2,1,0:T(8,128)} %project.1), calls=%async_computation | async-start | bytes 262144 | tf_op jit(solution)/shard_map/all_to_all | solution.py:388
  20.8 4.5 %collective-permute-start.1 = (f32[32,2]{1,0:T(8,128)S(1)}, f32[32,2]{1,0:T(8,128)S(1)}, u32[]{:S(2)}, u32[]{:S(2)}) collective-permute-start(f32[32,2]{1,0:T(8,128)S(1)} %get-tuple-element.25), channel_id=1, source_target_pairs={{1,0},{2,1},{3,2},{4,3},{5,4},{6,5},{7,6},{8,7},{9,8},{10,9},{11,1... | collective-permute-start | bytes 776 | tf_op jit(solution)/shard_map/ppermute | solution.py:391
  21.8 7.0 %collective-permute-start = (f32[32,2]{1,0:T(8,128)S(1)}, f32[32,2]{1,0:T(8,128)S(1)}, u32[]{:S(2)}, u32[]{:S(2)}) collective-permute-start(f32[32,2]{1,0:T(8,128)S(1)} %get-tuple-element.24), channel_id=1, source_target_pairs={{0,1},{1,2},{2,3},{3,4},{4,5},{5,6},{6,7},{7,8},{8,9},{9,10},{10,1... | collective-permute-start | bytes 776 | tf_op jit(solution)/shard_map/ppermute | solution.py:390
  32.7 0.7 copy-start.4
  40.0 6.7 %copy-start.8 = (s32[4,5760]{1,0:T(4,128)S(1)}, s32[4,5760]{1,0:T(4,128)}, u32[]{:S(2)}) copy-start(s32[4,5760]{1,0:T(4,128)} %param.9) | copy-start | bytes 276484
  40.0 7.0 %copy-start.2 = (f32[32,5760]{1,0:T(8,128)S(1)}, f32[32,5760]{1,0:T(8,128)}, u32[]{:S(2)}) copy-start(f32[32,5760]{1,0:T(8,128)} %space_ref.1) | copy-start | bytes 2211844
  40.0 31.7 %all-to-all-start.1 = ((f32[16,8,2176]{2,1,0:T(8,128)}), f32[16,8,2176]{2,1,0:T(8,128)S(1)}, u32[]{:S(2)}, u32[]{:S(2)}) async-start(f32[16,8,2176]{2,1,0:T(8,128)} %get-tuple-element.9), calls=%async_computation.1 | async-start | bytes 2228224 | tf_op jit(solution)/shard_map/all_to_all | solution.py:414
  71.7 1.0 copy-start
  74.7 23.2 %all-to-all-start.2 = ((f32[4,8,2048]{2,1,0:T(8,128)}), f32[4,8,2048]{2,1,0:T(8,128)S(1)}, u32[]{:S(2)}, u32[]{:S(2)}) async-start(f32[4,8,2048]{2,1,0:T(8,128)} %get-tuple-element.10), calls=%async_computation.2 | async-start | bytes 524288 | tf_op jit(solution)/shard_map/all_to_all | solution.py:416
  82.5 15.4 %collective-permute-start.4 = (f32[34,1024]{1,0:T(8,128)S(1)}, f32[34,1024]{1,0:T(8,128)S(1)}, u32[]{:S(2)}, u32[]{:S(2)}) collective-permute-start(f32[34,1024]{1,0:T(8,128)S(1)} %get-tuple-element.20), channel_id=1, source_target_pairs={{0,240},{16,32},{32,16},{48,64},{64,48},{80,96},{96,80},{112,128},... | collective-permute-start | bytes 417800 | tf_op jit(solution)/shard_map/ppermute | solution.py:368
  86.6 11.3 %collective-permute-start.5 = (f32[34,1024]{1,0:T(8,128)S(1)}, f32[34,1024]{1,0:T(8,128)S(1)}, u32[]{:S(2)}, u32[]{:S(2)}) collective-permute-start(f32[34,1024]{1,0:T(8,128)S(1)} %get-tuple-element.21), channel_id=1, source_target_pairs={{0,16},{16,0},{32,48},{48,32},{64,80},{80,64},{96,112},{112,96},{1... | collective-permute-start | bytes 417800 | tf_op jit(solution)/shard_map/ppermute | solution.py:367
  97.9 10.6 %copy-start.3 = (f32[4,8,2048]{2,1,0:T(8,128)}, f32[4,8,2048]{2,1,0:T(8,128)S(1)}, u32[]{:S(2)}) copy-start(f32[4,8,2048]{2,1,0:T(8,128)S(1)} %all-to-all-done.2) | copy-start | bytes 786436
  97.9 8.6 %collective-permute-start.2 = (f32[32,896]{1,0:T(8,128)S(1)}, f32[32,896]{1,0:T(8,128)S(1)}, u32[]{:S(2)}, u32[]{:S(2)}) collective-permute-start(f32[32,896]{1,0:T(8,128)S(1)} %get-tuple-element.23), channel_id=1, source_target_pairs={{0,16},{16,0},{32,48},{48,32},{64,80},{80,64},{96,112},{112,96},{1... | collective-permute-start | bytes 344072 | tf_op jit(solution)/shard_map/ppermute | solution.py:367
  98.0 10.4 %collective-permute-start.3 = (f32[32,896]{1,0:T(8,128)S(1)}, f32[32,896]{1,0:T(8,128)S(1)}, u32[]{:S(2)}, u32[]{:S(2)}) collective-permute-start(f32[32,896]{1,0:T(8,128)S(1)} %get-tuple-element.22), channel_id=1, source_target_pairs={{0,240},{16,32},{32,16},{48,64},{64,48},{80,96},{96,80},{112,128},... | collective-permute-start | bytes 344072 | tf_op jit(solution)/shard_map/ppermute | solution.py:368
  106.5 2.0 %copy-start.5 = (f32[32,896]{1,0:T(8,128)}, f32[32,896]{1,0:T(8,128)S(1)}, u32[]{:S(2)}) copy-start(f32[32,896]{1,0:T(8,128)S(1)} %collective-permute-done.2.near_ref) | copy-start | bytes 344068
  108.5 0.6 copy-start.6
  116.3 3.6 %copy-start.9 = (f32[32,16]{1,0:T(8,128)S(1)}, f32[32,16]{1,0:T(8,128)}, u32[]{:S(2)}) copy-start(f32[32,16]{1,0:T(8,128)} %get-tuple-element.16) | copy-start | bytes 6148
  116.3 16.1 %all-to-all-start.3 = ((f32[4,32,1536]{2,1,0:T(8,128)}), f32[4,32,1536]{2,1,0:T(8,128)S(1)}, u32[]{:S(2)}, u32[]{:S(2)}) async-start(f32[4,32,1536]{2,1,0:T(8,128)} %sweeps.1), calls=%async_computation.3 | async-start | bytes 1572864 | tf_op jit(solution)/shard_map/all_to_all | solution.py:422
  132.4 0.9 copy-start.1

commit v2 on v1

v2 whole, which is shorter than its diff:
```python
import jax
import jax.numpy as jnp
from jax import lax
from jax.experimental import pallas as pl
from jax.experimental.pallas import tpu as pltpu
from jax.sharding import PartitionSpec as P


RANK = 32
NLON = 360
ROWS = 16
SWEEPS = 8
LANES = 128
PARTS = 4
WIDTH = NLON // PARTS
STRIDE = WIDTH + 14
PIECE = ROWS * STRIDE
HIGHEST = lax.Precision.HIGHEST
F32 = jnp.float32
NT = (((1,), (1,)), ((), ()))

Y_GROUPS = [[y * 4 + z for y in range(4)] for z in range(4)]
Z_GROUPS = [[y * 4 + z for z in range(4)] for y in range(4)]
SWAP_NEAR = [(i, i ^ 1) for i in range(16)]
SWAP_FAR = [(i, (i + 1) % 16 if i % 2 else (i - 1) % 16) for i in range(16)]


def lane_iota(rows):
    return lax.broadcasted_iota(jnp.int32, (rows, LANES), 1)


def row_iota(rows):
    return lax.broadcasted_iota(jnp.int32, (rows, LANES), 0)


def turn(x, shift):
    shift = shift % LANES
    return x if shift == 0 else pltpu.roll(x, shift, axis=1)


def packed(rep, width):
    lane = lane_iota(8)
    total = jnp.zeros((8, LANES), F32)
    for g in range(4):
        here = (lane >= g * width) & (lane < (g + 1) * width)
        total = jnp.where(here, rep[8 * g : 8 * g + 8], total)
    return total


def unpacked(pack, width, at):
    lane = lane_iota(8)
    keep = (lane >= at) & (lane < at + width)
    tiles = [jnp.where(keep, turn(pack, at - g * width), 0.0) for g in range(4)]
    return jnp.concatenate(tiles, axis=0)


def eliminated(a):
    row = row_iota(RANK)
    for k in range(RANK):
        pivot_row = a[k : k + 1, :]
        q = pivot_row / pivot_row[:, k : k + 1]
        a = jnp.where(row == k, q, a - a[:, k : k + 1] * q)
    return a


def split_3(x):
    first = x.astype(jnp.bfloat16)
    rest = x - first.astype(F32)
    second = rest.astype(jnp.bfloat16)
    third = (rest - second.astype(F32)).astype(jnp.bfloat16)
    return first, second, third


def factor_lanes(vf):
    eye = jnp.where(lax.broadcasted_iota(jnp.int32, (RANK, RANK), 0) == lax.broadcasted_iota(jnp.int32, (RANK, RANK), 1), 1.0, 0.0)
    turned = lax.dot_general(eye, vf, NT, precision=HIGHEST, preferred_element_type=F32)
    chosen = jnp.where(lane_iota(8) // 16 == row_iota(8), 1.0, 0.0)
    return jnp.dot(turned, chosen, precision=HIGHEST, preferred_element_type=F32)


def project_kernel(data_ref, space_ref, vf_ref, out_ref, acc_ref):
    step = pl.program_id(0)

    @pl.when(step == 0)
    def _():
        acc_ref[...] = jnp.zeros_like(acc_ref)

    space = space_ref[...]
    data = data_ref[...].reshape(LANES, space.shape[1])
    d1, d2, d3 = split_3(data)
    s1, s2, s3 = split_3(space)
    x1 = jnp.concatenate([d1, s1], axis=0)
    x2 = jnp.concatenate([d2, s2], axis=0)
    x3 = jnp.concatenate([d3, s3], axis=0)
    p1 = lax.dot_general(jnp.concatenate([s1, s2, s3], axis=0), x1, NT, preferred_element_type=F32)
    p2 = lax.dot_general(jnp.concatenate([s1, s2], axis=0), x2, NT, preferred_element_type=F32)
    p3 = lax.dot_general(s1, x3, NT, preferred_element_type=F32)
    small = p1[64:96] + p2[32:64] + p3
    acc_ref[...] += p1[0:32] + (p1[32:64] + p2[0:32] + small)

    @pl.when(step == pl.num_programs(0) - 1)
    def _():
        rhs = acc_ref[:, 0:LANES] * factor_lanes(vf_ref[...])
        for s in (64, 32, 16):
            rhs = rhs + turn(rhs, s)
        gram = jnp.concatenate([acc_ref[:, LANES:]] * 4, axis=1)
        g = packed(gram, 32)
        r = packed(rhs, 16)
        for k in range(16):
            out_ref[k, :, 0:128] = g
            out_ref[k, :, 128:256] = r


def project(data, space, vf):
    chunk = 1152
    return pl.pallas_call(
        project_kernel,
        grid=(5760 // chunk,),
        in_specs=[
            pl.BlockSpec((8, 16, chunk), lambda i: (0, 0, i)),
            pl.BlockSpec((RANK, chunk), lambda i: (0, i)),
            pl.BlockSpec((8, RANK), lambda i: (0, 0)),
        ],
        out_specs=pl.BlockSpec((16, 8, 256), lambda i: (0, 0, 0)),
        out_shape=jax.ShapeDtypeStruct((16, 8, 256), F32),
        scratch_shapes=[pltpu.VMEM((RANK, LANES + RANK), F32)],
        cost_estimate=pl.CostEstimate(flops=4_000_000_000, bytes_accessed=8_000_000, transcendentals=0),
        name="project",
    )(data, space, vf)


def grant(mebibytes):
    return pltpu.CompilerParams(vmem_limit_bytes=mebibytes * 1024 * 1024)


def pack_pieces(pieces, width, store):
    lane = lane_iota(RANK)
    held = None
    for i, piece in enumerate(pieces):
        t, off = divmod(i * width, LANES)
        moved = turn(piece, off)
        value = moved if off == 0 else jnp.where(lane < off, held, moved)
        if off + width >= LANES:
            store(t, value)
            held = moved
        else:
            held = value
    if (i + 1) * width % LANES:
        store((i + 1) * width // LANES, held)


def spot(start):
    return lax.div(start, LANES), lax.rem(start, LANES)


def placed(ref, start, to):
    t, off = divmod(start, LANES)
    lo, hi = ref[:, t * LANES : (t + 1) * LANES], ref[:, (t + 1) * LANES : (t + 2) * LANES]
    return turn(jnp.where(lane_iota(RANK) >= off, lo, hi), to - off)


def window(ref, start):
    count = ref.shape[1] // LANES
    t0, off = start // LANES, start % LANES
    lo = ref[:, t0 * LANES : (t0 + 1) * LANES] if 0 <= t0 < count else None
    t1 = t0 + 1
    hi = ref[:, t1 * LANES : (t1 + 1) * LANES] if off and 0 <= t1 < count else None
    if lo is None:
        return turn(hi, -off)
    if hi is None:
        return turn(lo, -off)
    return turn(jnp.where(lane_iota(ref.shape[0]) >= off, lo, hi), -off)


def tile(t):
    return pl.ds(pl.multiple_of(t * LANES, LANES), LANES)


def hour_kernel(got_ref, side_ref, vg_ref, vf_ref, data_ref, tf_ref, out_ref, dbuf, terms, sem):
    copy = pltpu.make_async_copy(data_ref, dbuf, sem)
    copy.start()
    total = got_ref[0]
    for k in range(1, 16):
        total = total + got_ref[k]
    lane = lane_iota(RANK)
    eye = jnp.where(lane == row_iota(RANK), 1.0, 0.0)
    gram = unpacked(total[:, 0:128], 32, 0)
    rhs = unpacked(total[:, 128:256], 16, 32)
    a = gram * vg_ref[...] + 3.0 * eye + rhs + side_ref[...]
    a = eliminated(a)
    tf = jnp.where((lane >= 32) & (lane < 48), a, 0.0)
    tf_ref[...] = turn(tf, -32)[:, 0:16]
    four = jnp.concatenate([tf] * 4, axis=0)
    hour_gram = packed(
        lax.dot_general(tf, four, NT, precision=HIGHEST, preferred_element_type=F32), 32
    )
    rep = tf
    for s in (64, 32, 16):
        rep = rep + turn(rep, s)
    weighted = rep * factor_lanes(vf_ref[...])
    copy.wait()
    w1, w2, w3 = split_3(weighted)
    w123 = jnp.concatenate([w1, w2, w3], axis=0)
    for c in range(5):
        at = slice(c * 1152, (c + 1) * 1152)
        d1, d2, d3 = split_3(dbuf[:, :, at].reshape(LANES, 1152))
        p1 = jnp.dot(w123, d1, preferred_element_type=F32)
        p2 = jnp.dot(w123[0:64], d2, preferred_element_type=F32)
        p3 = jnp.dot(w1, d3, preferred_element_type=F32)
        terms[:, at] = p1[0:32] + (p1[32:64] + p2[0:32] + (p1[64:96] + p2[32:64] + p3))
    for y in range(PARTS):

        def store(t, value):
            for z in range(4):
                out_ref[y * 4 + z, :, t * LANES : (t + 1) * LANES] = value[8 * z : 8 * z + 8]

        held = None
        for i in range(ROWS):
            t, off = divmod(i * STRIDE, LANES)
            base = i * NLON
            spin = lax.rem(lane + LANES - off, LANES)
            if y == 0:
                moved = placed(terms, base, off + 7)
                moved = jnp.where(spin < 7, placed(terms, base + NLON - 7, off), moved)
            else:
                moved = placed(terms, base + y * WIDTH - 7, off)
            if y == PARTS - 1:
                moved = jnp.where(spin < 97, moved, placed(terms, base, off + 97))
            value = moved if off == 0 else jnp.where(lane < off, held, moved)
            held = value
            if off + STRIDE >= LANES:
                store(t, value)
                held = moved
    for k in range(16):
        out_ref[k, :, PIECE:] = hour_gram


def hour_mode(got, side, vg_lanes, vf, data):
    vmem = pl.BlockSpec(memory_space=pltpu.VMEM)
    return pl.pallas_call(
        hour_kernel,
        in_specs=[vmem, vmem, vmem, vmem, pl.BlockSpec(memory_space=pl.ANY)],
        out_specs=(vmem, vmem),
        out_shape=(
            jax.ShapeDtypeStruct((RANK, 16), F32),
            jax.ShapeDtypeStruct((16, 8, PIECE + LANES), F32),
        ),
        scratch_shapes=[
            pltpu.VMEM((8, 16, 5760), F32),
            pltpu.VMEM((RANK, 5760 + LANES), F32),
            pltpu.SemaphoreType.DMA,
        ],
        compiler_params=grant(62),
        cost_estimate=pl.CostEstimate(flops=5_000_000_000, bytes_accessed=8_000_000, transcendentals=0),
        name="hour_mode",
    )(got, side, vg_lanes, vf, data)


def total_kernel(got_ref, piece_ref, gram_ref):
    for c in range(PIECE // LANES + 1):
        at = slice(c * LANES, (c + 1) * LANES)
        total = got_ref[0, :, at]
        for k in range(1, 16):
            total = total + got_ref[k, :, at]
        if c < PIECE // LANES:
            for k in range(4):
                piece_ref[k, :, at] = total
        else:
            gram_ref[...] = total


def totals(got):
    vmem = pl.BlockSpec(memory_space=pltpu.VMEM)
    return pl.pallas_call(
        total_kernel,
        in_specs=[vmem],
        out_specs=(vmem, vmem),
        out_shape=(
            jax.ShapeDtypeStruct((4, 8, PIECE), F32),
            jax.ShapeDtypeStruct((8, LANES), F32),
        ),
        compiler_params=grant(8),
        name="totals",
    )(got)


def operator_kernel(gram_ref, vg_ref, weight_ref, inv_ref, scale_ref):
    lane = lane_iota(RANK)
    row = row_iota(RANK)
    on_diag = lane == row
    gram = unpacked(gram_ref[...], 32, 0)
    diag = jnp.where(on_diag, gram, 0.0)
    scale_col = jnp.sqrt(jnp.sum(diag, axis=1, keepdims=True) + 1e-06)
    scale_row = jnp.sqrt(jnp.sum(diag, axis=0, keepdims=True) + 1e-06)
    op = gram / (scale_col * scale_row) * vg_ref[...] + 2.0 * jnp.where(on_diag, 1.0, 0.0)
    a = eliminated(op + jnp.where(lane == row + 32, 1.0, 0.0))
    inv = jnp.where((lane >= 32) & (lane < 64), a, 0.0)
    half = 0.5 * inv
    high = half.astype(jnp.bfloat16).astype(F32)
    low = half - high
    weight = turn(high, -32) + high + turn(low, 32) + turn(low, 64)
    weight_ref[...] = weight.astype(jnp.bfloat16)
    inv_ref[...] = turn(inv, -32)
    scale_ref[...] = jnp.broadcast_to(scale_col, (RANK, LANES))


def operator(gram, vg_lanes):
    vmem = pl.BlockSpec(memory_space=pltpu.VMEM)
    return pl.pallas_call(
        operator_kernel,
        in_specs=[vmem, vmem],
        out_specs=(vmem, vmem, vmem),
        out_shape=(
            jax.ShapeDtypeStruct((RANK, LANES), jnp.bfloat16),
            jax.ShapeDtypeStruct((RANK, LANES), F32),
            jax.ShapeDtypeStruct((RANK, LANES), F32),
        ),
        name="operator",
        compiler_params=grant(4),
        cost_estimate=pl.CostEstimate(flops=4_000_000_000, bytes_accessed=100_000, transcendentals=0),
    )(gram, vg_lanes)


EXT = ROWS + 16
EDGE = 6 * LANES


def sweep_kernel(
    even_ref, rhs_ref, near_ref, far_ref, start_ref, weight_ref, inv_ref, scale_ref, out_ref, state, base, x4, codes
):
    even = even_ref[0] == 1
    scale = scale_ref[...]
    inv = inv_ref[:, 0:RANK]
    for i in range(1, EXT - 1):
        at = slice(i * LANES, (i + 1) * LANES)
        if i < 8:
            first = (i + 8) * STRIDE - (PIECE - EDGE) - 1
            v = jnp.where(even, window(far_ref, first), window(near_ref, first))
        elif i < 8 + ROWS:
            v = window(rhs_ref, (i - 8) * STRIDE - 1)
        else:
            first = (i - 24) * STRIDE - 1
            v = jnp.where(even, window(near_ref, first), window(far_ref, first))
        state[:, at] = v / scale
    for c in range(EXT // 2):
        at = slice(max(1, 2 * c) * LANES, min(EXT - 1, 2 * c + 2) * LANES)
        base[:, at] = jnp.dot(inv, state[:, at], precision=HIGHEST, preferred_element_type=F32)
    for i in range(EXT):
        at = slice(i * LANES, (i + 1) * LANES)
        state[:, at] = start_ref[0:RANK, at]
        codes[0:8, at] = jnp.broadcast_to(start_ref[RANK : RANK + 1, at], (8, LANES))
        codes[8:16, at] = jnp.broadcast_to(start_ref[RANK + 1 : RANK + 2, at], (8, LANES))
    weight = weight_ref[...]

    def line(i):
        at = slice(i * LANES, (i + 1) * LANES)
        tiles = [state[8 * g : 8 * g + 8, at] for g in range(4)]
        return [(turn(c, -1), c, turn(c, 1)) for c in tiles]

    def sweep(_, carry):
        before, here = line(0), line(1)
        for i in range(1, EXT - 1):
            at = slice(i * LANES, (i + 1) * LANES)
            after = line(i + 1)
            picks = [[codes[8 * d : 8 * d + 8, at] == k for k in (1.0, 2.0, 3.0)] for d in range(2)]

            def pick(d, triple):
                ahead, same, behind = triple
                same_at, ahead_at, behind_at = picks[d]
                rest = jnp.where(same_at, same, 0.0)
                return jnp.where(ahead_at, ahead, jnp.where(behind_at, behind, rest))

            near = jnp.concatenate(
                [
                    (here[g][0] + here[g][2]) + (pick(0, before[g]) + pick(1, after[g]))
                    for g in range(4)
                ],
                axis=0,
            )
            high = near.astype(jnp.bfloat16)
            low = (near - high.astype(F32)).astype(jnp.bfloat16)
            x4[0:32, at] = high
            x4[32:64, at] = low
            x4[64:96, at] = high
            x4[96:128, at] = low
            before, here = here, after
        for c in range(EXT // 2):
            first, last = max(1, 2 * c), min(EXT - 1, 2 * c + 2)
            at = slice(first * LANES, last * LANES)
            state[:, at] = base[:, at] + jnp.dot(weight, x4[:, at], preferred_element_type=F32)
        return carry

    lax.fori_loop(0, SWEEPS, sweep, 0)

    def store(t, value):
        for k in range(PARTS):
            out_ref[k, :, t * LANES : (t + 1) * LANES] = value

    pack_pieces(
        [turn(state[:, (8 + i) * LANES : (9 + i) * LANES], -8) for i in range(ROWS)], WIDTH, store
    )


def sweeps(even, rhs, near, far, start, weight, inv, scale):
    vmem = pl.BlockSpec(memory_space=pltpu.VMEM)
    return pl.pallas_call(
        sweep_kernel,
        in_specs=[pl.BlockSpec(memory_space=pltpu.SMEM)] + [vmem] * 7,
        out_specs=vmem,
        out_shape=jax.ShapeDtypeStruct((PARTS, RANK, 12 * LANES), F32),
        scratch_shapes=[
            pltpu.VMEM((RANK, EXT * LANES), F32),
            pltpu.VMEM((RANK, EXT * LANES), F32),
            pltpu.VMEM((4 * RANK, EXT * LANES), jnp.bfloat16),
            pltpu.VMEM((16, EXT * LANES), F32),
        ],
        compiler_params=grant(12),
        name="sweeps",
    )(even, rhs, near, far, start, weight, inv, scale)


def join_kernel(got_ref, out_ref):
    lane = lane_iota(RANK)

    def row(i, held):
        for y in range(PARTS):
            to_tile, off = spot(i * NLON + y * WIDTH)
            first, at = spot(i * WIDTH)
            joint = jnp.where(lane >= at, got_ref[y, :, tile(first)], got_ref[y, :, tile(first + 1)])
            moved = pltpu.roll(joint, lax.rem(off + LANES - at, LANES), axis=1)
            value = jnp.where(lane < off, held, moved)
            out_ref[:, tile(to_tile)] = value
            held = jnp.where(off + WIDTH >= LANES, moved, value)
        return held

    lax.fori_loop(0, ROWS, row, jnp.zeros((RANK, LANES), F32))


def join(got):
    vmem = pl.BlockSpec(memory_space=pltpu.VMEM)
    return pl.pallas_call(
        join_kernel,
        in_specs=[vmem],
        out_specs=vmem,
        out_shape=jax.ShapeDtypeStruct((RANK, ROWS * NLON), F32),
        compiler_params=grant(8),
        name="join",
    )(got)


def link_codes(links):
    column = jnp.arange(links.shape[1], dtype=jnp.int32) % NLON
    target = (links % NLON - column + NLON) % NLON
    code = jnp.where(target == 1, 2.0, jnp.where(target == NLON - 1, 3.0, 1.0))
    return jnp.where(links >= 0, code, 0.0).astype(F32)


def swapped(edge_near, edge_far):
    far = lax.ppermute(edge_far, "lat", SWAP_FAR)
    near = lax.ppermute(edge_near, "lat", SWAP_NEAR)
    return near, far


def edges(block, width, even):
    top, bottom = block[:, :width], block[:, block.shape[1] - width :]
    return swapped(jnp.where(even, bottom, top), jnp.where(even, top, bottom))


def per_device(data, space_init, time_init, variable_factor, neighbours):
    tm = lax.axis_index("tm")
    lat = lax.axis_index("lat")
    even = lat % 2 == 0
    part = tm // 4

    hours = time_init.T
    low = lax.ppermute(hours[-2:], "tm", [(i, (i + 1) % 16) for i in range(16)])
    high = lax.ppermute(hours[:2], "tm", [((i + 1) % 16, i) for i in range(16)])
    sums = project(data, space_init, variable_factor)
    got = lax.all_to_all(sums, "lat", 0, 0, tiled=True)

    var_gram = jnp.dot(variable_factor.T, variable_factor, precision=HIGHEST, preferred_element_type=F32)
    vg_lanes = jnp.pad(var_gram, ((0, 0), (0, LANES - RANK)))
    low = jnp.where(tm == 0, 0.0, low)
    high = jnp.where(tm == 15, 0.0, high)
    padded = jnp.concatenate([low, hours, high], axis=0)
    stencil = padded[:-4] - 4.0 * padded[1:-3] - 4.0 * padded[3:-1] + padded[4:]
    side = jnp.pad((-0.5 * stencil).T, ((0, 0), (32, 80)))

    own = jnp.concatenate([space_init, link_codes(neighbours[2:4])], axis=0)
    own, _ = lax.optimization_barrier((own, sums[0, 0, 0]))
    own = own.reshape(RANK + 2, ROWS, NLON)
    own = jnp.concatenate([own[:, :, NLON - 8 :], own, own[:, :, :30]], axis=2)
    own = lax.dynamic_slice_in_dim(own, part * WIDTH, LANES, axis=2)
    own = own.reshape(RANK + 2, ROWS * LANES)
    start_near, start_far = edges(own, 8 * LANES, even)
    start = jnp.concatenate(
        [
            jnp.where(even, start_far, start_near),
            own,
            jnp.where(even, start_near, start_far),
        ],
        axis=1,
    )

    time_factor, terms = hour_mode(got, side, vg_lanes, variable_factor, data)
    got = lax.all_to_all(terms, "tm", 0, 0, tiled=True)
    pieces, gram = totals(got)
    rhs = lax.all_to_all(pieces, "tm", 0, 0, tiled=True, axis_index_groups=Z_GROUPS)
    weight, inv, scale = operator(gram, vg_lanes)
    rhs = rhs.reshape(RANK, PIECE)
    near, far = edges(rhs, EDGE, even)
    even_flag = jnp.where(even, 1, 0).astype(jnp.int32).reshape(1)
    blocks = sweeps(even_flag, rhs, near, far, start, weight, inv, scale)
    blocks = lax.all_to_all(blocks, "tm", 0, 0, tiled=True, axis_index_groups=Y_GROUPS)
    return (time_factor, join(blocks))


def solution(mesh):
    placed_at = (P(None, "tm", "lat"), P(None, "lat"), P(None, "tm"), P(), P(None, "lat"))
    return jax.shard_map(
        per_device,
        mesh=mesh,
        in_specs=placed_at,
        out_specs=(P(None, "tm"), P(None, "lat")),
        check_vma=False,
    )
```

time: 140 us -> 122 us (0.87)
  Pallas kernels: 34.5 us -> 24.6 us
  waiting for transfers between devices: 56.4 us -> 50.3 us
  local copies, waits for them, and re-layouts: 7.7 us -> 3.78 us
  starting transfers between devices: 37.8 us -> 40.6 us
    all_to_all x1, waiting for transfers between devices: 23.2 us -> 7.55 us  [per_device(): got = lax.all_to_all(terms, 'tm', 0, 0, tiled=True)]
    all_to_all x1, waiting for transfers between devices: 0.01 us -> 5.87 us  [per_device(): lax.all_to_all(pieces, 'tm', 0, 0, tiled=True, axis_index_groups=Z_GROUPS)]
    ppermute x6, waiting for transfers between devices: 18.3 us -> 22.7 us  [the longest x2 17.6 us: swapped(): far = lax.ppermute(edge_far, 'lat', SWAP_FAR)]
    pallas_call x1, Pallas kernels: 6.04 us -> 2.33 us  [join(): pl.pallas_call(join_kernel, in_specs=[vmem], out_specs=vmem, out_shape=ja...]
    ppermute x6, starting transfers between devices: 9.69 us -> 12.8 us  [the longest x2 10.7 us: swapped(): far = lax.ppermute(edge_far, 'lat', SWAP_FAR)]
    unnamed x26 -> x18, local copies, waits for them, and re-layouts: 4.11 us -> 1.56 us
    pallas_call x1, Pallas kernels: 8.46 us -> 6.1 us  [project(): pl.pallas_call(project_kernel, grid=(5760 // chunk,), in_specs=[pl.BlockS...]
  transfers between devices with their start and end apart: 10 -> 10, of which waited for: 7 -> 8; matrix products, arithmetic and copies ran while one was open for 4% -> 3% of each run, Pallas kernels for 3% -> 2%
where the time goes in v2:
time: 122 us; the launch traced here: 121 us
  waiting for transfers between devices  50.3 us (41%)
  starting transfers between devices  40.6 us (33%)
  Pallas kernels  24.6 us (20%)
  local copies, waits for them, and re-layouts  3.78 us (3%)
    ppermute x2, waiting for transfers between devices, swapped(): far = lax.ppermute(edge_far, 'lat', SWAP_FAR)  17.6 us
    all_to_all x1, waiting for transfers between devices, per_device(): lax.all_to_all(blocks, 'tm', 0, 0, tiled=True, axis_index_groups=Y_GROUPS)  10.9 us
    ppermute x2, starting transfers between devices, swapped(): far = lax.ppermute(edge_far, 'lat', SWAP_FAR)  10.7 us
    all_to_all x1, starting transfers between devices, per_device(): got = lax.all_to_all(sums, 'lat', 0, 0, tiled=True)  10.1 us
    all_to_all x1, waiting for transfers between devices, per_device(): got = lax.all_to_all(terms, 'tm', 0, 0, tiled=True)  7.55 us
    all_to_all x1, starting transfers between devices, per_device(): lax.all_to_all(pieces, 'tm', 0, 0, tiled=True, axis_index_groups=Z_GROUPS)  7.34 us
    all_to_all x1, starting transfers between devices, per_device(): got = lax.all_to_all(terms, 'tm', 0, 0, tiled=True)  6.7 us
    pallas_call x1, Pallas kernels, sweeps(): pl.pallas_call(sweep_kernel, in_specs=[pl.BlockSpec(memory_space=pltpu.SM...  6.56 us
  transfers between devices with their start and end apart: 10, of which 8 were waited for; matrix products, arithmetic and copies ran while one was open for 3% of the time, Pallas kernels for 2%

profile of v2, /device:TPU:32, one launch (start us, length us, event | category | flops | bytes accessed | tf_op | source)
XLA Modules:
  0.0 121.2 jit_solution(8981663626926698257)
XLA Ops:
  0.7 6.1 %project.1 = f32[16,8,256]{2,1,0:T(8,128)} custom-call(f32[8,16,5760]{2,1,0:T(8,128)} %data_ref.3, f32[32,5760]{1,0:T(8,128)} %space_ref.1, f32[8,32]{1,0:T(8,128)} %vf_ref.3), custom_call_target="tpu_custom_call" | custom-call | flops 4000000000 | bytes 8000000 | tf_op jit(solution)/shard_map/project/pallas_call | solution.py:116
  6.8 10.1 %all-to-all-start = ((f32[16,8,256]{2,1,0:T(8,128)}), f32[16,8,256]{2,1,0:T(8,128)S(1)}, u32[]{:S(2)}, u32[]{:S(2)}) async-start(f32[16,8,256]{2,1,0:T(8,128)} %project.1), calls=%async_computation | async-start | bytes 262144 | tf_op jit(solution)/shard_map/all_to_all | solution.py:479
  17.1 1.0 collective-permute-start.1
  18.1 1.0 collective-permute-start
  19.1 0.2 fusion.15
  19.3 0.6 pad.9.vg_ref
  19.9 1.6 %collective-permute-done.1 = f32[2,32]{0,1:T(8,128)S(1)} collective-permute-done((f32[2,32]{0,1:T(8,128)S(1)}, f32[2,32]{0,1:T(8,128)S(1)}, u32[]{:S(2)}, u32[]{:S(2)}) %collective-permute-start.1) | collective-permute-done | bytes 288 | tf_op jit(solution)/shard_map/ppermute | solution.py:477
  21.6 3.5 %collective-permute-done = f32[2,32]{0,1:T(8,128)S(1)} collective-permute-done((f32[2,32]{0,1:T(8,128)S(1)}, f32[2,32]{0,1:T(8,128)S(1)}, u32[]{:S(2)}, u32[]{:S(2)}) %collective-permute-start) | collective-permute-done | bytes 288 | tf_op jit(solution)/shard_map/ppermute | solution.py:476
  25.2 0.7 pad.8.side_ref
  25.9 3.1 %all-to-all-done.got_ref = f32[16,8,256]{2,1,0:T(8,128)S(1)} async-done(((f32[16,8,256]{2,1,0:T(8,128)}), f32[16,8,256]{2,1,0:T(8,128)S(1)}, u32[]{:S(2)}, u32[]{:S(2)}) %all-to-all-start) | async-done | bytes 131104 | tf_op jit(solution)/shard_map/all_to_all | solution.py:479
  29.0 0.7 copy-done.2
  29.7 6.0 %hour_mode.1 = (f32[32,16]{1,0:T(8,128)}, f32[16,8,1792]{2,1,0:T(8,128)}) custom-call(f32[16,8,256]{2,1,0:T(8,128)} %copy-done.2, f32[32,128]{1,0:T(8,128)} %pad.8.side_ref, f32[32,128]{1,0:T(8,128)} %pad.9.vg_ref, f32[8,32]{1,0:T(8,128)} %vf_ref.3, f32[8,16,5760]{2,1,0:T(8,128)} %data_ref.3), custom_call_target="tpu_custom_call" | custom-call | flops 5000000000 | bytes 8000000 | tf_op jit(solution)/shard_map/hour_mode/pallas_call | solution.py:240
  35.7 6.7 %all-to-all-start.1 = ((f32[16,8,1792]{2,1,0:T(8,128)}), f32[16,8,1792]{2,1,0:T(8,128)S(1)}, u32[]{:S(2)}, u32[]{:S(2)}) async-start(f32[16,8,1792]{2,1,0:T(8,128)} %get-tuple-element.10), calls=%async_computation.1 | async-start | bytes 1835008 | tf_op jit(solution)/shard_map/all_to_all | solution.py:506
  42.5 0.3 compare_select_fusion.2
  42.8 0.7 reshape.27
  43.6 0.1 slice.65
  43.8 0.3 fusion.1
  44.1 0.1 copy.9
  44.2 4.8 %collective-permute-start.4 = (f32[34,1024]{1,0:T(8,128)S(1)}, f32[34,1024]{1,0:T(8,128)S(1)}, u32[]{:S(2)}, u32[]{:S(2)}) collective-permute-start(f32[34,1024]{1,0:T(8,128)S(1)} %get-tuple-element.20), channel_id=1, source_target_pairs={{0,240},{16,32},{32,16},{48,64},{64,48},{80,96},{96,80},{112,128},... | collective-permute-start | bytes 417800 | tf_op jit(solution)/shard_map/ppermute | solution.py:459
  49.0 14.1 %collective-permute-done.4 = f32[34,1024]{1,0:T(8,128)S(1)} collective-permute-done((f32[34,1024]{1,0:T(8,128)S(1)}, f32[34,1024]{1,0:T(8,128)S(1)}, u32[]{:S(2)}, u32[]{:S(2)}) %collective-permute-start.4) | collective-permute-done | bytes 139296 | tf_op jit(solution)/shard_map/ppermute | solution.py:459
  63.1 7.6 %all-to-all-done.1.got_ref = f32[16,8,1792]{2,1,0:T(8,128)S(1)} async-done(((f32[16,8,1792]{2,1,0:T(8,128)}), f32[16,8,1792]{2,1,0:T(8,128)S(1)}, u32[]{:S(2)}, u32[]{:S(2)}) %all-to-all-start.1) | async-done | bytes 917536 | tf_op jit(solution)/shard_map/all_to_all | solution.py:506
  70.7 0.7 totals.1
  71.4 7.3 %all-to-all-start.2 = ((f32[4,8,1664]{2,1,0:T(8,128)}), f32[4,8,1664]{2,1,0:T(8,128)S(1)}, u32[]{:S(2)}, u32[]{:S(2)}) async-start(f32[4,8,1664]{2,1,0:T(8,128)} %get-tuple-element.11), calls=%async_computation.2 | async-start | bytes 425984 | tf_op jit(solution)/shard_map/all_to_all | solution.py:508
  78.8 5.9 %all-to-all-done.2 = f32[4,8,1664]{2,1,0:T(8,128)S(1)} async-done(((f32[4,8,1664]{2,1,0:T(8,128)}), f32[4,8,1664]{2,1,0:T(8,128)S(1)}, u32[]{:S(2)}, u32[]{:S(2)}) %all-to-all-start.2) | async-done | bytes 213024 | tf_op jit(solution)/shard_map/all_to_all | solution.py:508
  84.8 5.9 %collective-permute-start.3 = (f32[32,768]{1,0:T(8,128)S(1)}, f32[32,768]{1,0:T(8,128)S(1)}, u32[]{:S(2)}, u32[]{:S(2)}) collective-permute-start(f32[32,768]{1,0:T(8,128)S(1)} %get-tuple-element.22), channel_id=1, source_target_pairs={{0,240},{16,32},{32,16},{48,64},{64,48},{80,96},{96,80},{112,128},... | collective-permute-start | bytes 294920 | tf_op jit(solution)/shard_map/ppermute | solution.py:459
  90.7 2.9 %operator.1 = (bf16[32,128]{1,0:T(8,128)(2,1)S(1)}, f32[32,128]{1,0:T(8,128)S(1)}, f32[32,128]{1,0:T(8,128)S(1)}) custom-call(f32[8,128]{1,0:T(8,128)S(1)} %get-tuple-element.12.gram_ref, f32[32,128]{1,0:T(8,128)S(1)} %copy-done), custom_call_target="tpu_custom_call" | custom-call | flops 4000000000 | bytes 100000 | tf_op jit(solution)/shard_map/operator/pallas_call | solution.py:309
  93.6 3.5 %collective-permute-done.3.far_ref = f32[32,768]{1,0:T(8,128)S(1)} collective-permute-done((f32[32,768]{1,0:T(8,128)S(1)}, f32[32,768]{1,0:T(8,128)S(1)}, u32[]{:S(2)}, u32[]{:S(2)}) %collective-permute-start.3) | collective-permute-done | bytes 98336 | tf_op jit(solution)/shard_map/ppermute | solution.py:459
  97.1 6.6 %sweeps.1 = f32[4,32,1536]{2,1,0:T(8,128)} custom-call(s32[1]{0:T(128)} %bitcast.2.even_ref, f32[32,1664]{1,0:T(8,128)S(1)} %bitcast.11, f32[32,768]{1,0:T(8,128)S(1)} %collective-permute-done.2.near_ref, f32[32,768]{1,0:T(8,128)S(1)} %collective-permute-done.3.far_ref, f32[34,4096]{1,0:T(8,128)S(1)} %pad_maximum_fusion.1.start_ref, ...), custom_call_target="tpu_custom_call" | custom-call | tf_op jit(solution)/shard_map/sweeps/pallas_call | solution.py:406
  103.7 3.6 %all-to-all-start.3 = ((f32[4,32,1536]{2,1,0:T(8,128)}), f32[4,32,1536]{2,1,0:T(8,128)S(1)}, u32[]{:S(2)}, u32[]{:S(2)}) async-start(f32[4,32,1536]{2,1,0:T(8,128)} %sweeps.1), calls=%async_computation.3 | async-start | bytes 1572864 | tf_op jit(solution)/shard_map/all_to_all | solution.py:514
  107.3 0.7 copy.8
  108.0 10.9 %all-to-all-done.3.got_ref = f32[4,32,1536]{2,1,0:T(8,128)S(1)} async-done(((f32[4,32,1536]{2,1,0:T(8,128)}), f32[4,32,1536]{2,1,0:T(8,128)S(1)}, u32[]{:S(2)}, u32[]{:S(2)}) %all-to-all-start.3) | async-done | bytes 786464 | tf_op jit(solution)/shard_map/all_to_all | solution.py:514
  118.9 2.3 %join.1 = f32[32,5760]{1,0:T(8,128)} custom-call(f32[4,32,1536]{2,1,0:T(8,128)S(1)} %all-to-all-done.3.got_ref), custom_call_target="tpu_custom_call" | custom-call | tf_op jit(solution)/shard_map/join/pallas_call | solution.py:441
  (30 shorter events, 0.6 us)
Async XLA Ops:
  0.6 18.5 %copy-start.4 = (f32[8,32]{1,0:T(8,128)S(1)}, f32[8,32]{1,0:T(8,128)}, u32[]{:S(2)}) copy-start(f32[8,32]{1,0:T(8,128)} %vf_ref.3) | copy-start | bytes 3076
  0.6 16.3 %copy-start.6 = (f32[32,16]{0,1:T(8,128)S(1)}, f32[32,16]{0,1:T(8,128)}, u32[]{:S(2)}) copy-start(f32[32,16]{0,1:T(8,128)} %param.7) | copy-start | bytes 6148
  6.8 22.3 %all-to-all-start = ((f32[16,8,256]{2,1,0:T(8,128)}), f32[16,8,256]{2,1,0:T(8,128)S(1)}, u32[]{:S(2)}, u32[]{:S(2)}) async-start(f32[16,8,256]{2,1,0:T(8,128)} %project.1), calls=%async_computation | async-start | bytes 262144 | tf_op jit(solution)/shard_map/all_to_all | solution.py:479
  17.1 4.5 %collective-permute-start.1 = (f32[2,32]{0,1:T(8,128)S(1)}, f32[2,32]{0,1:T(8,128)S(1)}, u32[]{:S(2)}, u32[]{:S(2)}) collective-permute-start(f32[2,32]{0,1:T(8,128)S(1)} %get-tuple-element.25), channel_id=1, source_target_pairs={{1,0},{2,1},{3,2},{4,3},{5,4},{6,5},{7,6},{8,7},{9,8},{10,9},{11,1... | collective-permute-start | bytes 776 | tf_op jit(solution)/shard_map/ppermute | solution.py:477
  18.1 7.0 %collective-permute-start = (f32[2,32]{0,1:T(8,128)S(1)}, f32[2,32]{0,1:T(8,128)S(1)}, u32[]{:S(2)}, u32[]{:S(2)}) collective-permute-start(f32[2,32]{0,1:T(8,128)S(1)} %get-tuple-element.24), channel_id=1, source_target_pairs={{0,1},{1,2},{2,3},{3,4},{4,5},{5,6},{6,7},{7,8},{8,9},{9,10},{10,1... | collective-permute-start | bytes 776 | tf_op jit(solution)/shard_map/ppermute | solution.py:476
  29.0 0.7 copy-start.2
  35.7 6.7 %copy-start.3 = (s32[4,5760]{1,0:T(4,128)S(1)}, s32[4,5760]{1,0:T(4,128)}, u32[]{:S(2)}) copy-start(s32[4,5760]{1,0:T(4,128)} %param.9) | copy-start | bytes 276484
  35.7 7.0 %copy-start.1 = (f32[32,5760]{1,0:T(8,128)S(1)}, f32[32,5760]{1,0:T(8,128)}, u32[]{:S(2)}) copy-start(f32[32,5760]{1,0:T(8,128)} %space_ref.1) | copy-start | bytes 2211844
  35.7 34.9 %all-to-all-start.1 = ((f32[16,8,1792]{2,1,0:T(8,128)}), f32[16,8,1792]{2,1,0:T(8,128)S(1)}, u32[]{:S(2)}, u32[]{:S(2)}) async-start(f32[16,8,1792]{2,1,0:T(8,128)} %get-tuple-element.10), calls=%async_computation.1 | async-start | bytes 1835008 | tf_op jit(solution)/shard_map/all_to_all | solution.py:506
  44.2 18.8 %collective-permute-start.4 = (f32[34,1024]{1,0:T(8,128)S(1)}, f32[34,1024]{1,0:T(8,128)S(1)}, u32[]{:S(2)}, u32[]{:S(2)}) collective-permute-start(f32[34,1024]{1,0:T(8,128)S(1)} %get-tuple-element.20), channel_id=1, source_target_pairs={{0,240},{16,32},{32,16},{48,64},{64,48},{80,96},{96,80},{112,128},... | collective-permute-start | bytes 417800 | tf_op jit(solution)/shard_map/ppermute | solution.py:459
  49.0 14.1 %collective-permute-start.5 = (f32[34,1024]{1,0:T(8,128)S(1)}, f32[34,1024]{1,0:T(8,128)S(1)}, u32[]{:S(2)}, u32[]{:S(2)}) collective-permute-start(f32[34,1024]{1,0:T(8,128)S(1)} %get-tuple-element.21), channel_id=1, source_target_pairs={{0,16},{16,0},{32,48},{48,32},{64,80},{80,64},{96,112},{112,96},{1... | collective-permute-start | bytes 417800 | tf_op jit(solution)/shard_map/ppermute | solution.py:460
  71.4 19.3 %copy-start = (f32[32,128]{1,0:T(8,128)S(1)}, f32[32,128]{1,0:T(8,128)}, u32[]{:S(2)}) copy-start(f32[32,128]{1,0:T(8,128)} %pad.9.vg_ref) | copy-start | bytes 49156
  71.4 13.3 %all-to-all-start.2 = ((f32[4,8,1664]{2,1,0:T(8,128)}), f32[4,8,1664]{2,1,0:T(8,128)S(1)}, u32[]{:S(2)}, u32[]{:S(2)}) async-start(f32[4,8,1664]{2,1,0:T(8,128)} %get-tuple-element.11), calls=%async_computation.2 | async-start | bytes 425984 | tf_op jit(solution)/shard_map/all_to_all | solution.py:508
  84.7 8.9 %collective-permute-start.2 = (f32[32,768]{1,0:T(8,128)S(1)}, f32[32,768]{1,0:T(8,128)S(1)}, u32[]{:S(2)}, u32[]{:S(2)}) collective-permute-start(f32[32,768]{1,0:T(8,128)S(1)} %get-tuple-element.23), channel_id=1, source_target_pairs={{0,16},{16,0},{32,48},{48,32},{64,80},{80,64},{96,112},{112,96},{1... | collective-permute-start | bytes 294920 | tf_op jit(solution)/shard_map/ppermute | solution.py:460
  84.8 12.3 %collective-permute-start.3 = (f32[32,768]{1,0:T(8,128)S(1)}, f32[32,768]{1,0:T(8,128)S(1)}, u32[]{:S(2)}, u32[]{:S(2)}) collective-permute-start(f32[32,768]{1,0:T(8,128)S(1)} %get-tuple-element.22), channel_id=1, source_target_pairs={{0,240},{16,32},{32,16},{48,64},{64,48},{80,96},{96,80},{112,128},... | collective-permute-start | bytes 294920 | tf_op jit(solution)/shard_map/ppermute | solution.py:459
  103.7 3.6 %copy-start.5 = (f32[32,16]{1,0:T(8,128)S(1)}, f32[32,16]{1,0:T(8,128)}, u32[]{:S(2)}) copy-start(f32[32,16]{1,0:T(8,128)} %get-tuple-element.16) | copy-start | bytes 6148
  103.7 15.3 %all-to-all-start.3 = ((f32[4,32,1536]{2,1,0:T(8,128)}), f32[4,32,1536]{2,1,0:T(8,128)S(1)}, u32[]{:S(2)}, u32[]{:S(2)}) async-start(f32[4,32,1536]{2,1,0:T(8,128)} %sweeps.1), calls=%async_computation.3 | async-start | bytes 1572864 | tf_op jit(solution)/shard_map/all_to_all | solution.py:514

commit v3 on v2

--- a/solution.py
+++ b/solution.py
@@ -78,6 +78,15 @@
     return jnp.dot(turned, chosen, precision=HIGHEST, preferred_element_type=F32)
 
 
+TN = (((0,), (0,)), ((), ()))
+
+
+def gram_lanes(vf):
+    chosen = jnp.where(lane_iota(RANK) == row_iota(RANK), 1.0, 0.0)
+    wide = jnp.dot(vf, chosen, precision=HIGHEST, preferred_element_type=F32)
+    return lax.dot_general(vf, wide, TN, precision=HIGHEST, preferred_element_type=F32)
+
+
 def project_kernel(data_ref, space_ref, vf_ref, out_ref, acc_ref):
     step = pl.program_id(0)
 
@@ -92,18 +101,22 @@
     x1 = jnp.concatenate([d1, s1], axis=0)
     x2 = jnp.concatenate([d2, s2], axis=0)
     x3 = jnp.concatenate([d3, s3], axis=0)
-    p1 = lax.dot_general(jnp.concatenate([s1, s2, s3], axis=0), x1, NT, preferred_element_type=F32)
-    p2 = lax.dot_general(jnp.concatenate([s1, s2], axis=0), x2, NT, preferred_element_type=F32)
-    p3 = lax.dot_general(s1, x3, NT, preferred_element_type=F32)
-    small = p1[64:96] + p2[32:64] + p3
-    acc_ref[...] += p1[0:32] + (p1[32:64] + p2[0:32] + small)
+    side = jnp.concatenate([s1, s2, s3, s1], axis=0)
+    first, mid, last = acc_ref.at[0], acc_ref.at[1], acc_ref.at[2]
+    first[...] += lax.dot_general(x1, side, NT, preferred_element_type=F32)
+    mid[...] += lax.dot_general(x2, side, NT, preferred_element_type=F32)
+    last[...] += lax.dot_general(x3, side, NT, preferred_element_type=F32)
 
     @pl.when(step == pl.num_programs(0) - 1)
     def _():
-        rhs = acc_ref[:, 0:LANES] * factor_lanes(vf_ref[...])
+        p1, p2, p3 = acc_ref[0], acc_ref[1], acc_ref[2]
+        total = p1 + (turn(p1, -32) + p2 + (turn(p1, -64) + turn(p2, -32) + p3))
+        rhs = jnp.transpose(total[0:LANES])[0:RANK] * factor_lanes(vf_ref[...])
         for s in (64, 32, 16):
             rhs = rhs + turn(rhs, s)
-        gram = jnp.concatenate([acc_ref[:, LANES:]] * 4, axis=1)
+        gram = jnp.where(lane_iota(RANK) < RANK, total[LANES:], 0.0)
+        gram = gram + turn(gram, 32)
+        gram = gram + turn(gram, 64)
         g = packed(gram, 32)
         r = packed(rhs, 16)
         for k in range(16):
@@ -112,7 +125,7 @@
 
 
 def project(data, space, vf):
-    chunk = 1152
+    chunk = 5760
     return pl.pallas_call(
         project_kernel,
         grid=(5760 // chunk,),
@@ -123,14 +136,14 @@
         ],
         out_specs=pl.BlockSpec((16, 8, 256), lambda i: (0, 0, 0)),
         out_shape=jax.ShapeDtypeStruct((16, 8, 256), F32),
-        scratch_shapes=[pltpu.VMEM((RANK, LANES + RANK), F32)],
+        scratch_shapes=[pltpu.VMEM((3, LANES + RANK, LANES), F32)],
         cost_estimate=pl.CostEstimate(flops=4_000_000_000, bytes_accessed=8_000_000, transcendentals=0),
         name="project",
     )(data, space, vf)
 
 
 def grant(mebibytes):
-    return pltpu.CompilerParams(vmem_limit_bytes=mebibytes * 1024 * 1024)
+    return pltpu.CompilerParams(vmem_limit_bytes=int(mebibytes * 1024 * 1024))
 
 
 def pack_pieces(pieces, width, store):
@@ -176,7 +189,7 @@
     return pl.ds(pl.multiple_of(t * LANES, LANES), LANES)
 
 
-def hour_kernel(got_ref, side_ref, vg_ref, vf_ref, data_ref, tf_ref, out_ref, dbuf, terms, sem):
+def hour_kernel(got_ref, stencil_ref, vf_ref, data_ref, tf_ref, out_ref, dbuf, terms, sem):
     copy = pltpu.make_async_copy(data_ref, dbuf, sem)
     copy.start()
     total = got_ref[0]
@@ -186,7 +199,12 @@
     eye = jnp.where(lane == row_iota(RANK), 1.0, 0.0)
     gram = unpacked(total[:, 0:128], 32, 0)
     rhs = unpacked(total[:, 128:256], 16, 32)
-    a = gram * vg_ref[...] + 3.0 * eye + rhs + side_ref[...]
+    vf = vf_ref[...]
+    chosen = jnp.where(lane_iota(16) == row_iota(16) + 32, 1.0, 0.0)
+    stencil = lax.dot_general(
+        stencil_ref[...], chosen, TN, precision=HIGHEST, preferred_element_type=F32
+    )
+    a = gram * gram_lanes(vf) + 3.0 * eye + rhs - 0.5 * stencil
     a = eliminated(a)
     tf = jnp.where((lane >= 32) & (lane < 48), a, 0.0)
     tf_ref[...] = turn(tf, -32)[:, 0:16]
@@ -197,7 +215,7 @@
     rep = tf
     for s in (64, 32, 16):
         rep = rep + turn(rep, s)
-    weighted = rep * factor_lanes(vf_ref[...])
+    weighted = rep * factor_lanes(vf)
     copy.wait()
     w1, w2, w3 = split_3(weighted)
     w123 = jnp.concatenate([w1, w2, w3], axis=0)
@@ -211,8 +229,7 @@
     for y in range(PARTS):
 
         def store(t, value):
-            for z in range(4):
-                out_ref[y * 4 + z, :, t * LANES : (t + 1) * LANES] = value[8 * z : 8 * z + 8]
+            out_ref[y, :, t * LANES : (t + 1) * LANES] = value
 
         held = None
         for i in range(ROWS):
@@ -231,42 +248,63 @@
             if off + STRIDE >= LANES:
                 store(t, value)
                 held = moved
-    for k in range(16):
-        out_ref[k, :, PIECE:] = hour_gram
-
-
-def hour_mode(got, side, vg_lanes, vf, data):
+    for y in range(PARTS):
+        out_ref[y, :, PIECE:] = jnp.concatenate([hour_gram] * 4, axis=0)
+
+
+def hour_mode(got, stencil, vf, data):
     vmem = pl.BlockSpec(memory_space=pltpu.VMEM)
     return pl.pallas_call(
         hour_kernel,
-        in_specs=[vmem, vmem, vmem, vmem, pl.BlockSpec(memory_space=pl.ANY)],
+        in_specs=[vmem, vmem, vmem, pl.BlockSpec(memory_space=pl.ANY)],
         out_specs=(vmem, vmem),
         out_shape=(
             jax.ShapeDtypeStruct((RANK, 16), F32),
-            jax.ShapeDtypeStruct((16, 8, PIECE + LANES), F32),
+            jax.ShapeDtypeStruct((PARTS, RANK, PIECE + LANES), F32),
         ),
         scratch_shapes=[
             pltpu.VMEM((8, 16, 5760), F32),
             pltpu.VMEM((RANK, 5760 + LANES), F32),
             pltpu.SemaphoreType.DMA,
         ],
-        compiler_params=grant(62),
+        compiler_params=grant(61.5),
         cost_estimate=pl.CostEstimate(flops=5_000_000_000, bytes_accessed=8_000_000, transcendentals=0),
         name="hour_mode",
-    )(got, side, vg_lanes, vf, data)
+    )(got, stencil, vf, data)
 
 
 def total_kernel(got_ref, piece_ref, gram_ref):
     for c in range(PIECE // LANES + 1):
         at = slice(c * LANES, (c + 1) * LANES)
         total = got_ref[0, :, at]
-        for k in range(1, 16):
+        for k in range(1, 4):
             total = total + got_ref[k, :, at]
         if c < PIECE // LANES:
             for k in range(4):
                 piece_ref[k, :, at] = total
         else:
             gram_ref[...] = total
+
+
+def part_kernel(got_ref, out_ref):
+    for z in range(4):
+        for c in range(PIECE // LANES + 1):
+            at = slice(c * LANES, (c + 1) * LANES)
+            rows = slice(8 * z, 8 * z + 8)
+            a, b = got_ref[0, rows, at] + got_ref[1, rows, at], got_ref[2, rows, at] + got_ref[3, rows, at]
+            out_ref[z, :, at] = a + b
+
+
+def part_totals(got):
+    vmem = pl.BlockSpec(memory_space=pltpu.VMEM)
+    return pl.pallas_call(
+        part_kernel,
+        in_specs=[vmem],
+        out_specs=vmem,
+        out_shape=jax.ShapeDtypeStruct((4, 8, PIECE + LANES), F32),
+        compiler_params=grant(8),
+        name="part_totals",
+    )(got)
 
 
 def totals(got):
@@ -284,7 +322,7 @@
     )(got)
 
 
-def operator_kernel(gram_ref, vg_ref, weight_ref, inv_ref, scale_ref):
+def operator_kernel(gram_ref, vf_ref, weight_ref, inv_ref, scale_ref):
     lane = lane_iota(RANK)
     row = row_iota(RANK)
     on_diag = lane == row
@@ -292,7 +330,7 @@
     diag = jnp.where(on_diag, gram, 0.0)
     scale_col = jnp.sqrt(jnp.sum(diag, axis=1, keepdims=True) + 1e-06)
     scale_row = jnp.sqrt(jnp.sum(diag, axis=0, keepdims=True) + 1e-06)
-    op = gram / (scale_col * scale_row) * vg_ref[...] + 2.0 * jnp.where(on_diag, 1.0, 0.0)
+    op = gram / (scale_col * scale_row) * gram_lanes(vf_ref[...]) + 2.0 * jnp.where(on_diag, 1.0, 0.0)
     a = eliminated(op + jnp.where(lane == row + 32, 1.0, 0.0))
     inv = jnp.where((lane >= 32) & (lane < 64), a, 0.0)
     half = 0.5 * inv
@@ -300,11 +338,13 @@
     low = half - high
     weight = turn(high, -32) + high + turn(low, 32) + turn(low, 64)
     weight_ref[...] = weight.astype(jnp.bfloat16)
-    inv_ref[...] = turn(inv, -32)
+    i1, i2, i3 = (part.astype(F32) for part in split_3(inv))
+    inv_ref[:, 0:128] = (turn(i1, -32) + i1 + turn(i1, 32) + turn(i2, 64)).astype(jnp.bfloat16)
+    inv_ref[:, 128:256] = (turn(i2, -32) + i3).astype(jnp.bfloat16)
     scale_ref[...] = jnp.broadcast_to(scale_col, (RANK, LANES))
 
 
-def operator(gram, vg_lanes):
+def operator(gram, vf):
     vmem = pl.BlockSpec(memory_space=pltpu.VMEM)
     return pl.pallas_call(
         operator_kernel,
@@ -312,13 +352,13 @@
         out_specs=(vmem, vmem, vmem),
         out_shape=(
             jax.ShapeDtypeStruct((RANK, LANES), jnp.bfloat16),
-            jax.ShapeDtypeStruct((RANK, LANES), F32),
+            jax.ShapeDtypeStruct((RANK, 2 * LANES), jnp.bfloat16),
             jax.ShapeDtypeStruct((RANK, LANES), F32),
         ),
         name="operator",
         compiler_params=grant(4),
         cost_estimate=pl.CostEstimate(flops=4_000_000_000, bytes_accessed=100_000, transcendentals=0),
-    )(gram, vg_lanes)
+    )(gram, vf)
 
 
 EXT = ROWS + 16
@@ -326,11 +366,11 @@
 
 
 def sweep_kernel(
-    even_ref, rhs_ref, near_ref, far_ref, start_ref, weight_ref, inv_ref, scale_ref, out_ref, state, base, x4, codes
+    even_ref, rhs_ref, near_ref, far_ref, start_ref, weight_ref, inv_ref, scale_ref, out_ref, state, base, codes
 ):
     even = even_ref[0] == 1
     scale = scale_ref[...]
-    inv = inv_ref[:, 0:RANK]
+    inv = inv_ref[:, 0 : 6 * RANK]
     for i in range(1, EXT - 1):
         at = slice(i * LANES, (i + 1) * LANES)
         if i < 8:
@@ -344,7 +384,9 @@
         state[:, at] = v / scale
     for c in range(EXT // 2):
         at = slice(max(1, 2 * c) * LANES, min(EXT - 1, 2 * c + 2) * LANES)
-        base[:, at] = jnp.dot(inv, state[:, at], precision=HIGHEST, preferred_element_type=F32)
+        x1, x2, x3 = split_3(state[:, at])
+        x6 = jnp.concatenate([x1, x2, x3, x1, x2, x1], axis=0)
+        base[:, at] = jnp.dot(inv, x6, preferred_element_type=F32)
     for i in range(EXT):
         at = slice(i * LANES, (i + 1) * LANES)
         state[:, at] = start_ref[0:RANK, at]
@@ -377,17 +419,15 @@
                 ],
                 axis=0,
             )
-            high = near.astype(jnp.bfloat16)
-            low = (near - high.astype(F32)).astype(jnp.bfloat16)
-            x4[0:32, at] = high
-            x4[32:64, at] = low
-            x4[64:96, at] = high
-            x4[96:128, at] = low
+            pair = near if i % 2 == 0 or i == 1 else jnp.concatenate([pair, near], axis=1)
+            if i % 2 == 1 or i == EXT - 2:
+                last = (i + 1) * LANES
+                done = slice(last - pair.shape[1], last)
+                high = pair.astype(jnp.bfloat16)
+                low = (pair - high.astype(F32)).astype(jnp.bfloat16)
+                x4 = jnp.concatenate([high, low, high, low], axis=0)
+                state[:, done] = base[:, done] + jnp.dot(weight, x4, preferred_element_type=F32)
             before, here = here, after
-        for c in range(EXT // 2):
-            first, last = max(1, 2 * c), min(EXT - 1, 2 * c + 2)
-            at = slice(first * LANES, last * LANES)
-            state[:, at] = base[:, at] + jnp.dot(weight, x4[:, at], preferred_element_type=F32)
         return carry
 
     lax.fori_loop(0, SWEEPS, sweep, 0)
@@ -411,7 +451,6 @@
         scratch_shapes=[
             pltpu.VMEM((RANK, EXT * LANES), F32),
             pltpu.VMEM((RANK, EXT * LANES), F32),
-            pltpu.VMEM((4 * RANK, EXT * LANES), jnp.bfloat16),
             pltpu.VMEM((16, EXT * LANES), F32),
         ],
         compiler_params=grant(12),
@@ -461,9 +500,9 @@
     return near, far
 
 
-def edges(block, width, even):
+def chosen_edges(block, width, even):
     top, bottom = block[:, :width], block[:, block.shape[1] - width :]
-    return swapped(jnp.where(even, bottom, top), jnp.where(even, top, bottom))
+    return jnp.where(even, bottom, top), jnp.where(even, top, bottom)
 
 
 def per_device(data, space_init, time_init, variable_factor, neighbours):
@@ -473,18 +512,15 @@
     part = tm // 4
 
     hours = time_init.T
-    low = lax.ppermute(hours[-2:], "tm", [(i, (i + 1) % 16) for i in range(16)])
-    high = lax.ppermute(hours[:2], "tm", [((i + 1) % 16, i) for i in range(16)])
+    low = lax.ppermute(hours, "tm", [(i, (i + 1) % 16) for i in range(16)])
+    high = lax.ppermute(hours, "tm", [((i + 1) % 16, i) for i in range(16)])
     sums = project(data, space_init, variable_factor)
     got = lax.all_to_all(sums, "lat", 0, 0, tiled=True)
 
-    var_gram = jnp.dot(variable_factor.T, variable_factor, precision=HIGHEST, preferred_element_type=F32)
-    vg_lanes = jnp.pad(var_gram, ((0, 0), (0, LANES - RANK)))
-    low = jnp.where(tm == 0, 0.0, low)
-    high = jnp.where(tm == 15, 0.0, high)
+    low = jnp.where(tm == 0, 0.0, low[-2:])
+    high = jnp.where(tm == 15, 0.0, high[:2])
     padded = jnp.concatenate([low, hours, high], axis=0)
     stencil = padded[:-4] - 4.0 * padded[1:-3] - 4.0 * padded[3:-1] + padded[4:]
-    side = jnp.pad((-0.5 * stencil).T, ((0, 0), (32, 80)))
 
     own = jnp.concatenate([space_init, link_codes(neighbours[2:4])], axis=0)
     own, _ = lax.optimization_barrier((own, sums[0, 0, 0]))
@@ -492,7 +528,9 @@
     own = jnp.concatenate([own[:, :, NLON - 8 :], own, own[:, :, :30]], axis=2)
     own = lax.dynamic_slice_in_dim(own, part * WIDTH, LANES, axis=2)
     own = own.reshape(RANK + 2, ROWS * LANES)
-    start_near, start_far = edges(own, 8 * LANES, even)
+    to_near, to_far = chosen_edges(own, 8 * LANES, even)
+    to_near, to_far, got = lax.optimization_barrier((to_near, to_far, got))
+    start_near, start_far = swapped(to_near, to_far)
     start = jnp.concatenate(
         [
             jnp.where(even, start_far, start_near),
@@ -502,13 +540,14 @@
         axis=1,
     )
 
-    time_factor, terms = hour_mode(got, side, vg_lanes, variable_factor, data)
-    got = lax.all_to_all(terms, "tm", 0, 0, tiled=True)
+    time_factor, terms = hour_mode(got, stencil, variable_factor, data)
+    got = lax.all_to_all(terms, "tm", 0, 0, tiled=True, axis_index_groups=Y_GROUPS)
+    got = lax.all_to_all(part_totals(got), "tm", 0, 0, tiled=True, axis_index_groups=Z_GROUPS)
     pieces, gram = totals(got)
     rhs = lax.all_to_all(pieces, "tm", 0, 0, tiled=True, axis_index_groups=Z_GROUPS)
-    weight, inv, scale = operator(gram, vg_lanes)
+    weight, inv, scale = operator(gram, variable_factor)
     rhs = rhs.reshape(RANK, PIECE)
-    near, far = edges(rhs, EDGE, even)
+    near, far = swapped(*chosen_edges(rhs, EDGE, even))
     even_flag = jnp.where(even, 1, 0).astype(jnp.int32).reshape(1)
     blocks = sweeps(even_flag, rhs, near, far, start, weight, inv, scale)
     blocks = lax.all_to_all(blocks, "tm", 0, 0, tiled=True, axis_index_groups=Y_GROUPS)

time: 122 us -> 111 us (0.910)
  starting transfers between devices: 40.6 us -> 36 us
  waiting for transfers between devices: 50.3 us -> 46 us
  Pallas kernels: 24.6 us -> 23.2 us
    ppermute x2, waiting for transfers between devices: 17.6 us -> 4.56 us  [swapped(): far = lax.ppermute(edge_far, 'lat', SWAP_FAR)]
    all_to_all x1 -> x2, waiting for transfers between devices: 7.55 us -> 19.1 us  [the longest x1 13.2 us: per_device(): lax.all_to_all(terms, 'tm', 0, 0, tiled=True, axis_index_groups=Y_GROUPS)]
    ppermute x2, starting transfers between devices: 10.7 us -> 0.37 us  [swapped(): far = lax.ppermute(edge_far, 'lat', SWAP_FAR)]
    all_to_all x1 -> x2, starting transfers between devices: 6.7 us -> 12.3 us  [the longest x1 7.83 us: per_device(): lax.all_to_all(part_totals(got), 'tm', 0, 0, tiled=True, axis_index_group...]
    ppermute x2, waiting for transfers between devices: 5.16 us -> 0.01 us  [the longest x1 0.01 us: per_device(): low = lax.ppermute(hours, 'tm', [(i, (i + 1) % 16) for i in range(16)])]
    all_to_all x1, waiting for transfers between devices: 3.15 us -> 7.72 us  [per_device(): got = lax.all_to_all(sums, 'lat', 0, 0, tiled=True)]
    ppermute x2, starting transfers between devices: 0.1 us -> 3.27 us  [swapped(): near = lax.ppermute(edge_near, 'lat', SWAP_NEAR)]
    all_to_all x1, starting transfers between devices: 7.34 us -> 4.25 us  [per_device(): lax.all_to_all(pieces, 'tm', 0, 0, tiled=True, axis_index_groups=Z_GROUPS)]
  transfers between devices with their start and end apart: 10 -> 11, of which waited for: 8 -> 6; matrix products, arithmetic and copies ran while one was open for 3% -> 3% of each run, Pallas kernels for 2% -> 8%
where the time goes in v3:
time: 111 us; the launch traced here: 110 us
  waiting for transfers between devices  46 us (41%)
  starting transfers between devices  36 us (32%)
  Pallas kernels  23.2 us (21%)
  local copies, waits for them, and re-layouts  2.8 us (3%)
  other arithmetic  1.39 us (1%)
    all_to_all x1, waiting for transfers between devices, per_device(): lax.all_to_all(terms, 'tm', 0, 0, tiled=True, axis_index_groups=Y_GROUPS)  13.2 us
    all_to_all x1, starting transfers between devices, per_device(): got = lax.all_to_all(sums, 'lat', 0, 0, tiled=True)  10.1 us
    all_to_all x1, waiting for transfers between devices, per_device(): lax.all_to_all(blocks, 'tm', 0, 0, tiled=True, axis_index_groups=Y_GROUPS)  8.77 us
    all_to_all x1, starting transfers between devices, per_device(): lax.all_to_all(part_totals(got), 'tm', 0, 0, tiled=True, axis_index_group...  7.83 us
    all_to_all x1, waiting for transfers between devices, per_device(): got = lax.all_to_all(sums, 'lat', 0, 0, tiled=True)  7.72 us
    pallas_call x1, Pallas kernels, hour_mode(): pl.pallas_call(hour_kernel, in_specs=[vmem, vmem, vmem, pl.BlockSpec(memo...  6.3 us
    all_to_all x1, waiting for transfers between devices, per_device(): lax.all_to_all(part_totals(got), 'tm', 0, 0, tiled=True, axis_index_group...  5.92 us
    all_to_all x1, waiting for transfers between devices, per_device(): lax.all_to_all(pieces, 'tm', 0, 0, tiled=True, axis_index_groups=Z_GROUPS)  5.78 us
  transfers between devices with their start and end apart: 11, of which 6 were waited for; matrix products, arithmetic and copies ran while one was open for 3% of the time, Pallas kernels for 8%

profile of v3, /device:TPU:32, one launch (start us, length us, event | category | flops | bytes accessed | tf_op | source)
XLA Modules:
  0.0 110.3 jit_solution(13394288518140291188)
XLA Ops:
  0.6 1.9 %collective-permute-start.1 = (f32[16,32]{1,0:T(8,128)}, f32[16,32]{1,0:T(8,128)S(1)}, u32[]{:S(2)}, u32[]{:S(2)}) collective-permute-start(f32[16,32]{1,0:T(8,128)} %bitcast.11), channel_id=1, source_target_pairs={{1,0},{2,1},{3,2},{4,3},{5,4},{6,5},{7,6},{8,7},{9,8},{10,9},{11,1... | collective-permute-start | bytes 6152 | tf_op jit(solution)/shard_map/ppermute | solution.py:516
  2.5 0.2 collective-permute-start
  2.8 4.7 %project.1 = f32[16,8,256]{2,1,0:T(8,128)} custom-call(f32[8,16,5760]{2,1,0:T(8,128)} %data_ref.3, f32[32,5760]{1,0:T(8,128)} %space_ref.1, f32[8,32]{1,0:T(8,128)} %vf_ref.5), custom_call_target="tpu_custom_call" | custom-call | flops 4000000000 | bytes 8000000 | tf_op jit(solution)/shard_map/project/pallas_call | solution.py:129
  7.5 10.1 %all-to-all-start = ((f32[16,8,256]{2,1,0:T(8,128)}), f32[16,8,256]{2,1,0:T(8,128)S(1)}, u32[]{:S(2)}, u32[]{:S(2)}) async-start(f32[16,8,256]{2,1,0:T(8,128)} %project.1), calls=%async_computation | async-start | bytes 262144 | tf_op jit(solution)/shard_map/all_to_all | solution.py:518
  17.7 0.3 compare_select_fusion.2
  18.0 0.7 reshape.25
  18.8 0.1 slice.57
  19.0 0.3 fusion.1
  19.3 0.1 copy.8
  19.5 0.5 copy-done.5
  20.0 0.6 fusion.11.stencil_ref
  20.6 7.7 %all-to-all-done.got_ref = f32[16,8,256]{2,1,0:T(8,128)S(1)} async-done(((f32[16,8,256]{2,1,0:T(8,128)}), f32[16,8,256]{2,1,0:T(8,128)S(1)}, u32[]{:S(2)}, u32[]{:S(2)}) %all-to-all-start) | async-done | bytes 131104 | tf_op jit(solution)/shard_map/all_to_all | solution.py:518
  28.3 0.7 copy-done.2
  28.9 6.3 %hour_mode.1 = (f32[32,16]{1,0:T(8,128)}, f32[4,32,1792]{2,1,0:T(8,128)}) custom-call(f32[16,8,256]{2,1,0:T(8,128)} %copy-done.2, f32[16,32]{1,0:T(8,128)} %fusion.11.stencil_ref, f32[8,32]{1,0:T(8,128)} %vf_ref.5, f32[8,16,5760]{2,1,0:T(8,128)} %data_ref.3), custom_call_target="tpu_custom_call" | custom-call | flops 5000000000 | bytes 8000000 | tf_op jit(solution)/shard_map/hour_mode/pallas_call | solution.py:257
  35.2 4.5 %all-to-all-start.1 = ((f32[4,32,1792]{2,1,0:T(8,128)}), f32[4,32,1792]{2,1,0:T(8,128)S(1)}, u32[]{:S(2)}, u32[]{:S(2)}) async-start(f32[4,32,1792]{2,1,0:T(8,128)} %get-tuple-element.14), calls=%async_computation.1 | async-start | bytes 1835008 | tf_op jit(solution)/shard_map/all_to_all | solution.py:544
  39.7 0.3 collective-permute-start.4
  40.0 0.2 collective-permute-start.5
  40.2 13.2 %all-to-all-done.1.got_ref = f32[4,32,1792]{2,1,0:T(8,128)S(1)} async-done(((f32[4,32,1792]{2,1,0:T(8,128)}), f32[4,32,1792]{2,1,0:T(8,128)S(1)}, u32[]{:S(2)}, u32[]{:S(2)}) %all-to-all-start.1) | async-done | bytes 917536 | tf_op jit(solution)/shard_map/all_to_all | solution.py:544
  53.4 0.7 part_totals.1
  54.2 7.8 %all-to-all-start.2 = ((f32[4,8,1792]{2,1,0:T(8,128)}), f32[4,8,1792]{2,1,0:T(8,128)S(1)}, u32[]{:S(2)}, u32[]{:S(2)}) async-start(f32[4,8,1792]{2,1,0:T(8,128)} %part_totals.1), calls=%async_computation.2 | async-start | bytes 458752 | tf_op jit(solution)/shard_map/all_to_all | solution.py:545
  62.0 5.9 %all-to-all-done.2.got_ref = f32[4,8,1792]{2,1,0:T(8,128)S(1)} async-done(((f32[4,8,1792]{2,1,0:T(8,128)}), f32[4,8,1792]{2,1,0:T(8,128)S(1)}, u32[]{:S(2)}, u32[]{:S(2)}) %all-to-all-start.2) | async-done | bytes 229408 | tf_op jit(solution)/shard_map/all_to_all | solution.py:545
  67.9 0.7 totals.1
  68.7 4.2 %all-to-all-start.3 = ((f32[4,8,1664]{2,1,0:T(8,128)}), f32[4,8,1664]{2,1,0:T(8,128)S(1)}, u32[]{:S(2)}, u32[]{:S(2)}) async-start(f32[4,8,1664]{2,1,0:T(8,128)} %get-tuple-element.15), calls=%async_computation.3 | async-start | bytes 425984 | tf_op jit(solution)/shard_map/all_to_all | solution.py:547
  72.9 5.8 %all-to-all-done.3 = f32[4,8,1664]{2,1,0:T(8,128)S(1)} async-done(((f32[4,8,1664]{2,1,0:T(8,128)}), f32[4,8,1664]{2,1,0:T(8,128)S(1)}, u32[]{:S(2)}, u32[]{:S(2)}) %all-to-all-start.3) | async-done | bytes 213024 | tf_op jit(solution)/shard_map/all_to_all | solution.py:547
  78.8 3.0 %collective-permute-start.2 = (f32[32,768]{1,0:T(8,128)S(1)}, f32[32,768]{1,0:T(8,128)S(1)}, u32[]{:S(2)}, u32[]{:S(2)}) collective-permute-start(f32[32,768]{1,0:T(8,128)S(1)} %get-tuple-element.29), channel_id=1, source_target_pairs={{0,16},{16,0},{32,48},{48,32},{64,80},{80,64},{96,112},{112,96},{1... | collective-permute-start | bytes 294920 | tf_op jit(solution)/shard_map/ppermute | solution.py:499
  81.9 3.0 %operator.1 = (bf16[32,128]{1,0:T(8,128)(2,1)S(1)}, bf16[32,256]{1,0:T(8,128)(2,1)S(1)}, f32[32,128]{1,0:T(8,128)S(1)}) custom-call(f32[8,128]{1,0:T(8,128)S(1)} %get-tuple-element.18.gram_ref, f32[8,32]{1,0:T(8,128)S(1)} %copy-done), custom_call_target="tpu_custom_call" | custom-call | flops 4000000000 | bytes 100000 | tf_op jit(solution)/shard_map/operator/pallas_call | solution.py:349
  84.9 4.6 %collective-permute-done.3.far_ref = f32[32,768]{1,0:T(8,128)S(1)} collective-permute-done((f32[32,768]{1,0:T(8,128)S(1)}, f32[32,768]{1,0:T(8,128)S(1)}, u32[]{:S(2)}, u32[]{:S(2)}) %collective-permute-start.3) | collective-permute-done | bytes 98336 | tf_op jit(solution)/shard_map/ppermute | solution.py:498
  89.5 5.4 %sweeps.1 = f32[4,32,1536]{2,1,0:T(8,128)} custom-call(s32[1]{0:T(128)} %bitcast.1.even_ref, f32[32,1664]{1,0:T(8,128)S(1)} %bitcast.7, f32[32,768]{1,0:T(8,128)S(1)} %collective-permute-done.2.near_ref, f32[32,768]{1,0:T(8,128)S(1)} %collective-permute-done.3.far_ref, f32[34,4096]{1,0:T(8,128)S(1)} %pad_maximum_fusion.1.start_ref, ...), custom_call_target="tpu_custom_call" | custom-call | tf_op jit(solution)/shard_map/sweeps/pallas_call | solution.py:446
  94.9 3.6 %all-to-all-start.4 = ((f32[4,32,1536]{2,1,0:T(8,128)}), f32[4,32,1536]{2,1,0:T(8,128)S(1)}, u32[]{:S(2)}, u32[]{:S(2)}) async-start(f32[4,32,1536]{2,1,0:T(8,128)} %sweeps.1), calls=%async_computation.4 | async-start | bytes 1572864 | tf_op jit(solution)/shard_map/all_to_all | solution.py:553
  98.5 0.7 copy.7
  99.2 8.8 %all-to-all-done.4.got_ref = f32[4,32,1536]{2,1,0:T(8,128)S(1)} async-done(((f32[4,32,1536]{2,1,0:T(8,128)}), f32[4,32,1536]{2,1,0:T(8,128)S(1)}, u32[]{:S(2)}, u32[]{:S(2)}) %all-to-all-start.4) | async-done | bytes 786464 | tf_op jit(solution)/shard_map/all_to_all | solution.py:553
  108.0 2.3 %join.1 = f32[32,5760]{1,0:T(8,128)} custom-call(f32[4,32,1536]{2,1,0:T(8,128)S(1)} %all-to-all-done.4.got_ref), custom_call_target="tpu_custom_call" | custom-call | tf_op jit(solution)/shard_map/join/pallas_call | solution.py:480
  (26 shorter events, 0.4 us)
Async XLA Ops:
  0.6 17.0 %copy-start.3 = (s32[4,5760]{1,0:T(4,128)S(1)}, s32[4,5760]{1,0:T(4,128)}, u32[]{:S(2)}) copy-start(s32[4,5760]{1,0:T(4,128)} %param.9) | copy-start | bytes 276484
  0.6 17.3 %copy-start.1 = (f32[32,5760]{1,0:T(8,128)S(1)}, f32[32,5760]{1,0:T(8,128)}, u32[]{:S(2)}) copy-start(f32[32,5760]{1,0:T(8,128)} %space_ref.1) | copy-start | bytes 2211844
  0.6 18.8 %collective-permute-start.1 = (f32[16,32]{1,0:T(8,128)}, f32[16,32]{1,0:T(8,128)S(1)}, u32[]{:S(2)}, u32[]{:S(2)}) collective-permute-start(f32[16,32]{1,0:T(8,128)} %bitcast.11), channel_id=1, source_target_pairs={{1,0},{2,1},{3,2},{4,3},{5,4},{6,5},{7,6},{8,7},{9,8},{10,9},{11,1... | collective-permute-start | bytes 6152 | tf_op jit(solution)/shard_map/ppermute | solution.py:516
  2.5 16.9 %collective-permute-start = (f32[16,32]{1,0:T(8,128)}, f32[16,32]{1,0:T(8,128)S(1)}, u32[]{:S(2)}, u32[]{:S(2)}) collective-permute-start(f32[16,32]{1,0:T(8,128)} %bitcast.12), channel_id=1, source_target_pairs={{0,1},{1,2},{2,3},{3,4},{4,5},{5,6},{6,7},{7,8},{8,9},{9,10},{10,1... | collective-permute-start | bytes 6152 | tf_op jit(solution)/shard_map/ppermute | solution.py:515
  7.5 20.8 %all-to-all-start = ((f32[16,8,256]{2,1,0:T(8,128)}), f32[16,8,256]{2,1,0:T(8,128)S(1)}, u32[]{:S(2)}, u32[]{:S(2)}) async-start(f32[16,8,256]{2,1,0:T(8,128)} %project.1), calls=%async_computation | async-start | bytes 262144 | tf_op jit(solution)/shard_map/all_to_all | solution.py:518
  19.3 0.7 copy-start.5
  28.3 0.7 copy-start.2
  35.2 18.2 %all-to-all-start.1 = ((f32[4,32,1792]{2,1,0:T(8,128)}), f32[4,32,1792]{2,1,0:T(8,128)S(1)}, u32[]{:S(2)}, u32[]{:S(2)}) async-start(f32[4,32,1792]{2,1,0:T(8,128)} %get-tuple-element.14), calls=%async_computation.1 | async-start | bytes 1835008 | tf_op jit(solution)/shard_map/all_to_all | solution.py:544
  39.7 22.3 %collective-permute-start.4 = (f32[34,1024]{1,0:T(8,128)S(1)}, f32[34,1024]{1,0:T(8,128)S(1)}, u32[]{:S(2)}, u32[]{:S(2)}) collective-permute-start(f32[34,1024]{1,0:T(8,128)S(1)} %get-tuple-element.16), channel_id=1, source_target_pairs={{0,240},{16,32},{32,16},{48,64},{64,48},{80,96},{96,80},{112,128},... | collective-permute-start | bytes 417800 | tf_op jit(solution)/shard_map/ppermute | solution.py:498
  40.0 22.0 %collective-permute-start.5 = (f32[34,1024]{1,0:T(8,128)S(1)}, f32[34,1024]{1,0:T(8,128)S(1)}, u32[]{:S(2)}, u32[]{:S(2)}) collective-permute-start(f32[34,1024]{1,0:T(8,128)S(1)} %get-tuple-element.17), channel_id=1, source_target_pairs={{0,16},{16,0},{32,48},{48,32},{64,80},{80,64},{96,112},{112,96},{1... | collective-permute-start | bytes 417800 | tf_op jit(solution)/shard_map/ppermute | solution.py:499
  54.2 13.8 %all-to-all-start.2 = ((f32[4,8,1792]{2,1,0:T(8,128)}), f32[4,8,1792]{2,1,0:T(8,128)S(1)}, u32[]{:S(2)}, u32[]{:S(2)}) async-start(f32[4,8,1792]{2,1,0:T(8,128)} %part_totals.1), calls=%async_computation.2 | async-start | bytes 458752 | tf_op jit(solution)/shard_map/all_to_all | solution.py:545
  68.7 13.2 %copy-start = (f32[8,32]{1,0:T(8,128)S(1)}, f32[8,32]{1,0:T(8,128)}, u32[]{:S(2)}) copy-start(f32[8,32]{1,0:T(8,128)} %vf_ref.5) | copy-start | bytes 3076
  68.7 10.1 %all-to-all-start.3 = ((f32[4,8,1664]{2,1,0:T(8,128)}), f32[4,8,1664]{2,1,0:T(8,128)S(1)}, u32[]{:S(2)}, u32[]{:S(2)}) async-start(f32[4,8,1664]{2,1,0:T(8,128)} %get-tuple-element.15), calls=%async_computation.3 | async-start | bytes 425984 | tf_op jit(solution)/shard_map/all_to_all | solution.py:547
  78.7 10.8 %collective-permute-start.3 = (f32[32,768]{1,0:T(8,128)S(1)}, f32[32,768]{1,0:T(8,128)S(1)}, u32[]{:S(2)}, u32[]{:S(2)}) collective-permute-start(f32[32,768]{1,0:T(8,128)S(1)} %get-tuple-element.28), channel_id=1, source_target_pairs={{0,240},{16,32},{32,16},{48,64},{64,48},{80,96},{96,80},{112,128},... | collective-permute-start | bytes 294920 | tf_op jit(solution)/shard_map/ppermute | solution.py:498
  78.8 10.7 %collective-permute-start.2 = (f32[32,768]{1,0:T(8,128)S(1)}, f32[32,768]{1,0:T(8,128)S(1)}, u32[]{:S(2)}, u32[]{:S(2)}) collective-permute-start(f32[32,768]{1,0:T(8,128)S(1)} %get-tuple-element.29), channel_id=1, source_target_pairs={{0,16},{16,0},{32,48},{48,32},{64,80},{80,64},{96,112},{112,96},{1... | collective-permute-start | bytes 294920 | tf_op jit(solution)/shard_map/ppermute | solution.py:499
  94.9 3.6 %copy-start.4 = (f32[32,16]{1,0:T(8,128)S(1)}, f32[32,16]{1,0:T(8,128)}, u32[]{:S(2)}) copy-start(f32[32,16]{1,0:T(8,128)} %get-tuple-element.22) | copy-start | bytes 6148
  94.9 13.1 %all-to-all-start.4 = ((f32[4,32,1536]{2,1,0:T(8,128)}), f32[4,32,1536]{2,1,0:T(8,128)S(1)}, u32[]{:S(2)}, u32[]{:S(2)}) async-start(f32[4,32,1536]{2,1,0:T(8,128)} %sweeps.1), calls=%async_computation.4 | async-start | bytes 1572864 | tf_op jit(solution)/shard_map/all_to_all | solution.py:553

commit v4 on v3

--- a/solution.py
+++ b/solution.py
@@ -399,9 +399,10 @@
         tiles = [state[8 * g : 8 * g + 8, at] for g in range(4)]
         return [(turn(c, -1), c, turn(c, 1)) for c in tiles]
 
-    def sweep(_, carry):
-        before, here = line(0), line(1)
-        for i in range(1, EXT - 1):
+    for step in range(SWEEPS):
+        low_row, high_row = 1 + step, EXT - 1 - step
+        before, here = line(low_row - 1), line(low_row)
+        for i in range(low_row, high_row):
             at = slice(i * LANES, (i + 1) * LANES)
             after = line(i + 1)
             picks = [[codes[8 * d : 8 * d + 8, at] == k for k in (1.0, 2.0, 3.0)] for d in range(2)]
@@ -419,8 +420,10 @@
                 ],
                 axis=0,
             )
-            pair = near if i % 2 == 0 or i == 1 else jnp.concatenate([pair, near], axis=1)
-            if i % 2 == 1 or i == EXT - 2:
+            if (i - low_row) % 2 == 0:
+                first = near
+            else:
+                pair = jnp.concatenate([first, near], axis=1)
                 last = (i + 1) * LANES
                 done = slice(last - pair.shape[1], last)
                 high = pair.astype(jnp.bfloat16)
@@ -428,9 +431,6 @@
                 x4 = jnp.concatenate([high, low, high, low], axis=0)
                 state[:, done] = base[:, done] + jnp.dot(weight, x4, preferred_element_type=F32)
             before, here = here, after
-        return carry
-
-    lax.fori_loop(0, SWEEPS, sweep, 0)
 
     def store(t, value):
         for k in range(PARTS):
@@ -472,7 +472,7 @@
             held = jnp.where(off + WIDTH >= LANES, moved, value)
         return held
 
-    lax.fori_loop(0, ROWS, row, jnp.zeros((RANK, LANES), F32))
+    lax.fori_loop(0, ROWS, row, jnp.zeros((RANK, LANES), F32), unroll=16)
 
 
 def join(got):

time: 111 us -> 108 us (0.973)
  Pallas kernels: 23.2 us -> 20.3 us
    pallas_call x1, Pallas kernels: 5.37 us -> 3.57 us  [sweeps(): pl.pallas_call(sweep_kernel, in_specs=[pl.BlockSpec(memory_space=pltpu.SM...]
    pallas_call x1, Pallas kernels: 2.33 us -> 1.2 us  [join(): pl.pallas_call(join_kernel, in_specs=[vmem], out_specs=vmem, out_shape=ja...]
where the time goes in v4:
time: 108 us; the launch traced here: 107 us
  waiting for transfers between devices  46 us (43%)
  starting transfers between devices  36 us (33%)
  Pallas kernels  20.3 us (19%)
  local copies, waits for them, and re-layouts  2.8 us (3%)
  other arithmetic  1.39 us (1%)
    all_to_all x1, waiting for transfers between devices, per_device(): lax.all_to_all(terms, 'tm', 0, 0, tiled=True, axis_index_groups=Y_GROUPS)  13.2 us
    all_to_all x1, starting transfers between devices, per_device(): got = lax.all_to_all(sums, 'lat', 0, 0, tiled=True)  10.1 us
    all_to_all x1, waiting for transfers between devices, per_device(): lax.all_to_all(blocks, 'tm', 0, 0, tiled=True, axis_index_groups=Y_GROUPS)  8.77 us
    all_to_all x1, starting transfers between devices, per_device(): lax.all_to_all(part_totals(got), 'tm', 0, 0, tiled=True, axis_index_group...  7.83 us
    all_to_all x1, waiting for transfers between devices, per_device(): got = lax.all_to_all(sums, 'lat', 0, 0, tiled=True)  7.72 us
    pallas_call x1, Pallas kernels, hour_mode(): pl.pallas_call(hour_kernel, in_specs=[vmem, vmem, vmem, pl.BlockSpec(memo...  6.3 us
    all_to_all x1, waiting for transfers between devices, per_device(): lax.all_to_all(part_totals(got), 'tm', 0, 0, tiled=True, axis_index_group...  5.92 us
    all_to_all x1, waiting for transfers between devices, per_device(): lax.all_to_all(pieces, 'tm', 0, 0, tiled=True, axis_index_groups=Z_GROUPS)  5.78 us
  transfers between devices with their start and end apart: 11, of which 6 were waited for; matrix products, arithmetic and copies ran while one was open for 3% of the time, Pallas kernels for 8%

profile of v4, /device:TPU:32, one launch (start us, length us, event | category | flops | bytes accessed | tf_op | source)
XLA Modules:
  0.0 107.4 jit_solution(11062981083264824697)
XLA Ops:
  0.6 1.9 %collective-permute-start.1 = (f32[16,32]{1,0:T(8,128)}, f32[16,32]{1,0:T(8,128)S(1)}, u32[]{:S(2)}, u32[]{:S(2)}) collective-permute-start(f32[16,32]{1,0:T(8,128)} %bitcast.11), channel_id=1, source_target_pairs={{1,0},{2,1},{3,2},{4,3},{5,4},{6,5},{7,6},{8,7},{9,8},{10,9},{11,1... | collective-permute-start | bytes 6152 | tf_op jit(solution)/shard_map/ppermute | solution.py:516
  2.5 0.2 collective-permute-start
  2.8 4.7 %project.1 = f32[16,8,256]{2,1,0:T(8,128)} custom-call(f32[8,16,5760]{2,1,0:T(8,128)} %data_ref.3, f32[32,5760]{1,0:T(8,128)} %space_ref.1, f32[8,32]{1,0:T(8,128)} %vf_ref.5), custom_call_target="tpu_custom_call" | custom-call | flops 4000000000 | bytes 8000000 | tf_op jit(solution)/shard_map/project/pallas_call | solution.py:129
  7.5 10.1 %all-to-all-start = ((f32[16,8,256]{2,1,0:T(8,128)}), f32[16,8,256]{2,1,0:T(8,128)S(1)}, u32[]{:S(2)}, u32[]{:S(2)}) async-start(f32[16,8,256]{2,1,0:T(8,128)} %project.1), calls=%async_computation | async-start | bytes 262144 | tf_op jit(solution)/shard_map/all_to_all | solution.py:518
  17.7 0.3 compare_select_fusion.2
  18.0 0.7 reshape.25
  18.8 0.1 slice.57
  19.0 0.3 fusion.1
  19.3 0.1 copy.8
  19.5 0.5 copy-done.5
  20.0 0.6 fusion.11.stencil_ref
  20.6 7.7 %all-to-all-done.got_ref = f32[16,8,256]{2,1,0:T(8,128)S(1)} async-done(((f32[16,8,256]{2,1,0:T(8,128)}), f32[16,8,256]{2,1,0:T(8,128)S(1)}, u32[]{:S(2)}, u32[]{:S(2)}) %all-to-all-start) | async-done | bytes 131104 | tf_op jit(solution)/shard_map/all_to_all | solution.py:518
  28.3 0.7 copy-done.2
  28.9 6.3 %hour_mode.1 = (f32[32,16]{1,0:T(8,128)}, f32[4,32,1792]{2,1,0:T(8,128)}) custom-call(f32[16,8,256]{2,1,0:T(8,128)} %copy-done.2, f32[16,32]{1,0:T(8,128)} %fusion.11.stencil_ref, f32[8,32]{1,0:T(8,128)} %vf_ref.5, f32[8,16,5760]{2,1,0:T(8,128)} %data_ref.3), custom_call_target="tpu_custom_call" | custom-call | flops 5000000000 | bytes 8000000 | tf_op jit(solution)/shard_map/hour_mode/pallas_call | solution.py:257
  35.2 4.5 %all-to-all-start.1 = ((f32[4,32,1792]{2,1,0:T(8,128)}), f32[4,32,1792]{2,1,0:T(8,128)S(1)}, u32[]{:S(2)}, u32[]{:S(2)}) async-start(f32[4,32,1792]{2,1,0:T(8,128)} %get-tuple-element.14), calls=%async_computation.1 | async-start | bytes 1835008 | tf_op jit(solution)/shard_map/all_to_all | solution.py:544
  39.7 0.3 collective-permute-start.4
  40.0 0.2 collective-permute-start.5
  40.2 13.2 %all-to-all-done.1.got_ref = f32[4,32,1792]{2,1,0:T(8,128)S(1)} async-done(((f32[4,32,1792]{2,1,0:T(8,128)}), f32[4,32,1792]{2,1,0:T(8,128)S(1)}, u32[]{:S(2)}, u32[]{:S(2)}) %all-to-all-start.1) | async-done | bytes 917536 | tf_op jit(solution)/shard_map/all_to_all | solution.py:544
  53.4 0.7 part_totals.1
  54.2 7.8 %all-to-all-start.2 = ((f32[4,8,1792]{2,1,0:T(8,128)}), f32[4,8,1792]{2,1,0:T(8,128)S(1)}, u32[]{:S(2)}, u32[]{:S(2)}) async-start(f32[4,8,1792]{2,1,0:T(8,128)} %part_totals.1), calls=%async_computation.2 | async-start | bytes 458752 | tf_op jit(solution)/shard_map/all_to_all | solution.py:545
  62.0 5.9 %all-to-all-done.2.got_ref = f32[4,8,1792]{2,1,0:T(8,128)S(1)} async-done(((f32[4,8,1792]{2,1,0:T(8,128)}), f32[4,8,1792]{2,1,0:T(8,128)S(1)}, u32[]{:S(2)}, u32[]{:S(2)}) %all-to-all-start.2) | async-done | bytes 229408 | tf_op jit(solution)/shard_map/all_to_all | solution.py:545
  67.9 0.7 totals.1
  68.6 4.2 %all-to-all-start.3 = ((f32[4,8,1664]{2,1,0:T(8,128)}), f32[4,8,1664]{2,1,0:T(8,128)S(1)}, u32[]{:S(2)}, u32[]{:S(2)}) async-start(f32[4,8,1664]{2,1,0:T(8,128)} %get-tuple-element.15), calls=%async_computation.3 | async-start | bytes 425984 | tf_op jit(solution)/shard_map/all_to_all | solution.py:547
  72.9 5.8 %all-to-all-done.3 = f32[4,8,1664]{2,1,0:T(8,128)S(1)} async-done(((f32[4,8,1664]{2,1,0:T(8,128)}), f32[4,8,1664]{2,1,0:T(8,128)S(1)}, u32[]{:S(2)}, u32[]{:S(2)}) %all-to-all-start.3) | async-done | bytes 213024 | tf_op jit(solution)/shard_map/all_to_all | solution.py:547
  78.8 3.0 %collective-permute-start.2 = (f32[32,768]{1,0:T(8,128)S(1)}, f32[32,768]{1,0:T(8,128)S(1)}, u32[]{:S(2)}, u32[]{:S(2)}) collective-permute-start(f32[32,768]{1,0:T(8,128)S(1)} %get-tuple-element.29), channel_id=1, source_target_pairs={{0,16},{16,0},{32,48},{48,32},{64,80},{80,64},{96,112},{112,96},{1... | collective-permute-start | bytes 294920 | tf_op jit(solution)/shard_map/ppermute | solution.py:499
  81.9 3.0 %operator.1 = (bf16[32,128]{1,0:T(8,128)(2,1)S(1)}, bf16[32,256]{1,0:T(8,128)(2,1)S(1)}, f32[32,128]{1,0:T(8,128)S(1)}) custom-call(f32[8,128]{1,0:T(8,128)S(1)} %get-tuple-element.18.gram_ref, f32[8,32]{1,0:T(8,128)S(1)} %copy-done), custom_call_target="tpu_custom_call" | custom-call | flops 4000000000 | bytes 100000 | tf_op jit(solution)/shard_map/operator/pallas_call | solution.py:349
  84.9 4.6 %collective-permute-done.3.far_ref = f32[32,768]{1,0:T(8,128)S(1)} collective-permute-done((f32[32,768]{1,0:T(8,128)S(1)}, f32[32,768]{1,0:T(8,128)S(1)}, u32[]{:S(2)}, u32[]{:S(2)}) %collective-permute-start.3) | collective-permute-done | bytes 98336 | tf_op jit(solution)/shard_map/ppermute | solution.py:498
  89.5 3.6 %sweeps.1 = f32[4,32,1536]{2,1,0:T(8,128)} custom-call(s32[1]{0:T(128)} %bitcast.1.even_ref, f32[32,1664]{1,0:T(8,128)S(1)} %bitcast.7, f32[32,768]{1,0:T(8,128)S(1)} %collective-permute-done.2.near_ref, f32[32,768]{1,0:T(8,128)S(1)} %collective-permute-done.3.far_ref, f32[34,4096]{1,0:T(8,128)S(1)} %pad_maximum_fusion.1.start_ref, ...), custom_call_target="tpu_custom_call" | custom-call | tf_op jit(solution)/shard_map/sweeps/pallas_call | solution.py:446
  93.1 3.6 %all-to-all-start.4 = ((f32[4,32,1536]{2,1,0:T(8,128)}), f32[4,32,1536]{2,1,0:T(8,128)S(1)}, u32[]{:S(2)}, u32[]{:S(2)}) async-start(f32[4,32,1536]{2,1,0:T(8,128)} %sweeps.1), calls=%async_computation.4 | async-start | bytes 1572864 | tf_op jit(solution)/shard_map/all_to_all | solution.py:553
  96.7 0.7 copy.7
  97.4 8.8 %all-to-all-done.4.got_ref = f32[4,32,1536]{2,1,0:T(8,128)S(1)} async-done(((f32[4,32,1536]{2,1,0:T(8,128)}), f32[4,32,1536]{2,1,0:T(8,128)S(1)}, u32[]{:S(2)}, u32[]{:S(2)}) %all-to-all-start.4) | async-done | bytes 786464 | tf_op jit(solution)/shard_map/all_to_all | solution.py:553
  106.2 1.2 %join.1 = f32[32,5760]{1,0:T(8,128)} custom-call(f32[4,32,1536]{2,1,0:T(8,128)S(1)} %all-to-all-done.4.got_ref), custom_call_target="tpu_custom_call" | custom-call | tf_op jit(solution)/shard_map/join/pallas_call | solution.py:480
  (26 shorter events, 0.4 us)
Async XLA Ops:
  0.6 17.0 %copy-start.3 = (s32[4,5760]{1,0:T(4,128)S(1)}, s32[4,5760]{1,0:T(4,128)}, u32[]{:S(2)}) copy-start(s32[4,5760]{1,0:T(4,128)} %param.9) | copy-start | bytes 276484
  0.6 17.3 %copy-start.1 = (f32[32,5760]{1,0:T(8,128)S(1)}, f32[32,5760]{1,0:T(8,128)}, u32[]{:S(2)}) copy-start(f32[32,5760]{1,0:T(8,128)} %space_ref.1) | copy-start | bytes 2211844
  0.6 18.8 %collective-permute-start.1 = (f32[16,32]{1,0:T(8,128)}, f32[16,32]{1,0:T(8,128)S(1)}, u32[]{:S(2)}, u32[]{:S(2)}) collective-permute-start(f32[16,32]{1,0:T(8,128)} %bitcast.11), channel_id=1, source_target_pairs={{1,0},{2,1},{3,2},{4,3},{5,4},{6,5},{7,6},{8,7},{9,8},{10,9},{11,1... | collective-permute-start | bytes 6152 | tf_op jit(solution)/shard_map/ppermute | solution.py:516
  2.5 16.9 %collective-permute-start = (f32[16,32]{1,0:T(8,128)}, f32[16,32]{1,0:T(8,128)S(1)}, u32[]{:S(2)}, u32[]{:S(2)}) collective-permute-start(f32[16,32]{1,0:T(8,128)} %bitcast.12), channel_id=1, source_target_pairs={{0,1},{1,2},{2,3},{3,4},{4,5},{5,6},{6,7},{7,8},{8,9},{9,10},{10,1... | collective-permute-start | bytes 6152 | tf_op jit(solution)/shard_map/ppermute | solution.py:515
  7.5 20.8 %all-to-all-start = ((f32[16,8,256]{2,1,0:T(8,128)}), f32[16,8,256]{2,1,0:T(8,128)S(1)}, u32[]{:S(2)}, u32[]{:S(2)}) async-start(f32[16,8,256]{2,1,0:T(8,128)} %project.1), calls=%async_computation | async-start | bytes 262144 | tf_op jit(solution)/shard_map/all_to_all | solution.py:518
  19.3 0.7 copy-start.5
  28.3 0.7 copy-start.2
  35.2 18.2 %all-to-all-start.1 = ((f32[4,32,1792]{2,1,0:T(8,128)}), f32[4,32,1792]{2,1,0:T(8,128)S(1)}, u32[]{:S(2)}, u32[]{:S(2)}) async-start(f32[4,32,1792]{2,1,0:T(8,128)} %get-tuple-element.14), calls=%async_computation.1 | async-start | bytes 1835008 | tf_op jit(solution)/shard_map/all_to_all | solution.py:544
  39.7 22.3 %collective-permute-start.4 = (f32[34,1024]{1,0:T(8,128)S(1)}, f32[34,1024]{1,0:T(8,128)S(1)}, u32[]{:S(2)}, u32[]{:S(2)}) collective-permute-start(f32[34,1024]{1,0:T(8,128)S(1)} %get-tuple-element.16), channel_id=1, source_target_pairs={{0,240},{16,32},{32,16},{48,64},{64,48},{80,96},{96,80},{112,128},... | collective-permute-start | bytes 417800 | tf_op jit(solution)/shard_map/ppermute | solution.py:498
  40.0 22.0 %collective-permute-start.5 = (f32[34,1024]{1,0:T(8,128)S(1)}, f32[34,1024]{1,0:T(8,128)S(1)}, u32[]{:S(2)}, u32[]{:S(2)}) collective-permute-start(f32[34,1024]{1,0:T(8,128)S(1)} %get-tuple-element.17), channel_id=1, source_target_pairs={{0,16},{16,0},{32,48},{48,32},{64,80},{80,64},{96,112},{112,96},{1... | collective-permute-start | bytes 417800 | tf_op jit(solution)/shard_map/ppermute | solution.py:499
  54.2 13.8 %all-to-all-start.2 = ((f32[4,8,1792]{2,1,0:T(8,128)}), f32[4,8,1792]{2,1,0:T(8,128)S(1)}, u32[]{:S(2)}, u32[]{:S(2)}) async-start(f32[4,8,1792]{2,1,0:T(8,128)} %part_totals.1), calls=%async_computation.2 | async-start | bytes 458752 | tf_op jit(solution)/shard_map/all_to_all | solution.py:545
  68.6 13.2 %copy-start = (f32[8,32]{1,0:T(8,128)S(1)}, f32[8,32]{1,0:T(8,128)}, u32[]{:S(2)}) copy-start(f32[8,32]{1,0:T(8,128)} %vf_ref.5) | copy-start | bytes 3076
  68.6 10.1 %all-to-all-start.3 = ((f32[4,8,1664]{2,1,0:T(8,128)}), f32[4,8,1664]{2,1,0:T(8,128)S(1)}, u32[]{:S(2)}, u32[]{:S(2)}) async-start(f32[4,8,1664]{2,1,0:T(8,128)} %get-tuple-element.15), calls=%async_computation.3 | async-start | bytes 425984 | tf_op jit(solution)/shard_map/all_to_all | solution.py:547
  78.7 10.8 %collective-permute-start.3 = (f32[32,768]{1,0:T(8,128)S(1)}, f32[32,768]{1,0:T(8,128)S(1)}, u32[]{:S(2)}, u32[]{:S(2)}) collective-permute-start(f32[32,768]{1,0:T(8,128)S(1)} %get-tuple-element.28), channel_id=1, source_target_pairs={{0,240},{16,32},{32,16},{48,64},{64,48},{80,96},{96,80},{112,128},... | collective-permute-start | bytes 294920 | tf_op jit(solution)/shard_map/ppermute | solution.py:498
  78.8 10.7 %collective-permute-start.2 = (f32[32,768]{1,0:T(8,128)S(1)}, f32[32,768]{1,0:T(8,128)S(1)}, u32[]{:S(2)}, u32[]{:S(2)}) collective-permute-start(f32[32,768]{1,0:T(8,128)S(1)} %get-tuple-element.29), channel_id=1, source_target_pairs={{0,16},{16,0},{32,48},{48,32},{64,80},{80,64},{96,112},{112,96},{1... | collective-permute-start | bytes 294920 | tf_op jit(solution)/shard_map/ppermute | solution.py:499
  93.1 3.6 %copy-start.4 = (f32[32,16]{1,0:T(8,128)S(1)}, f32[32,16]{1,0:T(8,128)}, u32[]{:S(2)}) copy-start(f32[32,16]{1,0:T(8,128)} %get-tuple-element.22) | copy-start | bytes 6148
  93.1 13.1 %all-to-all-start.4 = ((f32[4,32,1536]{2,1,0:T(8,128)}), f32[4,32,1536]{2,1,0:T(8,128)S(1)}, u32[]{:S(2)}, u32[]{:S(2)}) async-start(f32[4,32,1536]{2,1,0:T(8,128)} %sweeps.1), calls=%async_computation.4 | async-start | bytes 1572864 | tf_op jit(solution)/shard_map/all_to_all | solution.py:553

commit v5 on v4

--- a/solution.py
+++ b/solution.py
@@ -54,12 +54,23 @@
     return jnp.concatenate(tiles, axis=0)
 
 
+PANEL = 4
+
+
 def eliminated(a):
     row = row_iota(RANK)
-    for k in range(RANK):
-        pivot_row = a[k : k + 1, :]
-        q = pivot_row / pivot_row[:, k : k + 1]
-        a = jnp.where(row == k, q, a - a[:, k : k + 1] * q)
+    for first in range(0, RANK, PANEL):
+        cols = [jnp.broadcast_to(a[:, k : k + 1], (RANK, LANES)) for k in range(first, first + PANEL)]
+        for i in range(PANEL):
+            k = first + i
+            here = row == k
+            col = cols[i]
+            r = 1.0 / col[k : k + 1, :]
+            q = a[k : k + 1, :] * r
+            a = jnp.where(here, q, a - col * q)
+            for j in range(i + 1, PANEL):
+                t = cols[j][k : k + 1, :] * r
+                cols[j] = jnp.where(here, t, cols[j] - col * t)
     return a
 
 

time: 108 us -> 106 us (0.981)
  Pallas kernels: 20.3 us -> 17.2 us
  waiting for transfers between devices: 46 us -> 47.5 us
    pallas_call x1, Pallas kernels: 3.05 us -> 1.5 us  [operator(): pl.pallas_call(operator_kernel, in_specs=[vmem, vmem], out_specs=(vmem, v...]
    ppermute x2, waiting for transfers between devices: 4.58 us -> 6.13 us  [swapped(): far = lax.ppermute(edge_far, 'lat', SWAP_FAR)]
    pallas_call x1, Pallas kernels: 6.3 us -> 4.77 us  [hour_mode(): pl.pallas_call(hour_kernel, in_specs=[vmem, vmem, vmem, pl.BlockSpec(memo...]
  transfers between devices with their start and end apart: 11 -> 11, of which waited for: 6 -> 6; matrix products, arithmetic and copies ran while one was open for 3% -> 3% of each run, Pallas kernels for 8% -> 7%
where the time goes in v5:
time: 106 us
  waiting for transfers between devices  47.5 us (45%)
  starting transfers between devices  36 us (34%)
  Pallas kernels  17.2 us (16%)
  local copies, waits for them, and re-layouts  2.8 us (3%)
  other arithmetic  1.39 us (1%)
    all_to_all x1, waiting for transfers between devices, per_device(): lax.all_to_all(terms, 'tm', 0, 0, tiled=True, axis_index_groups=Y_GROUPS)  13.2 us
    all_to_all x1, starting transfers between devices, per_device(): got = lax.all_to_all(sums, 'lat', 0, 0, tiled=True)  10.1 us
    all_to_all x1, waiting for transfers between devices, per_device(): lax.all_to_all(blocks, 'tm', 0, 0, tiled=True, axis_index_groups=Y_GROUPS)  8.77 us
    all_to_all x1, starting transfers between devices, per_device(): lax.all_to_all(part_totals(got), 'tm', 0, 0, tiled=True, axis_index_group...  7.82 us
    all_to_all x1, waiting for transfers between devices, per_device(): got = lax.all_to_all(sums, 'lat', 0, 0, tiled=True)  7.72 us
    ppermute x2, waiting for transfers between devices, swapped(): far = lax.ppermute(edge_far, 'lat', SWAP_FAR)  6.13 us
    all_to_all x1, waiting for transfers between devices, per_device(): lax.all_to_all(part_totals(got), 'tm', 0, 0, tiled=True, axis_index_group...  5.92 us
    all_to_all x1, waiting for transfers between devices, per_device(): lax.all_to_all(pieces, 'tm', 0, 0, tiled=True, axis_index_groups=Z_GROUPS)  5.78 us
  transfers between devices with their start and end apart: 11, of which 6 were waited for; matrix products, arithmetic and copies ran while one was open for 3% of the time, Pallas kernels for 7%

profile of v5, /device:TPU:32, one launch (start us, length us, event | category | flops | bytes accessed | tf_op | source)
XLA Modules:
  0.0 105.8 jit_solution(13905725320219689920)
XLA Ops:
  0.6 1.9 %collective-permute-start.1 = (f32[16,32]{1,0:T(8,128)}, f32[16,32]{1,0:T(8,128)S(1)}, u32[]{:S(2)}, u32[]{:S(2)}) collective-permute-start(f32[16,32]{1,0:T(8,128)} %bitcast.11), channel_id=1, source_target_pairs={{1,0},{2,1},{3,2},{4,3},{5,4},{6,5},{7,6},{8,7},{9,8},{10,9},{11,1... | collective-permute-start | bytes 6152 | tf_op jit(solution)/shard_map/ppermute | solution.py:527
  2.5 0.2 collective-permute-start
  2.8 4.7 %project.1 = f32[16,8,256]{2,1,0:T(8,128)} custom-call(f32[8,16,5760]{2,1,0:T(8,128)} %data_ref.3, f32[32,5760]{1,0:T(8,128)} %space_ref.1, f32[8,32]{1,0:T(8,128)} %vf_ref.5), custom_call_target="tpu_custom_call" | custom-call | flops 4000000000 | bytes 8000000 | tf_op jit(solution)/shard_map/project/pallas_call | solution.py:140
  7.5 10.1 %all-to-all-start = ((f32[16,8,256]{2,1,0:T(8,128)}), f32[16,8,256]{2,1,0:T(8,128)S(1)}, u32[]{:S(2)}, u32[]{:S(2)}) async-start(f32[16,8,256]{2,1,0:T(8,128)} %project.1), calls=%async_computation | async-start | bytes 262144 | tf_op jit(solution)/shard_map/all_to_all | solution.py:529
  17.7 0.3 compare_select_fusion.2
  18.0 0.7 reshape.25
  18.8 0.1 slice.57
  19.0 0.3 fusion.1
  19.3 0.1 copy.8
  19.5 0.5 copy-done.5
  20.0 0.6 fusion.11.stencil_ref
  20.6 7.7 %all-to-all-done.got_ref = f32[16,8,256]{2,1,0:T(8,128)S(1)} async-done(((f32[16,8,256]{2,1,0:T(8,128)}), f32[16,8,256]{2,1,0:T(8,128)S(1)}, u32[]{:S(2)}, u32[]{:S(2)}) %all-to-all-start) | async-done | bytes 131104 | tf_op jit(solution)/shard_map/all_to_all | solution.py:529
  28.3 0.7 copy-done.2
  28.9 4.8 %hour_mode.1 = (f32[32,16]{1,0:T(8,128)}, f32[4,32,1792]{2,1,0:T(8,128)}) custom-call(f32[16,8,256]{2,1,0:T(8,128)} %copy-done.2, f32[16,32]{1,0:T(8,128)} %fusion.11.stencil_ref, f32[8,32]{1,0:T(8,128)} %vf_ref.5, f32[8,16,5760]{2,1,0:T(8,128)} %data_ref.3), custom_call_target="tpu_custom_call" | custom-call | flops 5000000000 | bytes 8000000 | tf_op jit(solution)/shard_map/hour_mode/pallas_call | solution.py:268
  33.7 4.5 %all-to-all-start.1 = ((f32[4,32,1792]{2,1,0:T(8,128)}), f32[4,32,1792]{2,1,0:T(8,128)S(1)}, u32[]{:S(2)}, u32[]{:S(2)}) async-start(f32[4,32,1792]{2,1,0:T(8,128)} %get-tuple-element.14), calls=%async_computation.1 | async-start | bytes 1835008 | tf_op jit(solution)/shard_map/all_to_all | solution.py:555
  38.2 0.3 collective-permute-start.4
  38.5 0.2 collective-permute-start.5
  38.7 13.2 %all-to-all-done.1.got_ref = f32[4,32,1792]{2,1,0:T(8,128)S(1)} async-done(((f32[4,32,1792]{2,1,0:T(8,128)}), f32[4,32,1792]{2,1,0:T(8,128)S(1)}, u32[]{:S(2)}, u32[]{:S(2)}) %all-to-all-start.1) | async-done | bytes 917536 | tf_op jit(solution)/shard_map/all_to_all | solution.py:555
  51.9 0.7 part_totals.1
  52.6 7.8 %all-to-all-start.2 = ((f32[4,8,1792]{2,1,0:T(8,128)}), f32[4,8,1792]{2,1,0:T(8,128)S(1)}, u32[]{:S(2)}, u32[]{:S(2)}) async-start(f32[4,8,1792]{2,1,0:T(8,128)} %part_totals.1), calls=%async_computation.2 | async-start | bytes 458752 | tf_op jit(solution)/shard_map/all_to_all | solution.py:556
  60.5 5.9 %all-to-all-done.2.got_ref = f32[4,8,1792]{2,1,0:T(8,128)S(1)} async-done(((f32[4,8,1792]{2,1,0:T(8,128)}), f32[4,8,1792]{2,1,0:T(8,128)S(1)}, u32[]{:S(2)}, u32[]{:S(2)}) %all-to-all-start.2) | async-done | bytes 229408 | tf_op jit(solution)/shard_map/all_to_all | solution.py:556
  66.4 0.7 totals.1
  67.1 4.2 %all-to-all-start.3 = ((f32[4,8,1664]{2,1,0:T(8,128)}), f32[4,8,1664]{2,1,0:T(8,128)S(1)}, u32[]{:S(2)}, u32[]{:S(2)}) async-start(f32[4,8,1664]{2,1,0:T(8,128)} %get-tuple-element.15), calls=%async_computation.3 | async-start | bytes 425984 | tf_op jit(solution)/shard_map/all_to_all | solution.py:558
  71.4 5.8 %all-to-all-done.3 = f32[4,8,1664]{2,1,0:T(8,128)S(1)} async-done(((f32[4,8,1664]{2,1,0:T(8,128)}), f32[4,8,1664]{2,1,0:T(8,128)S(1)}, u32[]{:S(2)}, u32[]{:S(2)}) %all-to-all-start.3) | async-done | bytes 213024 | tf_op jit(solution)/shard_map/all_to_all | solution.py:558
  77.3 3.0 %collective-permute-start.2 = (f32[32,768]{1,0:T(8,128)S(1)}, f32[32,768]{1,0:T(8,128)S(1)}, u32[]{:S(2)}, u32[]{:S(2)}) collective-permute-start(f32[32,768]{1,0:T(8,128)S(1)} %get-tuple-element.29), channel_id=1, source_target_pairs={{0,16},{16,0},{32,48},{48,32},{64,80},{80,64},{96,112},{112,96},{1... | collective-permute-start | bytes 294920 | tf_op jit(solution)/shard_map/ppermute | solution.py:510
  80.3 1.5 %operator.1 = (bf16[32,128]{1,0:T(8,128)(2,1)S(1)}, bf16[32,256]{1,0:T(8,128)(2,1)S(1)}, f32[32,128]{1,0:T(8,128)S(1)}) custom-call(f32[8,128]{1,0:T(8,128)S(1)} %get-tuple-element.18.gram_ref, f32[8,32]{1,0:T(8,128)S(1)} %copy-done), custom_call_target="tpu_custom_call" | custom-call | flops 4000000000 | bytes 100000 | tf_op jit(solution)/shard_map/operator/pallas_call | solution.py:360
  81.8 6.1 %collective-permute-done.3.far_ref = f32[32,768]{1,0:T(8,128)S(1)} collective-permute-done((f32[32,768]{1,0:T(8,128)S(1)}, f32[32,768]{1,0:T(8,128)S(1)}, u32[]{:S(2)}, u32[]{:S(2)}) %collective-permute-start.3) | collective-permute-done | bytes 98336 | tf_op jit(solution)/shard_map/ppermute | solution.py:509
  88.0 3.6 %sweeps.1 = f32[4,32,1536]{2,1,0:T(8,128)} custom-call(s32[1]{0:T(128)} %bitcast.1.even_ref, f32[32,1664]{1,0:T(8,128)S(1)} %bitcast.7, f32[32,768]{1,0:T(8,128)S(1)} %collective-permute-done.2.near_ref, f32[32,768]{1,0:T(8,128)S(1)} %collective-permute-done.3.far_ref, f32[34,4096]{1,0:T(8,128)S(1)} %pad_maximum_fusion.1.start_ref, ...), custom_call_target="tpu_custom_call" | custom-call | tf_op jit(solution)/shard_map/sweeps/pallas_call | solution.py:457
  91.5 3.6 %all-to-all-start.4 = ((f32[4,32,1536]{2,1,0:T(8,128)}), f32[4,32,1536]{2,1,0:T(8,128)S(1)}, u32[]{:S(2)}, u32[]{:S(2)}) async-start(f32[4,32,1536]{2,1,0:T(8,128)} %sweeps.1), calls=%async_computation.4 | async-start | bytes 1572864 | tf_op jit(solution)/shard_map/all_to_all | solution.py:564
  95.2 0.7 copy.7
  95.9 8.8 %all-to-all-done.4.got_ref = f32[4,32,1536]{2,1,0:T(8,128)S(1)} async-done(((f32[4,32,1536]{2,1,0:T(8,128)}), f32[4,32,1536]{2,1,0:T(8,128)S(1)}, u32[]{:S(2)}, u32[]{:S(2)}) %all-to-all-start.4) | async-done | bytes 786464 | tf_op jit(solution)/shard_map/all_to_all | solution.py:564
  104.6 1.2 %join.1 = f32[32,5760]{1,0:T(8,128)} custom-call(f32[4,32,1536]{2,1,0:T(8,128)S(1)} %all-to-all-done.4.got_ref), custom_call_target="tpu_custom_call" | custom-call | tf_op jit(solution)/shard_map/join/pallas_call | solution.py:491
  (26 shorter events, 0.4 us)
Async XLA Ops:
  0.6 17.0 %copy-start.3 = (s32[4,5760]{1,0:T(4,128)S(1)}, s32[4,5760]{1,0:T(4,128)}, u32[]{:S(2)}) copy-start(s32[4,5760]{1,0:T(4,128)} %param.9) | copy-start | bytes 276484
  0.6 17.3 %copy-start.1 = (f32[32,5760]{1,0:T(8,128)S(1)}, f32[32,5760]{1,0:T(8,128)}, u32[]{:S(2)}) copy-start(f32[32,5760]{1,0:T(8,128)} %space_ref.1) | copy-start | bytes 2211844
  0.6 18.8 %collective-permute-start.1 = (f32[16,32]{1,0:T(8,128)}, f32[16,32]{1,0:T(8,128)S(1)}, u32[]{:S(2)}, u32[]{:S(2)}) collective-permute-start(f32[16,32]{1,0:T(8,128)} %bitcast.11), channel_id=1, source_target_pairs={{1,0},{2,1},{3,2},{4,3},{5,4},{6,5},{7,6},{8,7},{9,8},{10,9},{11,1... | collective-permute-start | bytes 6152 | tf_op jit(solution)/shard_map/ppermute | solution.py:527
  2.5 16.9 %collective-permute-start = (f32[16,32]{1,0:T(8,128)}, f32[16,32]{1,0:T(8,128)S(1)}, u32[]{:S(2)}, u32[]{:S(2)}) collective-permute-start(f32[16,32]{1,0:T(8,128)} %bitcast.12), channel_id=1, source_target_pairs={{0,1},{1,2},{2,3},{3,4},{4,5},{5,6},{6,7},{7,8},{8,9},{9,10},{10,1... | collective-permute-start | bytes 6152 | tf_op jit(solution)/shard_map/ppermute | solution.py:526
  7.5 20.8 %all-to-all-start = ((f32[16,8,256]{2,1,0:T(8,128)}), f32[16,8,256]{2,1,0:T(8,128)S(1)}, u32[]{:S(2)}, u32[]{:S(2)}) async-start(f32[16,8,256]{2,1,0:T(8,128)} %project.1), calls=%async_computation | async-start | bytes 262144 | tf_op jit(solution)/shard_map/all_to_all | solution.py:529
  19.3 0.7 copy-start.5
  28.3 0.7 copy-start.2
  33.7 18.2 %all-to-all-start.1 = ((f32[4,32,1792]{2,1,0:T(8,128)}), f32[4,32,1792]{2,1,0:T(8,128)S(1)}, u32[]{:S(2)}, u32[]{:S(2)}) async-start(f32[4,32,1792]{2,1,0:T(8,128)} %get-tuple-element.14), calls=%async_computation.1 | async-start | bytes 1835008 | tf_op jit(solution)/shard_map/all_to_all | solution.py:555
  38.2 22.3 %collective-permute-start.4 = (f32[34,1024]{1,0:T(8,128)S(1)}, f32[34,1024]{1,0:T(8,128)S(1)}, u32[]{:S(2)}, u32[]{:S(2)}) collective-permute-start(f32[34,1024]{1,0:T(8,128)S(1)} %get-tuple-element.16), channel_id=1, source_target_pairs={{0,240},{16,32},{32,16},{48,64},{64,48},{80,96},{96,80},{112,128},... | collective-permute-start | bytes 417800 | tf_op jit(solution)/shard_map/ppermute | solution.py:509
  38.5 22.0 %collective-permute-start.5 = (f32[34,1024]{1,0:T(8,128)S(1)}, f32[34,1024]{1,0:T(8,128)S(1)}, u32[]{:S(2)}, u32[]{:S(2)}) collective-permute-start(f32[34,1024]{1,0:T(8,128)S(1)} %get-tuple-element.17), channel_id=1, source_target_pairs={{0,16},{16,0},{32,48},{48,32},{64,80},{80,64},{96,112},{112,96},{1... | collective-permute-start | bytes 417800 | tf_op jit(solution)/shard_map/ppermute | solution.py:510
  52.6 13.8 %all-to-all-start.2 = ((f32[4,8,1792]{2,1,0:T(8,128)}), f32[4,8,1792]{2,1,0:T(8,128)S(1)}, u32[]{:S(2)}, u32[]{:S(2)}) async-start(f32[4,8,1792]{2,1,0:T(8,128)} %part_totals.1), calls=%async_computation.2 | async-start | bytes 458752 | tf_op jit(solution)/shard_map/all_to_all | solution.py:556
  67.1 13.2 %copy-start = (f32[8,32]{1,0:T(8,128)S(1)}, f32[8,32]{1,0:T(8,128)}, u32[]{:S(2)}) copy-start(f32[8,32]{1,0:T(8,128)} %vf_ref.5) | copy-start | bytes 3076
  67.1 10.1 %all-to-all-start.3 = ((f32[4,8,1664]{2,1,0:T(8,128)}), f32[4,8,1664]{2,1,0:T(8,128)S(1)}, u32[]{:S(2)}, u32[]{:S(2)}) async-start(f32[4,8,1664]{2,1,0:T(8,128)} %get-tuple-element.15), calls=%async_computation.3 | async-start | bytes 425984 | tf_op jit(solution)/shard_map/all_to_all | solution.py:558
  77.2 10.8 %collective-permute-start.3 = (f32[32,768]{1,0:T(8,128)S(1)}, f32[32,768]{1,0:T(8,128)S(1)}, u32[]{:S(2)}, u32[]{:S(2)}) collective-permute-start(f32[32,768]{1,0:T(8,128)S(1)} %get-tuple-element.28), channel_id=1, source_target_pairs={{0,240},{16,32},{32,16},{48,64},{64,48},{80,96},{96,80},{112,128},... | collective-permute-start | bytes 294920 | tf_op jit(solution)/shard_map/ppermute | solution.py:509
  77.3 10.7 %collective-permute-start.2 = (f32[32,768]{1,0:T(8,128)S(1)}, f32[32,768]{1,0:T(8,128)S(1)}, u32[]{:S(2)}, u32[]{:S(2)}) collective-permute-start(f32[32,768]{1,0:T(8,128)S(1)} %get-tuple-element.29), channel_id=1, source_target_pairs={{0,16},{16,0},{32,48},{48,32},{64,80},{80,64},{96,112},{112,96},{1... | collective-permute-start | bytes 294920 | tf_op jit(solution)/shard_map/ppermute | solution.py:510
  91.5 3.6 %copy-start.4 = (f32[32,16]{1,0:T(8,128)S(1)}, f32[32,16]{1,0:T(8,128)}, u32[]{:S(2)}) copy-start(f32[32,16]{1,0:T(8,128)} %get-tuple-element.22) | copy-start | bytes 6148
  91.5 13.1 %all-to-all-start.4 = ((f32[4,32,1536]{2,1,0:T(8,128)}), f32[4,32,1536]{2,1,0:T(8,128)S(1)}, u32[]{:S(2)}, u32[]{:S(2)}) async-start(f32[4,32,1536]{2,1,0:T(8,128)} %sweeps.1), calls=%async_computation.4 | async-start | bytes 1572864 | tf_op jit(solution)/shard_map/all_to_all | solution.py:564

commit v6 on v5

--- a/solution.py
+++ b/solution.py
@@ -173,10 +173,6 @@
         store((i + 1) * width // LANES, held)
 
 
-def spot(start):
-    return lax.div(start, LANES), lax.rem(start, LANES)
-
-
 def placed(ref, start, to):
     t, off = divmod(start, LANES)
     lo, hi = ref[:, t * LANES : (t + 1) * LANES], ref[:, (t + 1) * LANES : (t + 2) * LANES]
@@ -194,10 +190,6 @@
     if hi is None:
         return turn(lo, -off)
     return turn(jnp.where(lane_iota(ref.shape[0]) >= off, lo, hi), -off)
-
-
-def tile(t):
-    return pl.ds(pl.multiple_of(t * LANES, LANES), LANES)
 
 
 def hour_kernel(got_ref, stencil_ref, vf_ref, data_ref, tf_ref, out_ref, dbuf, terms, sem):
@@ -444,8 +436,16 @@
             before, here = here, after
 
     def store(t, value):
+        groups = [value[8 * g : 8 * g + 8] for g in range(4)]
+        if t == 11:
+            lane = lane_iota(8)
+            joint = groups[0]
+            for g in range(1, 4):
+                joint = jnp.where(lane >= 32 * g, turn(groups[g], 32 * g), joint)
+            groups = [joint]
         for k in range(PARTS):
-            out_ref[k, :, t * LANES : (t + 1) * LANES] = value
+            for g, group in enumerate(groups):
+                out_ref[k, 32 * t + 8 * g : 32 * t + 8 * g + 8, :] = group
 
     pack_pieces(
         [turn(state[:, (8 + i) * LANES : (9 + i) * LANES], -8) for i in range(ROWS)], WIDTH, store
@@ -458,7 +458,7 @@
         sweep_kernel,
         in_specs=[pl.BlockSpec(memory_space=pltpu.SMEM)] + [vmem] * 7,
         out_specs=vmem,
-        out_shape=jax.ShapeDtypeStruct((PARTS, RANK, 12 * LANES), F32),
+        out_shape=jax.ShapeDtypeStruct((PARTS, 360, LANES), F32),
         scratch_shapes=[
             pltpu.VMEM((RANK, EXT * LANES), F32),
             pltpu.VMEM((RANK, EXT * LANES), F32),
@@ -472,18 +472,26 @@
 def join_kernel(got_ref, out_ref):
     lane = lane_iota(RANK)
 
-    def row(i, held):
+    def read(y, t):
+        if t < 11:
+            return got_ref[y, 32 * t : 32 * t + 32, :]
+        last = got_ref[y, 352:360, :]
+        return jnp.concatenate([turn(last, -32 * g) for g in range(4)], axis=0)
+
+    held = None
+    for i in range(ROWS):
         for y in range(PARTS):
-            to_tile, off = spot(i * NLON + y * WIDTH)
-            first, at = spot(i * WIDTH)
-            joint = jnp.where(lane >= at, got_ref[y, :, tile(first)], got_ref[y, :, tile(first + 1)])
-            moved = pltpu.roll(joint, lax.rem(off + LANES - at, LANES), axis=1)
-            value = jnp.where(lane < off, held, moved)
-            out_ref[:, tile(to_tile)] = value
-            held = jnp.where(off + WIDTH >= LANES, moved, value)
-        return held
-
-    lax.fori_loop(0, ROWS, row, jnp.zeros((RANK, LANES), F32), unroll=16)
+            to_tile, off = divmod(i * NLON + y * WIDTH, LANES)
+            first, at = divmod(i * WIDTH, LANES)
+            joint = read(y, first)
+            if at + WIDTH > LANES:
+                joint = jnp.where(lane >= at, joint, read(y, first + 1))
+            moved = turn(joint, off - at)
+            value = moved if off == 0 else jnp.where(lane < off, held, moved)
+            held = value
+            if off + WIDTH >= LANES:
+                out_ref[:, to_tile * LANES : (to_tile + 1) * LANES] = value
+                held = moved
 
 
 def join(got):

time: 106 us -> 106 us (level)
  no operation moved by 1% of the time
where the time goes in v6:
time: 106 us
  waiting for transfers between devices  47.3 us (45%)
  starting transfers between devices  36 us (34%)
  Pallas kernels  17.4 us (16%)
  local copies, waits for them, and re-layouts  2.8 us (3%)
  other arithmetic  1.39 us (1%)
    all_to_all x1, waiting for transfers between devices, per_device(): lax.all_to_all(terms, 'tm', 0, 0, tiled=True, axis_index_groups=Y_GROUPS)  13.2 us
    all_to_all x1, starting transfers between devices, per_device(): got = lax.all_to_all(sums, 'lat', 0, 0, tiled=True)  10.1 us
    all_to_all x1, waiting for transfers between devices, per_device(): lax.all_to_all(blocks, 'tm', 0, 0, tiled=True, axis_index_groups=Y_GROUPS)  8.51 us
    all_to_all x1, starting transfers between devices, per_device(): lax.all_to_all(part_totals(got), 'tm', 0, 0, tiled=True, axis_index_group...  7.82 us
    all_to_all x1, waiting for transfers between devices, per_device(): got = lax.all_to_all(sums, 'lat', 0, 0, tiled=True)  7.72 us
    ppermute x2, waiting for transfers between devices, swapped(): far = lax.ppermute(edge_far, 'lat', SWAP_FAR)  6.13 us
    all_to_all x1, waiting for transfers between devices, per_device(): lax.all_to_all(part_totals(got), 'tm', 0, 0, tiled=True, axis_index_group...  5.92 us
    all_to_all x1, waiting for transfers between devices, per_device(): lax.all_to_all(pieces, 'tm', 0, 0, tiled=True, axis_index_groups=Z_GROUPS)  5.78 us
  transfers between devices with their start and end apart: 11, of which 6 were waited for; matrix products, arithmetic and copies ran while one was open for 3% of the time, Pallas kernels for 7%

profile of v6, /device:TPU:32, one launch (start us, length us, event | category | flops | bytes accessed | tf_op | source)
XLA Modules:
  0.0 105.8 jit_solution(12285801527183684505)
XLA Ops:
  0.6 1.9 %collective-permute-start.1 = (f32[16,32]{1,0:T(8,128)}, f32[16,32]{1,0:T(8,128)S(1)}, u32[]{:S(2)}, u32[]{:S(2)}) collective-permute-start(f32[16,32]{1,0:T(8,128)} %bitcast.11), channel_id=1, source_target_pairs={{1,0},{2,1},{3,2},{4,3},{5,4},{6,5},{7,6},{8,7},{9,8},{10,9},{11,1... | collective-permute-start | bytes 6152 | tf_op jit(solution)/shard_map/ppermute | solution.py:535
  2.5 0.2 collective-permute-start
  2.8 4.7 %project.1 = f32[16,8,256]{2,1,0:T(8,128)} custom-call(f32[8,16,5760]{2,1,0:T(8,128)} %data_ref.3, f32[32,5760]{1,0:T(8,128)} %space_ref.1, f32[8,32]{1,0:T(8,128)} %vf_ref.5), custom_call_target="tpu_custom_call" | custom-call | flops 4000000000 | bytes 8000000 | tf_op jit(solution)/shard_map/project/pallas_call | solution.py:140
  7.5 10.1 %all-to-all-start = ((f32[16,8,256]{2,1,0:T(8,128)}), f32[16,8,256]{2,1,0:T(8,128)S(1)}, u32[]{:S(2)}, u32[]{:S(2)}) async-start(f32[16,8,256]{2,1,0:T(8,128)} %project.1), calls=%async_computation | async-start | bytes 262144 | tf_op jit(solution)/shard_map/all_to_all | solution.py:537
  17.7 0.3 compare_select_fusion.2
  18.0 0.7 reshape.25
  18.8 0.1 slice.57
  19.0 0.3 fusion.1
  19.3 0.1 copy.8
  19.5 0.5 copy-done.5
  20.0 0.6 fusion.11.stencil_ref
  20.6 7.7 %all-to-all-done.got_ref = f32[16,8,256]{2,1,0:T(8,128)S(1)} async-done(((f32[16,8,256]{2,1,0:T(8,128)}), f32[16,8,256]{2,1,0:T(8,128)S(1)}, u32[]{:S(2)}, u32[]{:S(2)}) %all-to-all-start) | async-done | bytes 131104 | tf_op jit(solution)/shard_map/all_to_all | solution.py:537
  28.3 0.7 copy-done.2
  28.9 4.8 %hour_mode.1 = (f32[32,16]{1,0:T(8,128)}, f32[4,32,1792]{2,1,0:T(8,128)}) custom-call(f32[16,8,256]{2,1,0:T(8,128)} %copy-done.2, f32[16,32]{1,0:T(8,128)} %fusion.11.stencil_ref, f32[8,32]{1,0:T(8,128)} %vf_ref.5, f32[8,16,5760]{2,1,0:T(8,128)} %data_ref.3), custom_call_target="tpu_custom_call" | custom-call | flops 5000000000 | bytes 8000000 | tf_op jit(solution)/shard_map/hour_mode/pallas_call | solution.py:260
  33.7 4.5 %all-to-all-start.1 = ((f32[4,32,1792]{2,1,0:T(8,128)}), f32[4,32,1792]{2,1,0:T(8,128)S(1)}, u32[]{:S(2)}, u32[]{:S(2)}) async-start(f32[4,32,1792]{2,1,0:T(8,128)} %get-tuple-element.14), calls=%async_computation.1 | async-start | bytes 1835008 | tf_op jit(solution)/shard_map/all_to_all | solution.py:563
  38.2 0.3 collective-permute-start.4
  38.5 0.2 collective-permute-start.5
  38.7 13.2 %all-to-all-done.1.got_ref = f32[4,32,1792]{2,1,0:T(8,128)S(1)} async-done(((f32[4,32,1792]{2,1,0:T(8,128)}), f32[4,32,1792]{2,1,0:T(8,128)S(1)}, u32[]{:S(2)}, u32[]{:S(2)}) %all-to-all-start.1) | async-done | bytes 917536 | tf_op jit(solution)/shard_map/all_to_all | solution.py:563
  51.9 0.7 part_totals.1
  52.6 7.8 %all-to-all-start.2 = ((f32[4,8,1792]{2,1,0:T(8,128)}), f32[4,8,1792]{2,1,0:T(8,128)S(1)}, u32[]{:S(2)}, u32[]{:S(2)}) async-start(f32[4,8,1792]{2,1,0:T(8,128)} %part_totals.1), calls=%async_computation.2 | async-start | bytes 458752 | tf_op jit(solution)/shard_map/all_to_all | solution.py:564
  60.5 5.9 %all-to-all-done.2.got_ref = f32[4,8,1792]{2,1,0:T(8,128)S(1)} async-done(((f32[4,8,1792]{2,1,0:T(8,128)}), f32[4,8,1792]{2,1,0:T(8,128)S(1)}, u32[]{:S(2)}, u32[]{:S(2)}) %all-to-all-start.2) | async-done | bytes 229408 | tf_op jit(solution)/shard_map/all_to_all | solution.py:564
  66.4 0.7 totals.1
  67.1 4.2 %all-to-all-start.3 = ((f32[4,8,1664]{2,1,0:T(8,128)}), f32[4,8,1664]{2,1,0:T(8,128)S(1)}, u32[]{:S(2)}, u32[]{:S(2)}) async-start(f32[4,8,1664]{2,1,0:T(8,128)} %get-tuple-element.15), calls=%async_computation.3 | async-start | bytes 425984 | tf_op jit(solution)/shard_map/all_to_all | solution.py:566
  71.4 5.8 %all-to-all-done.3 = f32[4,8,1664]{2,1,0:T(8,128)S(1)} async-done(((f32[4,8,1664]{2,1,0:T(8,128)}), f32[4,8,1664]{2,1,0:T(8,128)S(1)}, u32[]{:S(2)}, u32[]{:S(2)}) %all-to-all-start.3) | async-done | bytes 213024 | tf_op jit(solution)/shard_map/all_to_all | solution.py:566
  77.3 3.0 %collective-permute-start.2 = (f32[32,768]{1,0:T(8,128)S(1)}, f32[32,768]{1,0:T(8,128)S(1)}, u32[]{:S(2)}, u32[]{:S(2)}) collective-permute-start(f32[32,768]{1,0:T(8,128)S(1)} %get-tuple-element.29), channel_id=1, source_target_pairs={{0,16},{16,0},{32,48},{48,32},{64,80},{80,64},{96,112},{112,96},{1... | collective-permute-start | bytes 294920 | tf_op jit(solution)/shard_map/ppermute | solution.py:518
  80.3 1.5 %operator.1 = (bf16[32,128]{1,0:T(8,128)(2,1)S(1)}, bf16[32,256]{1,0:T(8,128)(2,1)S(1)}, f32[32,128]{1,0:T(8,128)S(1)}) custom-call(f32[8,128]{1,0:T(8,128)S(1)} %get-tuple-element.18.gram_ref, f32[8,32]{1,0:T(8,128)S(1)} %copy-done), custom_call_target="tpu_custom_call" | custom-call | flops 4000000000 | bytes 100000 | tf_op jit(solution)/shard_map/operator/pallas_call | solution.py:352
  81.8 6.1 %collective-permute-done.3.far_ref = f32[32,768]{1,0:T(8,128)S(1)} collective-permute-done((f32[32,768]{1,0:T(8,128)S(1)}, f32[32,768]{1,0:T(8,128)S(1)}, u32[]{:S(2)}, u32[]{:S(2)}) %collective-permute-start.3) | collective-permute-done | bytes 98336 | tf_op jit(solution)/shard_map/ppermute | solution.py:517
  88.0 3.8 %sweeps.1 = f32[4,360,128]{2,1,0:T(8,128)} custom-call(s32[1]{0:T(128)} %bitcast.1.even_ref, f32[32,1664]{1,0:T(8,128)S(1)} %bitcast.7, f32[32,768]{1,0:T(8,128)S(1)} %collective-permute-done.2.near_ref, f32[32,768]{1,0:T(8,128)S(1)} %collective-permute-done.3.far_ref, f32[34,4096]{1,0:T(8,128)S(1)} %pad_maximum_fusion.1.start_ref, ...), custom_call_target="tpu_custom_call" | custom-call | tf_op jit(solution)/shard_map/sweeps/pallas_call | solution.py:457
  91.7 3.6 %all-to-all-start.4 = ((f32[4,360,128]{2,1,0:T(8,128)}), f32[4,360,128]{2,1,0:T(8,128)S(1)}, u32[]{:S(2)}, u32[]{:S(2)}) async-start(f32[4,360,128]{2,1,0:T(8,128)} %sweeps.1), calls=%async_computation.4 | async-start | bytes 1474560 | tf_op jit(solution)/shard_map/all_to_all | solution.py:572
  95.4 0.7 copy.7
  96.0 8.5 %all-to-all-done.4.got_ref = f32[4,360,128]{2,1,0:T(8,128)S(1)} async-done(((f32[4,360,128]{2,1,0:T(8,128)}), f32[4,360,128]{2,1,0:T(8,128)S(1)}, u32[]{:S(2)}, u32[]{:S(2)}) %all-to-all-start.4) | async-done | bytes 737312 | tf_op jit(solution)/shard_map/all_to_all | solution.py:572
  104.6 1.2 %join.1 = f32[32,5760]{1,0:T(8,128)} custom-call(f32[4,360,128]{2,1,0:T(8,128)S(1)} %all-to-all-done.4.got_ref), custom_call_target="tpu_custom_call" | custom-call | tf_op jit(solution)/shard_map/join/pallas_call | solution.py:499
  (26 shorter events, 0.4 us)
Async XLA Ops:
  0.6 17.0 %copy-start.3 = (s32[4,5760]{1,0:T(4,128)S(1)}, s32[4,5760]{1,0:T(4,128)}, u32[]{:S(2)}) copy-start(s32[4,5760]{1,0:T(4,128)} %param.9) | copy-start | bytes 276484
  0.6 17.3 %copy-start.1 = (f32[32,5760]{1,0:T(8,128)S(1)}, f32[32,5760]{1,0:T(8,128)}, u32[]{:S(2)}) copy-start(f32[32,5760]{1,0:T(8,128)} %space_ref.1) | copy-start | bytes 2211844
  0.6 18.8 %collective-permute-start.1 = (f32[16,32]{1,0:T(8,128)}, f32[16,32]{1,0:T(8,128)S(1)}, u32[]{:S(2)}, u32[]{:S(2)}) collective-permute-start(f32[16,32]{1,0:T(8,128)} %bitcast.11), channel_id=1, source_target_pairs={{1,0},{2,1},{3,2},{4,3},{5,4},{6,5},{7,6},{8,7},{9,8},{10,9},{11,1... | collective-permute-start | bytes 6152 | tf_op jit(solution)/shard_map/ppermute | solution.py:535
  2.5 16.9 %collective-permute-start = (f32[16,32]{1,0:T(8,128)}, f32[16,32]{1,0:T(8,128)S(1)}, u32[]{:S(2)}, u32[]{:S(2)}) collective-permute-start(f32[16,32]{1,0:T(8,128)} %bitcast.12), channel_id=1, source_target_pairs={{0,1},{1,2},{2,3},{3,4},{4,5},{5,6},{6,7},{7,8},{8,9},{9,10},{10,1... | collective-permute-start | bytes 6152 | tf_op jit(solution)/shard_map/ppermute | solution.py:534
  7.5 20.8 %all-to-all-start = ((f32[16,8,256]{2,1,0:T(8,128)}), f32[16,8,256]{2,1,0:T(8,128)S(1)}, u32[]{:S(2)}, u32[]{:S(2)}) async-start(f32[16,8,256]{2,1,0:T(8,128)} %project.1), calls=%async_computation | async-start | bytes 262144 | tf_op jit(solution)/shard_map/all_to_all | solution.py:537
  19.3 0.7 copy-start.5
  28.3 0.7 copy-start.2
  33.7 18.2 %all-to-all-start.1 = ((f32[4,32,1792]{2,1,0:T(8,128)}), f32[4,32,1792]{2,1,0:T(8,128)S(1)}, u32[]{:S(2)}, u32[]{:S(2)}) async-start(f32[4,32,1792]{2,1,0:T(8,128)} %get-tuple-element.14), calls=%async_computation.1 | async-start | bytes 1835008 | tf_op jit(solution)/shard_map/all_to_all | solution.py:563
  38.2 22.3 %collective-permute-start.4 = (f32[34,1024]{1,0:T(8,128)S(1)}, f32[34,1024]{1,0:T(8,128)S(1)}, u32[]{:S(2)}, u32[]{:S(2)}) collective-permute-start(f32[34,1024]{1,0:T(8,128)S(1)} %get-tuple-element.16), channel_id=1, source_target_pairs={{0,240},{16,32},{32,16},{48,64},{64,48},{80,96},{96,80},{112,128},... | collective-permute-start | bytes 417800 | tf_op jit(solution)/shard_map/ppermute | solution.py:517
  38.5 22.0 %collective-permute-start.5 = (f32[34,1024]{1,0:T(8,128)S(1)}, f32[34,1024]{1,0:T(8,128)S(1)}, u32[]{:S(2)}, u32[]{:S(2)}) collective-permute-start(f32[34,1024]{1,0:T(8,128)S(1)} %get-tuple-element.17), channel_id=1, source_target_pairs={{0,16},{16,0},{32,48},{48,32},{64,80},{80,64},{96,112},{112,96},{1... | collective-permute-start | bytes 417800 | tf_op jit(solution)/shard_map/ppermute | solution.py:518
  52.6 13.8 %all-to-all-start.2 = ((f32[4,8,1792]{2,1,0:T(8,128)}), f32[4,8,1792]{2,1,0:T(8,128)S(1)}, u32[]{:S(2)}, u32[]{:S(2)}) async-start(f32[4,8,1792]{2,1,0:T(8,128)} %part_totals.1), calls=%async_computation.2 | async-start | bytes 458752 | tf_op jit(solution)/shard_map/all_to_all | solution.py:564
  67.1 13.2 %copy-start = (f32[8,32]{1,0:T(8,128)S(1)}, f32[8,32]{1,0:T(8,128)}, u32[]{:S(2)}) copy-start(f32[8,32]{1,0:T(8,128)} %vf_ref.5) | copy-start | bytes 3076
  67.1 10.1 %all-to-all-start.3 = ((f32[4,8,1664]{2,1,0:T(8,128)}), f32[4,8,1664]{2,1,0:T(8,128)S(1)}, u32[]{:S(2)}, u32[]{:S(2)}) async-start(f32[4,8,1664]{2,1,0:T(8,128)} %get-tuple-element.15), calls=%async_computation.3 | async-start | bytes 425984 | tf_op jit(solution)/shard_map/all_to_all | solution.py:566
  77.2 10.8 %collective-permute-start.3 = (f32[32,768]{1,0:T(8,128)S(1)}, f32[32,768]{1,0:T(8,128)S(1)}, u32[]{:S(2)}, u32[]{:S(2)}) collective-permute-start(f32[32,768]{1,0:T(8,128)S(1)} %get-tuple-element.28), channel_id=1, source_target_pairs={{0,240},{16,32},{32,16},{48,64},{64,48},{80,96},{96,80},{112,128},... | collective-permute-start | bytes 294920 | tf_op jit(solution)/shard_map/ppermute | solution.py:517
  77.3 10.7 %collective-permute-start.2 = (f32[32,768]{1,0:T(8,128)S(1)}, f32[32,768]{1,0:T(8,128)S(1)}, u32[]{:S(2)}, u32[]{:S(2)}) collective-permute-start(f32[32,768]{1,0:T(8,128)S(1)} %get-tuple-element.29), channel_id=1, source_target_pairs={{0,16},{16,0},{32,48},{48,32},{64,80},{80,64},{96,112},{112,96},{1... | collective-permute-start | bytes 294920 | tf_op jit(solution)/shard_map/ppermute | solution.py:518
  91.7 3.6 %copy-start.4 = (f32[32,16]{1,0:T(8,128)S(1)}, f32[32,16]{1,0:T(8,128)}, u32[]{:S(2)}) copy-start(f32[32,16]{1,0:T(8,128)} %get-tuple-element.22) | copy-start | bytes 6148
  91.7 12.8 %all-to-all-start.4 = ((f32[4,360,128]{2,1,0:T(8,128)}), f32[4,360,128]{2,1,0:T(8,128)S(1)}, u32[]{:S(2)}, u32[]{:S(2)}) async-start(f32[4,360,128]{2,1,0:T(8,128)} %sweeps.1), calls=%async_computation.4 | async-start | bytes 1474560 | tf_op jit(solution)/shard_map/all_to_all | solution.py:572
